TPU v7x, 32 devices: a whole 2x2x4 slice. The times are simulated.
32 devices in a mesh: section: 2 (over core), dp: 4 (over z), tensor: 4 (over y, x).
Axes of the slice: x: 2, y: 2, z: 4, core: 2. Of those that a mesh axis runs over, the one named last changes fastest.
Arguments:
- tokens: bfloat16 [2, 3072, 1024], P(None, ('dp', 'tensor')), may hold values from -6 to 6
- cotangent: bfloat16 [2, 3072, 1024], P(None, ('dp', 'tensor')), may hold values from -6 to 6
- mixer_in_weight: bfloat16 [2, 1024, 4, 1024], P('section', None, None, 'tensor'), may hold values from -0.1875 to 0.1875
- mixer_out_weight: bfloat16 [2, 1024, 1024], P('section', 'tensor'), may hold values from -0.1875 to 0.1875
- feed_in_weight: bfloat16 [2, 1024, 2, 2816], P('section', None, None, 'tensor'), may hold values from -0.1875 to 0.1875
- feed_out_weight: bfloat16 [2, 2816, 1024], P('section', 'tensor'), may hold values from -0.109375 to 0.109375
- decay_rate: float32 [2, 8], P('section', 'tensor'), may hold values from 3e-05 to 0.05
- block_starts: int32 [2, 12], replicated, may hold values from 0 to 1, as said below
Outputs:
- layer_outputs: bfloat16 [2, 2, 3072, 1024], P('section', None, ('dp', 'tensor'))
- input_grads: bfloat16 [2, 2, 3072, 1024], P('section', None, ('dp', 'tensor'))
- grad_mixer_in: float32 [2, 1024, 4, 1024], P('section', None, None, 'tensor')
- grad_mixer_out: float32 [2, 1024, 1024], P('section', 'tensor')
- grad_feed_in: float32 [2, 1024, 2, 2816], P('section', None, None, 'tensor')
- grad_feed_out: float32 [2, 2816, 1024], P('section', 'tensor')
Inputs may be any that keep to these rules, and one draw needn't show every extreme that they name: `block_starts`: the first block of every micro-batch is 1; every sequence spans 4 blocks or more and 12 blocks or fewer.
All inputs are finite; a program needn't handle non-finite values.
Results may differ from a plain program's by a relative error of at most 0.035.
Values may be sent and summed in bfloat16 or wider, within the bound.
A program may use at most 192 MiB of HBM per device.

v0:
```python
import jax
import jax.numpy as jnp
from jax import lax
from jax.sharding import PartitionSpec as P

D = 1024
HEAD = 128
BLOCK = 256
MB = 2


norm_eps = 1e-06
exact = lax.Precision.HIGHEST


def entering_2(shard, axis, combine, identity, reverse):
    peers, position = (lax.axis_size(axis), lax.axis_index(axis))
    everything = jax.tree.map(
        lambda part, kind: lax.all_gather(part.astype(kind), axis),
        shard,
        (jnp.bfloat16, jnp.bfloat16),
    )
    start = jax.tree.map(
        lambda part, zero: jnp.broadcast_to(jnp.asarray(zero, part.dtype), part.shape),
        shard,
        identity,
    )

    def lap(k, before):
        at = peers - 1 - k if reverse else k
        reached = at > position if reverse else at < position
        new = combine(
            before, jax.tree.map(lambda part, own: part[at].astype(own.dtype), everything, shard)
        )
        return jax.tree.map(lambda a, b: jnp.where(reached, a, b), new, before)

    return lax.fori_loop(0, peers, lap, start)


def shifted(block, axis, distance):
    devices = range(lax.axis_size(axis))
    route = [(i - distance, i) for i in devices if i - distance in devices]
    return lax.ppermute(block, axis, route)


def simple_norm(values):
    return values * lax.rsqrt(jnp.mean(values * values, axis=-1, keepdims=True) + norm_eps)


def norm_back(inputs, upstream):
    scale = lax.rsqrt(jnp.mean(inputs * inputs, axis=-1, keepdims=True) + norm_eps)
    normed = inputs * scale
    return scale * (upstream - normed * jnp.mean(upstream * normed, axis=-1, keepdims=True))


def swish_act(values):
    return values * jax.nn.sigmoid(values)


def swish_slope(values):
    sigmoid = jax.nn.sigmoid(values)
    return sigmoid * (1.0 + values * (1.0 - sigmoid))


def rotate(values, cosine, sine_part):
    half_width = values.shape[-1] // 2
    first_half = values[..., :half_width]
    second = values[..., half_width:]
    cosine = cosine[:, None, :]
    sine_part = sine_part[:, None, :]
    return jnp.concatenate(
        [first_half * cosine - second * sine_part, first_half * sine_part + second * cosine],
        axis=-1,
    )


def unrotate(values, cosine, sine_part):
    half_width = values.shape[-1] // 2
    first_half = values[..., :half_width]
    second = values[..., half_width:]
    cosine = cosine[:, None, :]
    sine_part = sine_part[:, None, :]
    return jnp.concatenate(
        [first_half * cosine + second * sine_part, second * cosine - first_half * sine_part],
        axis=-1,
    )


def angle_tables(places):
    frequency = 10000.0 ** (-jnp.arange(HEAD // 2, dtype=jnp.float32) / (HEAD // 2))
    angles = places.astype(jnp.float32)[:, None] * frequency[None, :]
    return (jnp.cos(angles), jnp.sin(angles))


def decay_tables(decay_rates):
    steps_in = jnp.arange(BLOCK, dtype=jnp.float32)
    distance = steps_in[:, None] - steps_in[None, :]
    decay_mask = jnp.where(
        distance[None] >= 0.0,
        jnp.exp(-decay_rates[:, None, None] * jnp.maximum(distance, 0.0)[None]),
        0.0,
    )
    query_decay = jnp.exp(-decay_rates[None, :] * (steps_in[:, None] + 1.0))
    key_decay = jnp.exp(-decay_rates[None, :] * (BLOCK - 1.0 - steps_in[:, None]))
    block_decay = jnp.exp(-decay_rates * BLOCK)
    return (decay_mask, query_decay, key_decay, block_decay)


def local_setup(starts, row_total, decay_rates):
    per_device = row_total // BLOCK
    first_block = lax.axis_index("dp") * per_device
    indices = jnp.arange(starts.shape[0], dtype=jnp.int32)
    begins = lax.cummax(jnp.where(starts > 0, indices, 0), axis=0)
    own_ids = first_block + jnp.arange(per_device, dtype=jnp.int32)
    offsets = (own_ids - lax.dynamic_slice_in_dim(begins, first_block, per_device)) * BLOCK
    places = (offsets[:, None] + jnp.arange(BLOCK, dtype=jnp.int32)[None, :]).reshape(-1)
    cosine, sine_part = angle_tables(places)
    resets = lax.dynamic_slice_in_dim(starts, first_block, per_device).astype(jnp.float32)
    return (cosine, sine_part, resets, decay_tables(decay_rates))


def cross_dot(left, right):
    return lax.dot_general(
        left, right, (((0,), (0,)), ((), ())), preferred_element_type=jnp.float32
    )


def back_dot(left, right):
    return lax.dot_general(
        left, right, (((1,), (1,)), ((), ())), preferred_element_type=jnp.float32
    )


def combine_maps(earlier, later):
    return (later[1][:, None, None] * earlier[0] + later[0], later[1] * earlier[1])


def gather_rows(values):
    return lax.all_gather(values, "tensor", axis=0, tiled=True)


def row_sums(left, right):
    return lax.psum_scatter(
        jnp.dot(left, right, preferred_element_type=jnp.float32).astype(jnp.bfloat16),
        "tensor",
        scatter_dimension=0,
        tiled=True,
    ).astype(jnp.float32)


def grad_rows(values):
    return lax.all_gather(values, "tensor", axis=0, tiled=True)


def grad_sums(left, right):
    return lax.psum_scatter(
        back_dot(left, right).astype(jnp.bfloat16), "tensor", scatter_dimension=0, tiled=True
    ).astype(jnp.float32)


def head_sum(values):
    return lax.psum(values, "tensor")


def intra_weights(queries, rotated_keys, decay_mask):
    scores = jnp.einsum(
        "cihd,cjhd->chij", queries, rotated_keys, preferred_element_type=jnp.float32
    )
    return (scores * decay_mask[None]).astype(jnp.bfloat16)


def block_states(rotated_keys, value_rows, key_decay):
    return jnp.einsum(
        "cjhd,cjhe->chde",
        rotated_keys.astype(jnp.float32) * key_decay[None, :, :, None],
        value_rows.astype(jnp.float32),
        precision=exact,
    )


def forward_summary(local_states, resets, block_decay):
    carried = jnp.zeros_like(local_states[0])
    factor = jnp.ones_like(block_decay)
    for slot_idx in range(local_states.shape[0]):
        survive = 1.0 - resets[slot_idx]
        carried = block_decay[:, None, None] * survive * carried + local_states[slot_idx]
        factor = block_decay * survive * factor
    return (carried, factor)


def states_in(before, local_states, resets, block_decay):
    leaving = before
    collected = []
    for slot_idx in range(local_states.shape[0]):
        entering = (1.0 - resets[slot_idx]) * leaving
        collected.append(entering)
        leaving = block_decay[:, None, None] * entering + local_states[slot_idx]
    return jnp.stack(collected)


def backward_summary(terms, resets, block_decay):
    carried = jnp.zeros_like(terms[0])
    factor = jnp.ones_like(block_decay)
    for slot_idx in reversed(range(terms.shape[0])):
        survive = 1.0 - resets[slot_idx]
        carried = survive * (terms[slot_idx] + block_decay[:, None, None] * carried)
        factor = survive * block_decay * factor
    return (carried, factor)


def state_grads(after, terms, resets, block_decay):
    running = after
    collected = []
    for slot_idx in reversed(range(terms.shape[0])):
        collected.append(running)
        running = (1.0 - resets[slot_idx]) * (
            terms[slot_idx] + block_decay[:, None, None] * running
        )
    return jnp.stack(collected[::-1])


def layer_forward(incoming, weights, decay_rates, starts):
    mixer_in, mixer_out, feed_in, feed_out = weights
    inputs = incoming.astype(jnp.float32)
    hidden = gather_rows(simple_norm(inputs).astype(jnp.bfloat16))
    row_total = hidden.shape[0]
    width = mixer_in.shape[-1]
    heads_here = width // HEAD
    per_device = row_total // BLOCK
    cosine, sine_part, resets, tables = local_setup(starts, row_total, decay_rates)
    decay_mask, query_decay, key_decay, block_decay = tables
    projected = jnp.dot(
        hidden, mixer_in.reshape(D, 4 * width), preferred_element_type=jnp.float32
    ).reshape(row_total, 4, width)
    head_shape = (row_total, heads_here, HEAD)
    block_shape = (per_device, BLOCK, heads_here, HEAD)
    queries = (
        rotate(swish_act(projected[:, 0].reshape(head_shape)), cosine, sine_part)
        .astype(jnp.bfloat16)
        .reshape(block_shape)
    )
    rotated_keys = (
        rotate(swish_act(projected[:, 1].reshape(head_shape)), cosine, sine_part)
        .astype(jnp.bfloat16)
        .reshape(block_shape)
    )
    value_rows = projected[:, 2].astype(jnp.bfloat16).reshape(block_shape)
    block_weights = intra_weights(queries, rotated_keys, decay_mask)
    inner_part = jnp.einsum(
        "chij,cjhd->cihd", block_weights, value_rows, preferred_element_type=jnp.float32
    )
    local_states = block_states(rotated_keys, value_rows, key_decay)
    carried, factor = forward_summary(local_states, resets, block_decay)
    before = entering_2(
        (carried, factor),
        "dp",
        combine_maps,
        (jnp.zeros_like(carried), jnp.ones_like(factor)),
        False,
    )[0]
    states = states_in(before, local_states, resets, block_decay)
    outer_part = jnp.einsum(
        "cihd,chde->cihe",
        queries.astype(jnp.float32) * query_decay[None, :, :, None],
        states,
        precision=exact,
    )
    attended = (inner_part + outer_part).reshape(row_total, width)
    scale = lax.rsqrt(head_sum(jnp.sum(attended * attended, axis=-1)) / D + norm_eps)
    gated = (attended * scale[:, None] * projected[:, 3]).astype(jnp.bfloat16)
    middle = inputs + row_sums(gated, mixer_out)
    hidden_two = gather_rows(simple_norm(middle).astype(jnp.bfloat16))
    paired = jnp.dot(
        hidden_two, feed_in.reshape(D, -1), preferred_element_type=jnp.float32
    ).reshape(row_total, 2, -1)
    product = (paired[:, 0] * paired[:, 1]).astype(jnp.bfloat16)
    leaving = middle + row_sums(product, feed_out)
    stored = (
        incoming,
        hidden,
        projected,
        queries,
        rotated_keys,
        value_rows,
        attended,
        scale,
        gated,
        middle,
        hidden_two,
        paired,
        product,
    )
    stored = stored + (states,)
    return (leaving.astype(jnp.bfloat16), stored)


def layer_backward(upstream, stored, weights, decay_rates, starts):
    mixer_in, mixer_out, feed_in, feed_out = weights
    (
        incoming,
        hidden,
        projected,
        queries,
        rotated_keys,
        value_rows,
        attended,
        scale,
        gated,
        middle,
        hidden_two,
        paired,
        product,
    ) = stored[:13]
    row_total = hidden.shape[0]
    width = mixer_in.shape[-1]
    heads_here = width // HEAD
    head_shape = (row_total, heads_here, HEAD)
    block_shape = (row_total // BLOCK, BLOCK, heads_here, HEAD)
    cosine, sine_part, resets, tables = local_setup(starts, row_total, decay_rates)
    decay_mask, query_decay, key_decay, block_decay = tables
    feed_rows = grad_rows(upstream)
    grad_feed_out = cross_dot(product, feed_rows)
    grad_product = back_dot(feed_rows, feed_out)
    grad_paired = (
        jnp.stack([grad_product * paired[:, 1], grad_product * paired[:, 0]], axis=1)
        .astype(jnp.bfloat16)
        .reshape(row_total, -1)
    )
    grad_feed_in = cross_dot(hidden_two, grad_paired)
    grad_middle = upstream.astype(jnp.float32) + norm_back(
        middle, grad_sums(grad_paired, feed_in.reshape(D, -1))
    )
    mixer_rows = grad_rows(grad_middle.astype(jnp.bfloat16))
    grad_mixer_out = cross_dot(gated, mixer_rows)
    grad_gated = back_dot(mixer_rows, mixer_out)
    normed = attended * scale[:, None]
    grad_normed = grad_gated * projected[:, 3]
    grad_gates = grad_gated * normed
    inner_sum = head_sum(jnp.sum(grad_normed * normed, axis=-1))
    grad_attended = scale[:, None] * (grad_normed - normed * (inner_sum / D)[:, None])
    grad_blocks = grad_attended.astype(jnp.bfloat16).reshape(block_shape)
    block_weights = intra_weights(queries, rotated_keys, decay_mask)
    grad_values = jnp.einsum(
        "chij,cihd->cjhd", block_weights, grad_blocks, preferred_element_type=jnp.float32
    )
    grad_weights = jnp.einsum(
        "cihd,cjhd->chij", grad_blocks, value_rows, preferred_element_type=jnp.float32
    )
    grad_scores = (grad_weights * decay_mask[None]).astype(jnp.bfloat16)
    grad_queries = jnp.einsum(
        "chij,cjhd->cihd", grad_scores, rotated_keys, preferred_element_type=jnp.float32
    )
    grad_keys = jnp.einsum(
        "chij,cihd->cjhd", grad_scores, queries, preferred_element_type=jnp.float32
    )
    states = stored[13]
    blocks_wide = grad_blocks.astype(jnp.float32)
    grad_queries = (
        grad_queries
        + jnp.einsum("cihe,chde->cihd", blocks_wide, states, precision=exact)
        * query_decay[None, :, :, None]
    )
    query_hat = queries.astype(jnp.float32) * query_decay[None, :, :, None]
    terms = jnp.einsum("cihd,cihe->chde", query_hat, blocks_wide, precision=exact)
    carried, factor = backward_summary(terms, resets, block_decay)
    after = entering_2(
        (carried, factor),
        "dp",
        combine_maps,
        (jnp.zeros_like(carried), jnp.ones_like(factor)),
        True,
    )[0]
    leaving_grads = state_grads(after, terms, resets, block_decay)
    grad_keys = (
        grad_keys
        + jnp.einsum(
            "cjhe,chde->cjhd", value_rows.astype(jnp.float32), leaving_grads, precision=exact
        )
        * key_decay[None, :, :, None]
    )
    grad_values = grad_values + jnp.einsum(
        "cjhd,chde->cjhe",
        rotated_keys.astype(jnp.float32) * key_decay[None, :, :, None],
        leaving_grads,
        precision=exact,
    )
    grad_q_pre = unrotate(grad_queries.reshape(head_shape), cosine, sine_part) * swish_slope(
        projected[:, 0].reshape(head_shape)
    )
    grad_k_pre = unrotate(grad_keys.reshape(head_shape), cosine, sine_part) * swish_slope(
        projected[:, 1].reshape(head_shape)
    )
    grad_projected = (
        jnp.stack(
            [
                grad_q_pre.reshape(row_total, width),
                grad_k_pre.reshape(row_total, width),
                grad_values.reshape(row_total, width),
                grad_gates,
            ],
            axis=1,
        )
        .astype(jnp.bfloat16)
        .reshape(row_total, 4 * width)
    )
    grad_mixer_in = cross_dot(hidden, grad_projected)
    grad_incoming = grad_middle + norm_back(
        incoming.astype(jnp.float32), grad_sums(grad_projected, mixer_in.reshape(D, -1))
    )
    return (
        grad_incoming.astype(jnp.bfloat16),
        (
            grad_mixer_in.reshape(mixer_in.shape),
            grad_mixer_out,
            grad_feed_in.reshape(feed_in.shape),
            grad_feed_out,
        ),
    )


def shards(
    tokens,
    cotangent,
    mixer_in_weight,
    mixer_out_weight,
    feed_in_weight,
    feed_out_weight,
    decay_rate,
    block_starts,
):
    section_idx = lax.axis_index("section")
    section_count = lax.axis_size("section")
    step_count = MB + section_count - 1
    weights = (mixer_in_weight[0], mixer_out_weight[0], feed_in_weight[0], feed_out_weight[0])
    decay_rates = decay_rate[0]
    received = jnp.zeros_like(tokens[0])
    outputs = jnp.zeros_like(tokens)
    stored_all = []
    for step_idx in range(step_count):
        micro_idx = step_idx - section_idx
        picked = jnp.clip(micro_idx, 0, MB - 1)
        valid = (micro_idx >= 0) & (micro_idx < MB)
        first_input = lax.dynamic_index_in_dim(tokens, picked, 0, keepdims=False)
        incoming = jnp.where(section_idx == 0, first_input, received)
        starts = lax.dynamic_index_in_dim(block_starts, picked, 0, keepdims=False)
        leaving, stored = layer_forward(incoming, weights, decay_rates, starts)
        stored_all.append(stored)
        outputs = jnp.where(
            valid, lax.dynamic_update_index_in_dim(outputs, leaving, picked, 0), outputs
        )
        if step_idx + 1 < step_count:
            received = shifted(leaving, "section", 1)
    stacked = jax.tree.map(lambda *members: jnp.stack(members), *stored_all)
    returned = jnp.zeros_like(tokens[0])
    input_grads = jnp.zeros_like(tokens)
    sums = tuple((jnp.zeros(matrix.shape, jnp.float32) for matrix in weights))
    for step_idx in range(step_count):
        micro_idx = step_idx - (section_count - 1 - section_idx)
        picked = jnp.clip(micro_idx, 0, MB - 1)
        valid = (micro_idx >= 0) & (micro_idx < MB)
        slot = jnp.clip(micro_idx + section_idx, 0, step_count - 1)
        stored = jax.tree.map(
            lambda member: lax.dynamic_index_in_dim(member, slot, 0, keepdims=False), stacked
        )
        seed_grad = lax.dynamic_index_in_dim(cotangent, picked, 0, keepdims=False)
        upstream = jnp.where(section_idx == section_count - 1, seed_grad, returned)
        starts = lax.dynamic_index_in_dim(block_starts, picked, 0, keepdims=False)
        grad_incoming, gradients = layer_backward(upstream, stored, weights, decay_rates, starts)
        sums = tuple(
            (
                running + jnp.where(valid, gradient, 0.0)
                for running, gradient in zip(sums, gradients)
            )
        )
        input_grads = jnp.where(
            valid,
            lax.dynamic_update_index_in_dim(input_grads, grad_incoming, picked, 0),
            input_grads,
        )
        if step_idx + 1 < step_count:
            returned = shifted(grad_incoming, "section", -1)
    totals = (
        lax.psum(sums[0].astype(jnp.bfloat16), "dp").astype(jnp.float32),
        lax.psum(sums[1].astype(jnp.bfloat16), "dp").astype(jnp.float32),
        lax.psum(sums[2].astype(jnp.bfloat16), "dp").astype(jnp.float32),
        lax.psum(sums[3].astype(jnp.bfloat16), "dp").astype(jnp.float32),
    )
    return (
        outputs[None],
        input_grads[None],
        totals[0][None],
        totals[1][None],
        totals[2][None],
        totals[3][None],
    )


def solution(mesh):
    placed = (
        P(None, ("dp", "tensor"), None),
        P(None, ("dp", "tensor"), None),
        P("section", None, None, "tensor"),
        P("section", "tensor", None),
        P("section", None, None, "tensor"),
        P("section", "tensor", None),
        P("section", "tensor"),
        P(),
    )
    return jax.shard_map(
        shards,
        mesh=mesh,
        in_specs=placed,
        out_specs=(
            P("section", None, ("dp", "tensor"), None),
            P("section", None, ("dp", "tensor"), None),
            P("section", None, None, "tensor"),
            P("section", "tensor", None),
            P("section", None, None, "tensor"),
            P("section", "tensor", None),
        ),
        check_vma=False,
    )
```

profile of v0, /device:TPU:0, one launch (start us, length us, event | category | flops | bytes accessed | tf_op | source)
XLA Modules:
  0.0 1810.5 jit_solution(5971297671339686558)
XLA Ops:
  98.2 15.1 all_gather.86
  158.7 27.5 %reduce-scatter.13.cloned.1.call-done = bf16[192,1024]{1,0:T(8,128)(2,1)} async-done(((bf16[768,1024]{1,0:T(8,128)(2,1)}), bf16[192,1024]{1,0:T(8,128)(2,1)}) %reduce-scatter.13.cloned.1.call-update) | async-done | bytes 393232 | tf_op jit(solution)/shard_map/reduce_scatter | solution.py:143
  189.8 31.1 %all-gather.22.cloned.1.call-done = bf16[768,1024]{1,0:T(8,128)(2,1)} async-done(((bf16[192,1024]{1,0:T(8,128)(2,1)}), bf16[768,1024]{1,0:T(8,128)(2,1)}) %all-gather.22.cloned.1.call-update) | async-done | bytes 1572880 | tf_op jit(solution)/shard_map/all_gather | solution.py:139
  229.5 31.0 %reduce-scatter.15.cloned.1.call-done = bf16[192,1024]{1,0:T(8,128)(2,1)} async-done(((bf16[768,1024]{1,0:T(8,128)(2,1)}), bf16[192,1024]{1,0:T(8,128)(2,1)}) %reduce-scatter.15.cloned.1.call-update) | async-done | bytes 393232 | tf_op jit(solution)/shard_map/reduce_scatter | solution.py:143
  279.9 18.4 %all-gather.24.cloned.1.call-done = bf16[768,1024]{1,0:T(8,128)(2,1)} async-done(((bf16[192,1024]{1,0:T(8,128)(2,1)}), bf16[768,1024]{1,0:T(8,128)(2,1)}) %all-gather.24.cloned.1.call-update) | async-done | bytes 1572880 | tf_op jit(solution)/shard_map/all_gather | solution.py:139
  358.9 18.8 %while.91 = (s32[]{:T(128)}, f32[2,128,128]{2,1,0:T(8,128)S(1)}, s32[]{:T(128)}, bf16[4,2]{0,1:T(2,128)(2,1)}, bf16[4,2,128,128]{3,2,1,0:T(8,128)(2,1)}, /*index=5*/s32[]{:T(128)}, s32[]{:T(128)}) while((s32[]{:T(128)}, f32[2,128,128]{2,1,0:T(8,128)S(1)}, s32[]{:T(128)}, bf16[4,2]{0,1:T(2,128)(2,1)}, ...), condition=%wide.region_12.13_spmd.clone, body=%wide.region_11.12_spmd.clone.sunk | while | flops 163846 | bytes 327829 | solution.py:37
  410.4 31.5 %reduce-scatter.17.cloned.1.call-done = bf16[192,1024]{1,0:T(8,128)(2,1)} async-done(((bf16[768,1024]{1,0:T(8,128)(2,1)}), bf16[192,1024]{1,0:T(8,128)(2,1)}) %reduce-scatter.17.cloned.1.call-update) | async-done | bytes 393232 | tf_op jit(solution)/shard_map/reduce_scatter | solution.py:143
  445.8 30.9 %all-gather.26.cloned.1.call-done = bf16[768,1024]{1,0:T(8,128)(2,1)} async-done(((bf16[192,1024]{1,0:T(8,128)(2,1)}), bf16[768,1024]{1,0:T(8,128)(2,1)}) %all-gather.26.cloned.1.call-update) | async-done | bytes 1572880 | tf_op jit(solution)/shard_map/all_gather | solution.py:139
  485.4 31.0 %reduce-scatter.19.cloned.1.call-done = bf16[192,1024]{1,0:T(8,128)(2,1)} async-done(((bf16[768,1024]{1,0:T(8,128)(2,1)}), bf16[192,1024]{1,0:T(8,128)(2,1)}) %reduce-scatter.19.cloned.1.call-update) | async-done | bytes 393232 | tf_op jit(solution)/shard_map/reduce_scatter | solution.py:143
  536.3 18.8 %all-gather.28.cloned.1.call-done = bf16[768,1024]{1,0:T(8,128)(2,1)} async-done(((bf16[192,1024]{1,0:T(8,128)(2,1)}), bf16[768,1024]{1,0:T(8,128)(2,1)}) %all-gather.28.cloned.1.call-update) | async-done | bytes 1572880 | tf_op jit(solution)/shard_map/all_gather | solution.py:139
  616.1 19.0 %while.92 = (s32[]{:T(128)}, f32[2,128,128]{2,1,0:T(8,128)S(1)}, s32[]{:T(128)}, bf16[4,2]{0,1:T(2,128)(2,1)}, bf16[4,2,128,128]{3,2,1,0:T(8,128)(2,1)}, /*index=5*/s32[]{:T(128)}, s32[]{:T(128)}) while((s32[]{:T(128)}, f32[2,128,128]{2,1,0:T(8,128)S(1)}, s32[]{:T(128)}, bf16[4,2]{0,1:T(2,128)(2,1)}, ...), condition=%wide.region_21.22_spmd.clone, body=%wide.region_20.21_spmd.clone.sunk | while | flops 163846 | bytes 327829 | solution.py:37
  668.5 31.5 %reduce-scatter.21.cloned.1.call-done = bf16[192,1024]{1,0:T(8,128)(2,1)} async-done(((bf16[768,1024]{1,0:T(8,128)(2,1)}), bf16[192,1024]{1,0:T(8,128)(2,1)}) %reduce-scatter.21.cloned.1.call-update) | async-done | bytes 393232 | tf_op jit(solution)/shard_map/reduce_scatter | solution.py:143
  705.6 29.2 %all-gather.30.cloned.1.call-done = bf16[768,1024]{1,0:T(8,128)(2,1)} async-done(((bf16[192,1024]{1,0:T(8,128)(2,1)}), bf16[768,1024]{1,0:T(8,128)(2,1)}) %all-gather.30.cloned.1.call-update) | async-done | bytes 1572880 | tf_op jit(solution)/shard_map/all_gather | solution.py:139
  954.8 18.8 %while.93 = (s32[]{:T(128)}, f32[2,128,128]{2,1,0:T(8,128)S(1)}, s32[]{:T(128)}, bf16[4,2]{0,1:T(2,128)(2,1)}, bf16[4,2,128,128]{3,2,1,0:T(8,128)(2,1)}, /*index=5*/s32[]{:T(128)}, s32[]{:T(128)}, s32[]{:T(128)}, s32[]{:T(128)}) while((s32[]{:T(128)}, f32[2,128,128]{2,1,0:T(8,128)S(1)}, s32[]{:T(128)}, bf16[4,2]{0,1:T(2,128)(2,1)}, ...), condition=%wide.region_35.36_spmd.clone, body=%wide.region_34.35_spmd.clone.sunk | while | flops 163850 | bytes 327891 | solution.py:37
  1011.3 25.8 %reduce-scatter.27.cloned.1.call-done = bf16[192,1024]{1,0:T(8,128)(2,1)} async-done(((bf16[768,1024]{1,0:T(8,128)(2,1)}), bf16[192,1024]{1,0:T(8,128)(2,1)}) %reduce-scatter.27.cloned.1.call-update) | async-done | bytes 393232 | tf_op jit(solution)/shard_map/reduce_scatter | solution.py:156
  1048.0 30.6 %all-gather.34.cloned.1.call-done = bf16[768,1024]{1,0:T(8,128)(2,1)} async-done(((bf16[192,1024]{1,0:T(8,128)(2,1)}), bf16[768,1024]{1,0:T(8,128)(2,1)}) %all-gather.34.cloned.1.call-update) | async-done | bytes 1572880 | tf_op jit(solution)/shard_map/all_gather | solution.py:152
  1088.3 31.0 %reduce-scatter.29.cloned.1.call-done = bf16[192,1024]{1,0:T(8,128)(2,1)} async-done(((bf16[768,1024]{1,0:T(8,128)(2,1)}), bf16[192,1024]{1,0:T(8,128)(2,1)}) %reduce-scatter.29.cloned.1.call-update) | async-done | bytes 393232 | tf_op jit(solution)/shard_map/reduce_scatter | solution.py:156
  1177.2 15.0 all_gather.103
  1192.2 18.3 %while.94 = (s32[]{:T(128)}, f32[2,128,128]{2,1,0:T(8,128)S(1)}, s32[]{:T(128)}, bf16[4,2]{0,1:T(2,128)(2,1)}, bf16[4,2,128,128]{3,2,1,0:T(8,128)(2,1)}, /*index=5*/s32[]{:T(128)}, s32[]{:T(128)}, s32[]{:T(128)}, s32[]{:T(128)}) while((s32[]{:T(128)}, f32[2,128,128]{2,1,0:T(8,128)S(1)}, s32[]{:T(128)}, bf16[4,2]{0,1:T(2,128)(2,1)}, ...), condition=%wide.region_46.47_spmd.clone, body=%wide.region_45.46_spmd.clone.sunk | while | flops 163850 | bytes 327891 | solution.py:37
  1245.5 30.7 %reduce-scatter.31.cloned.1.call-done = bf16[192,1024]{1,0:T(8,128)(2,1)} async-done(((bf16[768,1024]{1,0:T(8,128)(2,1)}), bf16[192,1024]{1,0:T(8,128)(2,1)}) %reduce-scatter.31.cloned.1.call-update) | async-done | bytes 393232 | tf_op jit(solution)/shard_map/reduce_scatter | solution.py:156
  1285.5 30.9 %all-gather.38.cloned.1.call-done = bf16[768,1024]{1,0:T(8,128)(2,1)} async-done(((bf16[192,1024]{1,0:T(8,128)(2,1)}), bf16[768,1024]{1,0:T(8,128)(2,1)}) %all-gather.38.cloned.1.call-update) | async-done | bytes 1572880 | tf_op jit(solution)/shard_map/all_gather | solution.py:152
  1341.2 15.8 reduce-scatter.33.cloned.1.call-done
  1457.2 18.4 %while.95 = (s32[]{:T(128)}, f32[2,128,128]{2,1,0:T(8,128)S(1)}, s32[]{:T(128)}, bf16[4,2]{0,1:T(2,128)(2,1)}, bf16[4,2,128,128]{3,2,1,0:T(8,128)(2,1)}, /*index=5*/s32[]{:T(128)}, s32[]{:T(128)}, s32[]{:T(128)}, s32[]{:T(128)}) while((s32[]{:T(128)}, f32[2,128,128]{2,1,0:T(8,128)S(1)}, s32[]{:T(128)}, bf16[4,2]{0,1:T(2,128)(2,1)}, ...), condition=%wide.region_57.58_spmd.clone, body=%wide.region_56.57_spmd.clone.sunk | while | flops 163850 | bytes 327891 | solution.py:37
  1548.1 243.9 %all-reduce.3.cloned.1.call-done = (bf16[1,1024,4,256]{3,1,2,0:T(8,128)(2,1)}, bf16[1,256,1024]{2,1,0:T(8,128)(2,1)}, bf16[1,1024,2,704]{1,3,2,0:T(8,128)(2,1)}, bf16[1,704,1024]{2,1,0:T(8,128)(2,1)}) async-done(((bf16[1,1024,4,256]{3,1,2,0:T(8,128)(2,1)}, bf16[1,256,1024]{2,1,0:T(8,128)(2,1)}, bf16[1,1024,2,704]{1,3,2,0:T(8,128)(2,1)}, bf16[1,704,1024]{2,1,0:T(8,128)(2,1)}), ...) | async-done | bytes 6946832 | tf_op jit(solution)/shard_map/psum | solution.py:483
  (908 shorter events, 1074.5 us)
Async XLA Ops:
  9.5 176.6 %reduce-scatter.13.cloned.1.call-start = ((), (), s32[]{:S(2)}) async-start(), calls=%async_computation.13 | async-start | bytes 1966080 | tf_op jit(solution)/shard_map/reduce_scatter | solution.py:143
  158.6 62.2 %all-gather.22.cloned.1.call-start = ((), (), s32[]{:S(2)}) async-start(), calls=%async_computation.14 | async-start | bytes 1966080 | tf_op jit(solution)/shard_map/all_gather | solution.py:139
  189.7 70.8 %reduce-scatter.15.cloned.1.call-start = ((), (), s32[]{:S(2)}) async-start(), calls=%async_computation.15 | async-start | bytes 1966080 | tf_op jit(solution)/shard_map/reduce_scatter | solution.py:143
  229.5 68.8 %all-gather.24.cloned.1.call-start = ((), (), s32[]{:S(2)}) async-start(), calls=%async_computation.16 | async-start | bytes 1966080 | tf_op jit(solution)/shard_map/all_gather | solution.py:139
  267.1 174.8 %reduce-scatter.17.cloned.1.call-start = ((), (), s32[]{:S(2)}) async-start(), calls=%async_computation.17 | async-start | bytes 1966080 | tf_op jit(solution)/shard_map/reduce_scatter | solution.py:143
  410.4 66.3 %all-gather.26.cloned.1.call-start = ((), (), s32[]{:S(2)}) async-start(), calls=%async_computation.18 | async-start | bytes 1966080 | tf_op jit(solution)/shard_map/all_gather | solution.py:139
  445.6 70.9 %reduce-scatter.19.cloned.1.call-start = ((), (), s32[]{:S(2)}) async-start(), calls=%async_computation.19 | async-start | bytes 1966080 | tf_op jit(solution)/shard_map/reduce_scatter | solution.py:143
  485.3 69.7 %all-gather.28.cloned.1.call-start = ((), (), s32[]{:S(2)}) async-start(), calls=%async_computation.20 | async-start | bytes 1966080 | tf_op jit(solution)/shard_map/all_gather | solution.py:139
  523.9 176.2 %reduce-scatter.21.cloned.1.call-start = ((), (), s32[]{:S(2)}) async-start(), calls=%async_computation.21 | async-start | bytes 1966080 | tf_op jit(solution)/shard_map/reduce_scatter | solution.py:143
  668.4 66.3 %all-gather.30.cloned.1.call-start = ((), (), s32[]{:S(2)}) async-start(), calls=%async_computation.22 | async-start | bytes 1966080 | tf_op jit(solution)/shard_map/all_gather | solution.py:139
  703.6 63.8 %all-gather.42.cloned.1.call-start = ((), (), s32[]{:S(2)}) async-start(), calls=%async_computation.35 | async-start | bytes 1966080 | tf_op jit(solution)/shard_map/all_gather | solution.py:152
  705.5 147.9 %reduce-scatter.25.cloned.1.call-start = ((), (), s32[]{:S(2)}) async-start(), calls=%async_computation.24 | async-start | bytes 1966080 | tf_op jit(solution)/shard_map/reduce_scatter | solution.py:156
  777.2 140.0 %all-gather.32.cloned.1.call-start = ((), (), s32[]{:S(2)}) async-start(), calls=%async_computation.25 | async-start | bytes 1966080 | tf_op jit(solution)/shard_map/all_gather | solution.py:152
  858.9 178.1 %reduce-scatter.27.cloned.1.call-start = ((), (), s32[]{:S(2)}) async-start(), calls=%async_computation.26 | async-start | bytes 1966080 | tf_op jit(solution)/shard_map/reduce_scatter | solution.py:156
  1008.7 70.0 %all-gather.34.cloned.1.call-start = ((), (), s32[]{:S(2)}) async-start(), calls=%async_computation.27 | async-start | bytes 1966080 | tf_op jit(solution)/shard_map/all_gather | solution.py:152
  1047.5 71.8 %reduce-scatter.29.cloned.1.call-start = ((), (), s32[]{:S(2)}) async-start(), calls=%async_computation.28 | async-start | bytes 1966080 | tf_op jit(solution)/shard_map/reduce_scatter | solution.py:156
  1088.2 66.1 %all-gather.36.cloned.1.call-start = ((), (), s32[]{:S(2)}) async-start(), calls=%async_computation.29 | async-start | bytes 1966080 | tf_op jit(solution)/shard_map/all_gather | solution.py:152
  1123.2 153.1 %reduce-scatter.31.cloned.1.call-start = ((), (), s32[]{:S(2)}) async-start(), calls=%async_computation.30 | async-start | bytes 1966080 | tf_op jit(solution)/shard_map/reduce_scatter | solution.py:156
  1245.5 71.0 %all-gather.38.cloned.1.call-start = ((), (), s32[]{:S(2)}) async-start(), calls=%async_computation.31 | async-start | bytes 1966080 | tf_op jit(solution)/shard_map/all_gather | solution.py:152
  1285.3 71.8 %reduce-scatter.33.cloned.1.call-start = ((), (), s32[]{:S(2)}) async-start(), calls=%async_computation.32 | async-start | bytes 1966080 | tf_op jit(solution)/shard_map/reduce_scatter | solution.py:156
  1326.0 95.5 %all-gather.40.cloned.1.call-start = ((), (), s32[]{:S(2)}) async-start(), calls=%async_computation.33 | async-start | bytes 1966080 | tf_op jit(solution)/shard_map/all_gather | solution.py:152
  1361.0 178.3 %reduce-scatter.23.cloned.1.call-start = ((), (), s32[]{:S(2)}) async-start(), calls=%async_computation.23 | async-start | bytes 1966080 | tf_op jit(solution)/shard_map/reduce_scatter | solution.py:143
  1397.9 145.9 %reduce-scatter.35.cloned.1.call-start = ((), (), s32[]{:S(2)}) async-start(), calls=%async_computation.34 | async-start | bytes 1966080 | tf_op jit(solution)/shard_map/reduce_scatter | solution.py:156
  1513.0 279.1 %all-reduce.3.cloned.1.call-start = ((), (), s32[]{:S(2)}) async-start(), calls=%async_computation.36 | async-start | bytes 13893632 | tf_op jit(solution)/shard_map/psum | solution.py:483
  (181 other events, 1468.6 us)
Sparse Core Ops, SparseCore 0:
  10.4 33.7 all-gather.19
  189.9 30.9 all-gather.21
  229.6 30.8 reduce-scatter.14
  267.3 30.9 all-gather.23
  410.5 31.4 reduce-scatter.16
  445.7 30.9 all-gather.25
  485.5 30.9 reduce-scatter.18
  524.0 30.9 all-gather.27
  668.5 31.4 reduce-scatter.20
  703.8 30.9 all-gather.29
  736.5 30.9 all-gather.41
  777.3 30.9 reduce-scatter.24
  859.0 28.2 all-gather.31
  1008.8 28.2 reduce-scatter.26
  1047.6 30.9 all-gather.33
  1088.3 30.8 reduce-scatter.28
  1123.3 30.9 all-gather.35
  1245.6 30.6 reduce-scatter.30
  1285.4 30.9 all-gather.37
  1326.1 30.8 reduce-scatter.32
  1361.1 30.9 all-gather.39
  1398.0 30.9 reduce-scatter.22
  1513.1 30.5 reduce-scatter.34
  1547.0 245.0 all-reduce.2
  (1 shorter events, 27.3 us)
where the time goes:
time: 1830 us; the launch traced here: 1810 us
  waiting for transfers between devices  709 us (39%)
  local copies, waits for them, and re-layouts  417 us (23%)
  other arithmetic  228 us (12%)
  blocking collectives  214 us (12%)
  matrix products  206 us (11%)
  between operations  27.7 us (2%)
    psum x1, waiting for transfers between devices, shards(): lax.psum(sums[0].astype(jnp.bfloat16), 'dp').astype(jnp.float32)  244 us
    all_gather x12, blocking collectives, entering_2(): lax.all_gather(part.astype(kind), axis)  158 us
    reduce_scatter x6, waiting for transfers between devices, row_sums(): lax.psum_scatter(jnp.dot(left, right, preferred_element_type=jnp.float32)...  153 us
    all_gather x6, waiting for transfers between devices, gather_rows(): return lax.all_gather(values, 'tensor', axis=0, tiled=True)  128 us
    reduce_scatter x6, waiting for transfers between devices, grad_sums(): lax.psum_scatter(back_dot(left, right).astype(jnp.bfloat16), 'tensor', sc...  103 us
    all_gather x6, waiting for transfers between devices, grad_rows(): return lax.all_gather(values, 'tensor', axis=0, tiled=True)  73 us
    concatenate x36, local copies, waits for them, and re-layouts, rotate(): jnp.concatenate([first_half * cosine - second * sine_part, first_half * s...  64.1 us
    unnamed x363, local copies, waits for them, and re-layouts  59.8 us
  transfers between devices with their start and end apart: 29, of which 24 were waited for; matrix products, arithmetic and copies ran while one was open for 19% of the time, Pallas kernels for 0%

commit v1 on v0

v1 whole, which is shorter than its diff:
```python
import functools

import jax
import jax.numpy as jnp
from jax import lax
from jax.experimental import pallas as pl
from jax.experimental.pallas import tpu as pltpu
from jax.sharding import PartitionSpec as P

D = 1024
HEAD = 128
BLOCK = 256
WIDTH = 256
HEADS_HERE = WIDTH // HEAD
norm_eps = 1e-06
MESH = pl.DeviceIdType.MESH
ANY = pl.BlockSpec(memory_space=pl.ANY)
SMEM = pl.BlockSpec(memory_space=pltpu.SMEM)
bf16, f32 = jnp.bfloat16, jnp.float32
VMEM_BYTES = 60 * 1024 * 1024


def place():
    return lax.axis_index("section"), lax.axis_index("dp"), lax.axis_index("tensor")


def partner(t, k):
    return ((t // 2 + k // 2) % 2) * 2 + (t + k) % 2


class Sems:
    def __init__(self, ref):
        self.ref, self.used = ref, 0

    def take(self):
        self.used += 1
        return self.ref.at[self.used - 1]


def remote(src, dst, send, recv, dev):
    return pltpu.make_async_remote_copy(
        src_ref=src, dst_ref=dst, send_sem=send, recv_sem=recv, device_id=dev, device_id_type=MESH
    )


def nn(a, b):
    return lax.dot_general(a, b, (((1,), (0,)), ((), ())), preferred_element_type=f32)


def nt(a, b):
    return lax.dot_general(a, b, (((1,), (1,)), ((), ())), preferred_element_type=f32)


def tn(a, b):
    return lax.dot_general(a, b, (((0,), (0,)), ((), ())), preferred_element_type=f32)


def rms_scale(v):
    return lax.rsqrt(jnp.mean(v * v, axis=-1, keepdims=True) + norm_eps)


def norm_back(v, u):
    q = rms_scale(v)
    n = v * q
    return q * (u - n * jnp.mean(u * n, axis=-1, keepdims=True))


def sig(v):
    return 1.0 / (1.0 + jnp.exp(-v))


def rows_of(p, n):
    return pl.ds(pl.multiple_of(p * n, n), n)


def entry(dp, s, d, t, core=False):
    barrier = pltpu.get_barrier_semaphore()
    count = 3
    for k in (1, 2, 3):
        pl.semaphore_signal(barrier, inc=1, device_id=(s, d, partner(t, k)), device_id_type=MESH)
    if core:
        pl.semaphore_signal(barrier, inc=1, device_id=(1 - s, d, t), device_id_type=MESH)
        count += 1
    if dp > 1:

        def greet(k, c):
            pl.semaphore_signal(
                barrier, inc=1, device_id=(s, (d + k) % dp, t), device_id_type=MESH
            )
            return c

        lax.fori_loop(1, dp, greet, 0)
        count += dp - 1
    pl.semaphore_wait(barrier, count)


class Gather:
    def __init__(self, block_at, half, ssem, rsem, base, where):
        self.at, self.half, self.ssem, self.rsem, self.base = block_at, half, ssem, rsem, base
        self.where = where

    def copy(self, n, peer, half, to):
        s, d, t = self.where
        ref = self.at(partner(t, peer), half)
        k = self.base + n
        return remote(ref, ref, self.ssem.at[k], self.rsem.at[k], (s, d, partner(t, to)))

    def mine(self, n):
        peer, half, to = ((0, 0, 1), (0, 1, 1), (0, 0, 2), (0, 1, 2), (1, 0, 2), (2, 1, 1))[n]
        return self.copy(n, peer, half, to)

    def arriving(self, n):
        s, d, t = self.where
        peer, half = ((1, 0), (1, 1), (2, 0), (2, 1), (3, 0), (3, 1))[n]
        ref = self.at(partner(t, peer), half)
        k = self.base + n
        return remote(ref, ref, self.ssem.at[k], self.rsem.at[k], (s, d, t))

    def start(self):
        self.mine(0).start()
        self.mine(3).start()
        self.mine(1).start()
        self.mine(2).start()

    def forward(self):
        self.arriving(0).wait_recv()
        self.mine(4).start()
        self.arriving(3).wait_recv()
        self.mine(5).start()

    def ready(self, k):
        if k == 1:
            self.arriving(1).wait_recv()
        elif k == 2:
            self.arriving(2).wait_recv()
        else:
            self.arriving(4).wait_recv()
            self.arriving(5).wait_recv()

    def drain(self):
        for n in range(6):
            self.mine(n).wait_send()


class Scatter:
    def __init__(self, part, got, via, rows, ssem, rsem, base, where):
        self.part, self.got, self.via, self.half = part, got, via, rows // 2
        self.ssem, self.rsem, self.base, self.where = ssem, rsem, base, where

    def copy(self, n):
        s, d, t = self.where
        h = self.half
        h0, h1 = pl.ds(0, h), pl.ds(h, h)
        src, dst, to = (
            (self.part.at[2, h0], self.via.at[0], 2),
            (self.part.at[2, h1], self.via.at[1], 1),
            (self.part.at[0, h1], self.got.at[0, h1], 1),
            (self.part.at[1, h0], self.got.at[1, h0], 2),
            (self.part.at[0, h0], self.got.at[0, h0], 1),
            (self.part.at[1, h1], self.got.at[1, h1], 2),
        )[n]
        k = self.base + n
        return remote(src, dst, self.ssem.at[k], self.rsem.at[k], (s, d, partner(t, to)))

    def put(self, k, value):
        self.part[k - 1] = value.astype(bf16)
        self.send(k)

    def send(self, k):
        if k == 3:
            self.copy(0).start()
            self.copy(1).start()
        elif k == 2:
            self.copy(3).start()
        else:
            self.copy(2).start()

    def combine(self):
        h = self.half
        self.copy(0).wait_recv()
        self.part[0, 0:h] = (self.part[0, 0:h].astype(f32) + self.via[0].astype(f32)).astype(bf16)
        self.copy(4).start()
        self.copy(1).wait_recv()
        self.part[1, h:] = (self.part[1, h:].astype(f32) + self.via[1].astype(f32)).astype(bf16)
        self.copy(5).start()

    def result(self):
        for n in (2, 3, 4, 5):
            self.copy(n).wait_recv()
        return self.got[0].astype(f32) + self.got[1].astype(f32)

    def drain(self):
        for n in range(6):
            self.copy(n).wait_send()


def prep_kernel(wi, wo, wfi, wfo, all_wi, all_wo, all_wfi, all_wfo, lsem, ssem, rsem):
    s, d, t = place()
    entry(1, s, d, t, core=True)
    other = (1 - s, d, t)

    def shard(p):
        return all_wo.at[s, rows_of(p, WIDTH)]

    def theirs(p):
        return all_wo.at[1 - s, rows_of(p, WIDTH)]

    pairs = ((wi, all_wi.at[s]), (wfi, all_wfi.at[s]), (wfo, all_wfo.at[s]), (wo, shard(t)))
    hops = [remote(wo, shard(t), ssem.at[6 + k], rsem.at[6 + k], (s, d, partner(t, k))) for k in (1, 2, 3)]
    for hop in hops:
        hop.start()
    over = [remote(src, dst, ssem.at[n], rsem.at[n], other) for n, (src, dst) in enumerate(pairs)]
    own = [pltpu.make_async_copy(src, dst, lsem.at[n]) for n, (src, dst) in enumerate(pairs)]
    for copy in over + own:
        copy.start()
    passed = []
    for k in (1, 2, 3):
        p = partner(t, k)
        remote(wo, shard(p), ssem.at[6 + k], rsem.at[6 + k], other).wait_recv()
        copy = remote(shard(p), shard(p), ssem.at[3 + k], rsem.at[3 + k], other)
        copy.start()
        passed.append(copy)
    for copy in own:
        copy.wait()
    incoming = (all_wi.at[1 - s], all_wfi.at[1 - s], all_wfo.at[1 - s], theirs(t))
    for n, dst in enumerate(incoming):
        remote(dst, dst, ssem.at[n], rsem.at[n], other).wait_recv()
    for k in (1, 2, 3):
        dst = theirs(partner(t, k))
        remote(dst, dst, ssem.at[3 + k], rsem.at[3 + k], other).wait_recv()
    for copy in over + passed + hops:
        copy.wait_send()


def share_weights(wi, wo, wfi, wfo):
    fp = wfo.shape[0]
    outs = (
        jax.ShapeDtypeStruct((2, D, 4 * WIDTH), bf16),
        jax.ShapeDtypeStruct((2, D, D), bf16),
        jax.ShapeDtypeStruct((2, 2, D, fp), bf16),
        jax.ShapeDtypeStruct((2, fp, D), bf16),
    )
    return pl.pallas_call(
        prep_kernel,
        out_shape=outs,
        in_specs=[ANY] * 4,
        out_specs=(ANY,) * 4,
        scratch_shapes=[
            pltpu.SemaphoreType.DMA((4,)),
            pltpu.SemaphoreType.DMA((10,)),
            pltpu.SemaphoreType.DMA((10,)),
        ],
        compiler_params=pltpu.CompilerParams(collective_id=0, has_side_effects=True),
        name="share_weights",
    )(wi, wo, wfi, wfo)


def scalar_table(starts, rates, dp, blocks):
    d = lax.axis_index("dp")
    survive = 1.0 - starts.astype(f32).reshape(dp, blocks)
    decay = jnp.exp(-rates * BLOCK)
    factor = jnp.prod(survive, axis=1)[:, None] * (decay**blocks)[None, :]
    at = jnp.arange(dp)
    low, high = jnp.minimum(at, d), jnp.maximum(at, d)
    between = (at[None, :] > low[:, None]) & (at[None, :] < high[:, None])
    through = jnp.prod(jnp.where(between[:, :, None], factor[None], 1.0), axis=1)
    forward = jnp.where((at < d)[:, None], through, 0.0)
    backward = jnp.where((at > d)[:, None], through, 0.0)
    mine = lax.dynamic_index_in_dim(survive, d, 0, keepdims=False)
    return jnp.concatenate([mine, rates, decay, forward.reshape(-1), backward.reshape(-1)])


def decay_fill(scal, nb, mask, mask_t, qd, kd):
    for h in range(HEADS_HERE):
        r = scal[nb + h]
        i = lax.broadcasted_iota(jnp.int32, (BLOCK, BLOCK), 0).astype(f32)
        j = lax.broadcasted_iota(jnp.int32, (BLOCK, BLOCK), 1).astype(f32)
        gap = i - j
        mask[h] = jnp.where(gap >= 0.0, jnp.exp(-r * jnp.maximum(gap, 0.0)), 0.0)
        if mask_t is not None:
            mask_t[h] = jnp.where(gap <= 0.0, jnp.exp(-r * jnp.maximum(-gap, 0.0)), 0.0)
        i = lax.broadcasted_iota(jnp.int32, (BLOCK, HEAD), 0).astype(f32)
        qd[h] = jnp.exp(-r * (i + 1.0))
        kd[h] = jnp.exp(-r * (BLOCK - 1.0 - i))


def head(h):
    return slice(h * HEAD, (h + 1) * HEAD)


def send_states(dp, where, zout, zin, zs, zr, later):
    s, d, t = where

    def each(k, c):
        to = d + k if later else d - k

        @pl.when((to < dp) if later else (to >= 0))
        def _():
            remote(zout, zin.at[d], zs.at[k], zr.at[d], (s, to, t)).start()

        return c

    lax.fori_loop(1, dp, each, 0)


def sent_states(dp, where, zout, zin, zs, zr, later):
    s, d, t = where

    def each(k, c):
        to = d + k if later else d - k

        @pl.when((to < dp) if later else (to >= 0))
        def _():
            remote(zout, zin.at[d], zs.at[k], zr.at[d], (s, to, t)).wait_send()

        return c

    lax.fori_loop(1, dp, each, 0)


def take_states(dp, where, zout, zin, zs, zr, later, scal, base, run):
    s, d, t = where
    run[...] = jnp.zeros_like(run)

    def each(k, c):
        @pl.when((k < d) if later else (k > d))
        def _():
            remote(zout, zin.at[k], zs.at[0], zr.at[k], (s, d, t)).wait_recv()
            for h in range(HEADS_HERE):
                run[h] += scal[base + 2 * k + h] * zin[k, h].astype(f32)

        return c

    lax.fori_loop(0, dp, each, 0)


def forward_kernel(
    dp, layer, first, x_in, all_wi, all_wo, all_wfi, all_wfo, cos2, sin2, scal,
    y_out, hidden_o, zq_o, zk_o, gate_o, q_o, k_o, v_o, att_o, sc_o, states_o, branch_o, mid_o,
    hid2_o, pair_o,
    wi, wo, wfi, wfo, cosv, sinv, xf, hidden, zq, zk, gate, q, k, v, att, sc, states, branch, mid, hid2,
    pair, mask, qd, kd, loc, zout, zin, run, u, y, part, got, via, ssq, own, yb,
    lsem, ssem, rsem, zs, zr,
):
    where = s, d, t = place()
    rows = x_in.shape[-2]
    total = 4 * rows
    nb = total // BLOCK
    local = Sems(lsem)

    def load(src, dst):
        copy = pltpu.make_async_copy(src, dst, local.take())
        copy.start()
        return copy

    x_src = x_in.at[s] if first else x_in
    got_x = load(x_src, xf.at[rows_of(t, rows)])
    got_wi = load(all_wi.at[layer], wi)
    got_cos, got_sin = load(cos2, cosv), load(sin2, sinv)
    got_wo = load(all_wo.at[layer], wo)
    got_wfi = load(all_wfi.at[layer], wfi)
    got_wfo = load(all_wfo.at[layer], wfo)
    entry(dp, s, d, t)
    got_x.wait()

    half = rows // 2
    gx = Gather(
        lambda p, h: xf.at[pl.ds(pl.multiple_of(p * rows + h * half, half), half)],
        half, ssem, rsem, 0, where,
    )
    gx.start()
    decay_fill(scal, nb, mask, None, qd, kd)
    got_wi.wait()
    got_cos.wait()
    got_sin.wait()

    def project(i, c):
        for n in (1, 2, 3):

            @pl.when(i == n)
            def _(n=n):
                if n == 1:
                    gx.forward()
                gx.ready(n)

        r = rows_of(partner(t, i), rows)
        xv = xf[r, :].astype(f32)
        hid = (xv * rms_scale(xv)).astype(bf16)
        hidden[r, :] = hid
        cs, sn = cosv[r, :], sinv[r, :]
        for n, (pre, post) in enumerate(((zq, q), (zk, k))):
            z = nn(hid, wi[:, n * WIDTH : (n + 1) * WIDTH])
            pre[r, :] = z
            a = z * sig(z)
            for h in range(HEADS_HERE):
                ah = a[:, head(h)]
                post[r, head(h)] = (ah * cs + pltpu.roll(ah, HEAD // 2, 1) * sn).astype(bf16)
        v[r, :] = nn(hid, wi[:, 2 * WIDTH : 3 * WIDTH]).astype(bf16)
        gate[r, :] = nn(hid, wi[:, 3 * WIDTH :])
        return c

    lax.fori_loop(0, 4, project, 0)
    stores = [load(hidden, hidden_o), load(zq, zq_o), load(zk, zk_o), load(gate, gate_o)]
    stores += [load(q, q_o), load(k, k_o), load(v, v_o)]

    def local_state(b, c):
        r = rows_of(b, BLOCK)
        for h in range(HEADS_HERE):
            kdec = (k[r, head(h)].astype(f32) * kd[h]).astype(bf16)
            loc[b, h] = tn(kdec, v[r, head(h)])
        return c

    lax.fori_loop(0, nb, local_state, 0)
    for h in range(HEADS_HERE):
        carried = loc[0, h]
        for b in range(1, nb):
            carried = (scal[nb + 2 + h] * scal[b]) * carried + loc[b, h]
        zout[h] = carried.astype(bf16)
    send_states(dp, where, zout, zin, zs, zr, True)

    def inner(b, c):
        r = rows_of(b, BLOCK)
        for h in range(HEADS_HERE):
            w = (nt(q[r, head(h)], k[r, head(h)]) * mask[h]).astype(bf16)
            att[r, head(h)] = nn(w, v[r, head(h)])
        return c

    lax.fori_loop(0, nb, inner, 0)
    take_states(dp, where, zout, zin, zs, zr, True, scal, nb + 4, run)

    def outer(b, c):
        r = rows_of(b, BLOCK)
        for h in range(HEADS_HERE):
            entering = scal[b] * run[h]
            states[b, h] = entering
            run[h] = scal[nb + 2 + h] * entering + loc[b, h]
            qdec = (q[r, head(h)].astype(f32) * qd[h]).astype(bf16)
            a = att[r, head(h)] + nn(qdec, entering.astype(bf16))
            att[r, head(h)] = a
            u[t, r, head(h)] = (a * gate[r, head(h)]).astype(bf16)
        return c

    lax.fori_loop(0, nb, outer, 0)

    hu = total // 2
    gu = Gather(lambda p, h: u.at[p, pl.ds(h * hu, hu)], hu, ssem, rsem, 6, where)
    gu.start()
    for b in range(nb):
        a = att[b * BLOCK : (b + 1) * BLOCK, :]
        ssq[0, :, b * BLOCK : (b + 1) * BLOCK] = lax.dot_general(
            jnp.ones((8, WIDTH), f32), a * a, (((1,), (1,)), ((), ())),
            preferred_element_type=f32, precision=lax.Precision.HIGHEST,
        )
    sums = [
        remote(ssq.at[0], ssq.at[n], ssem.at[11 + n], rsem.at[11 + n], (s, d, partner(t, n)))
        for n in (1, 2, 3)
    ]
    for copy in sums:
        copy.start()
    stores += [load(att, att_o), load(states, states_o)]
    got_wo.wait()
    y[...] = jnp.zeros_like(y)

    def out_project(i, c):
        for n in (1, 2, 3):

            @pl.when(i == n)
            def _(n=n):
                if n == 1:
                    gu.forward()
                gu.ready(n)

        p = partner(t, i)

        def chunk(m, c):
            r = rows_of(m, rows)
            y[r, :] += nn(u[p, r, :], wo[rows_of(p, WIDTH), :])
            return c

        return lax.fori_loop(0, 4, chunk, c)

    lax.fori_loop(0, 4, out_project, 0)
    for copy in sums:
        copy.wait_recv()
    whole = ssq[0] + ssq[1] + ssq[2] + ssq[3]
    sc[...] = jnp.transpose(lax.rsqrt(whole * (1.0 / D) + norm_eps))
    got_wfi.wait()
    got_wfo.wait()
    out = Scatter(part, got, via, rows, ssem, rsem, 15, where)

    def feed(i, c):
        e = 3 - i
        r = rows_of(partner(t, e), rows)
        br = sc[r, 0:1] * y[r, :]
        branch[r, :] = br.astype(bf16)
        m = xf[r, :].astype(f32) + br
        h2 = (m * rms_scale(m)).astype(bf16)
        hid2[r, :] = h2
        p0, p1 = nn(h2, wfi[0]), nn(h2, wfi[1])
        pair[0, r, :] = p0
        pair[1, r, :] = p1
        o = nn((p0 * p1).astype(bf16), wfo[...])
        for n in (1, 2, 3):

            @pl.when(e == n)
            def _(n=n):
                out.put(n, o)

        @pl.when(e == 0)
        def _():
            mid[...] = m
            own[...] = o + m

        return c

    lax.fori_loop(0, 4, feed, 0)
    stores += [load(sc, sc_o), load(branch, branch_o), load(mid, mid_o), load(hid2, hid2_o)]
    stores += [load(pair, pair_o)]
    out.combine()
    yb[...] = (own[...] + out.result()).astype(bf16)
    stores += [load(yb, y_out)]
    gx.drain()
    gu.drain()
    out.drain()
    for copy in sums:
        copy.wait_send()
    sent_states(dp, where, zout, zin, zs, zr, True)
    for copy in stores:
        copy.wait()


def layer_forward(layer, first, x, weights, cos2, sin2, scal, dp, uid):
    rows = x.shape[-2]
    total = 4 * rows
    nb = total // BLOCK
    fp = weights[3].shape[1]
    saved = [
        ((rows, D), bf16), ((total, D), bf16), ((total, WIDTH), f32), ((total, WIDTH), f32),
        ((total, WIDTH), f32), ((total, WIDTH), bf16), ((total, WIDTH), bf16),
        ((total, WIDTH), bf16), ((total, WIDTH), f32), ((total, 8), f32),
        ((nb, HEADS_HERE, HEAD, HEAD), f32), ((total, D), bf16), ((rows, D), f32),
        ((total, D), bf16), ((2, total, fp), f32),
    ]
    scratch = [
        ((D, 4 * WIDTH), bf16), ((D, D), bf16), ((2, D, fp), bf16), ((fp, D), bf16),
        ((total, HEAD), f32), ((total, HEAD), f32), ((total, D), bf16),
    ]
    scratch += saved[1:]
    scratch += [
        ((HEADS_HERE, BLOCK, BLOCK), f32), ((HEADS_HERE, BLOCK, HEAD), f32),
        ((HEADS_HERE, BLOCK, HEAD), f32), ((nb, HEADS_HERE, HEAD, HEAD), f32),
        ((HEADS_HERE, HEAD, HEAD), bf16), ((dp, HEADS_HERE, HEAD, HEAD), bf16),
        ((HEADS_HERE, HEAD, HEAD), f32), ((4, total, WIDTH), bf16), ((total, D), f32),
        ((3, rows, D), bf16), ((2, rows, D), bf16), ((2, rows // 2, D), bf16),
        ((4, 8, total), f32), ((rows, D), f32), ((rows, D), bf16),
    ]
    flops = 2 * total * D * (4 * WIDTH + D + 3 * fp)
    return pl.pallas_call(
        functools.partial(forward_kernel, dp, layer, first),
        out_shape=tuple(jax.ShapeDtypeStruct(a, b) for a, b in saved),
        in_specs=[ANY] * 7 + [SMEM],
        out_specs=(ANY,) * len(saved),
        scratch_shapes=[pltpu.VMEM(a, b) for a, b in scratch]
        + [
            pltpu.SemaphoreType.DMA((24,)),
            pltpu.SemaphoreType.DMA((21,)),
            pltpu.SemaphoreType.DMA((21,)),
            pltpu.SemaphoreType.DMA((dp,)),
            pltpu.SemaphoreType.DMA((dp,)),
        ],
        compiler_params=pltpu.CompilerParams(
            collective_id=uid, has_side_effects=True, vmem_limit_bytes=VMEM_BYTES
        ),
        cost_estimate=pl.CostEstimate(flops=flops, bytes_accessed=20 << 20, transcendentals=0),
        name="layer_forward",
    )(x, *weights, cos2, sin2, scal)


def backward_kernel(
    dp, layer, last, first, g_in, x_in, all_wi, all_wo, all_wfi, all_wfo, cos2, sin2, scal,
    hidden_i, zq_i, zk_i, gate_i, q_i, k_i, v_i, att_i, sc_i, states_i, branch_i, mid_i, hid2_i, pair_i,
    g_out, gwi_o, gwo_o, gwfi_o, gwfo_o,
    wi, wo, wfi, wfo, cosv, sinv, gf, xr, hidden, zq, zk, gate, q, k, v, att, sc, states, branch, mid,
    hid2, pair, mask, mask_t, qd, kd, terms, zout, zin, run, gpair, prod, gb, gm, gated, gatt, dv, dk, gp,
    part, got, via, part2, got2, via2, own, own2, gwi, gwo, gwfi, gwfo, gr,
    lsem, ssem, rsem, zs, zr,
):
    where = s, d, t = place()
    rows = g_out.shape[0]
    total = 4 * rows
    nb = total // BLOCK
    local = Sems(lsem)

    def load(src, dst):
        copy = pltpu.make_async_copy(src, dst, local.take())
        copy.start()
        return copy

    got_g = load(g_in.at[s] if last else g_in, gf.at[rows_of(t, rows)])
    early = [load(all_wfo.at[layer], wfo), load(pair_i, pair), load(all_wfi.at[layer], wfi)]
    mids = [load(mid_i, mid), load(hid2_i, hid2)]
    gates = [
        load(all_wo.at[layer, rows_of(t, WIDTH)], wo), load(branch_i, branch), load(sc_i, sc),
        load(att_i, att), load(gate_i, gate),
    ]
    attn = [
        load(q_i, q), load(k_i, k), load(v_i, v), load(states_i, states), load(cos2, cosv),
        load(sin2, sinv), load(zq_i, zq), load(zk_i, zk),
    ]
    ends = [
        load(all_wi.at[layer], wi), load(hidden_i, hidden), load(x_in.at[s] if first else x_in, xr)
    ]
    entry(dp, s, d, t)
    got_g.wait()
    half = rows // 2

    def block_of(ref):
        return lambda p, h: ref.at[pl.ds(pl.multiple_of(p * rows + h * half, half), half)]

    gg = Gather(block_of(gf), half, ssem, rsem, 0, where)
    gg.start()
    decay_fill(scal, nb, mask, mask_t, qd, kd)
    for copy in early:
        copy.wait()
    sums = Scatter(part, got, via, rows, ssem, rsem, 6, where)

    def feed(i, c):
        for n in (1, 2, 3):

            @pl.when(i == n)
            def _(n=n):
                if n == 1:
                    gg.forward()
                gg.ready(n)

        r = rows_of(partner(t, i), rows)
        grad = nt(gf[r, :], wfo[...])
        p0, p1 = pair[0, r, :], pair[1, r, :]
        prod[r, :] = (p0 * p1).astype(bf16)
        g0, g1 = (grad * p1).astype(bf16), (grad * p0).astype(bf16)
        gpair[0, r, :] = g0
        gpair[1, r, :] = g1
        o = nt(g0, wfi[0]) + nt(g1, wfi[1])
        for n in (1, 2, 3):

            @pl.when(i == n)
            def _(n=n):
                sums.put(n, o)

        @pl.when(i == 0)
        def _():
            own[...] = o

        return c

    lax.fori_loop(0, 4, feed, 0)
    sums.combine()
    for copy in mids:
        copy.wait()
    fp = wfo.shape[0]

    def feed_weights(n, c):
        cols = rows_of(n, 256)
        a = hid2[:, cols]
        gwfi[0, cols, :] = tn(a, gpair[0]).astype(bf16)
        gwfi[1, cols, :] = tn(a, gpair[1]).astype(bf16)
        return c

    def out_weights(n, c):
        cols = rows_of(n, 256)
        gwfo[cols, :] = tn(prod[:, cols], gf[...]).astype(bf16)
        return c

    lax.fori_loop(0, D // 256, feed_weights, 0)
    lax.fori_loop(0, fp // 256, out_weights, 0)
    stores = [load(gwfi, gwfi_o), load(gwfo, gwfo_o)]
    me = rows_of(t, rows)
    grad_middle = gf[me, :].astype(f32) + norm_back(mid[...], own[...] + sums.result())
    gm[...] = grad_middle
    gb[me, :] = grad_middle.astype(bf16)

    gbg = Gather(block_of(gb), half, ssem, rsem, 12, where)
    gbg.start()
    for copy in gates:
        copy.wait()

    def gating(i, c):
        for n in (1, 2, 3):

            @pl.when(i == n)
            def _(n=n):
                if n == 1:
                    gbg.forward()
                gbg.ready(n)

        r = rows_of(partner(t, i), rows)
        b = gb[r, :]
        grad = nt(b, wo[...])
        dots = jnp.sum(b.astype(f32) * branch[r, :].astype(f32), axis=-1, keepdims=True) * (1.0 / D)
        scale = sc[r, 0:1]
        normed = att[r, :] * scale
        gt = gate[r, :]
        gp[r, 3 * WIDTH :] = (grad * normed).astype(bf16)
        gated[r, :] = (normed * gt).astype(bf16)
        gatt[r, :] = (scale * (grad * gt - normed * dots)).astype(bf16)
        return c

    lax.fori_loop(0, 4, gating, 0)
    for copy in attn:
        copy.wait()

    def term(b, c):
        r = rows_of(b, BLOCK)
        for h in range(HEADS_HERE):
            qdec = (q[r, head(h)].astype(f32) * qd[h]).astype(bf16)
            terms[b, h] = tn(qdec, gatt[r, head(h)])
        return c

    lax.fori_loop(0, nb, term, 0)
    for h in range(HEADS_HERE):
        carried = scal[nb - 1] * terms[nb - 1, h]
        for b in reversed(range(nb - 1)):
            carried = scal[b] * (terms[b, h] + scal[nb + 2 + h] * carried)
        zout[h] = carried.astype(bf16)
    send_states(dp, where, zout, zin, zs, zr, False)

    def unturn(pre, grad, r, h):
        back = grad * cosv[r, :] - pltpu.roll(grad, HEAD // 2, 1) * sinv[r, :]
        z = pre[r, head(h)]
        g = sig(z)
        return (back * (g * (1.0 + z * (1.0 - g)))).astype(bf16)

    def inner(b, c):
        r = rows_of(b, BLOCK)
        for h in range(HEADS_HERE):
            qh, kh, vh, gh = q[r, head(h)], k[r, head(h)], v[r, head(h)], gatt[r, head(h)]
            w_t = (nt(kh, qh) * mask_t[h]).astype(bf16)
            dv[r, head(h)] = nn(w_t, gh)
            ds = (nt(gh, vh) * mask[h]).astype(bf16)
            ds_t = (nt(vh, gh) * mask_t[h]).astype(bf16)
            dk[r, head(h)] = nn(ds_t, qh)
            dq = nn(ds, kh) + nt(gh, states[b, h].astype(bf16)) * qd[h]
            gp[r, head(h)] = unturn(zq, dq, r, h)
        return c

    lax.fori_loop(0, nb, inner, 0)
    take_states(dp, where, zout, zin, zs, zr, False, scal, nb + 4 + 2 * dp, run)

    def outer(i, c):
        b = nb - 1 - i
        r = rows_of(b, BLOCK)
        for h in range(HEADS_HERE):
            after = run[h]
            low = after.astype(bf16)
            run[h] = scal[b] * (terms[b, h] + scal[nb + 2 + h] * after)
            kdec = (k[r, head(h)].astype(f32) * kd[h]).astype(bf16)
            dkh = dk[r, head(h)] + nt(v[r, head(h)], low) * kd[h]
            k_cols = slice(WIDTH + h * HEAD, WIDTH + (h + 1) * HEAD)
            v_cols = slice(2 * WIDTH + h * HEAD, 2 * WIDTH + (h + 1) * HEAD)
            gp[r, k_cols] = unturn(zk, dkh, r, h)
            gp[r, v_cols] = (dv[r, head(h)] + nn(kdec, low)).astype(bf16)
        return c

    lax.fori_loop(0, nb, outer, 0)
    for copy in ends:
        copy.wait()
    ins = Scatter(part2, got2, via2, rows, ssem, rsem, 18, where)

    def back_in(i, c):
        e = 3 - i
        r = rows_of(partner(t, e), rows)
        o = nt(gp[r, :], wi[...])
        for n in (1, 2, 3):

            @pl.when(e == n)
            def _(n=n):
                ins.put(n, o)

        @pl.when(e == 0)
        def _():
            own2[...] = o

        return c

    lax.fori_loop(0, 4, back_in, 0)
    ins.combine()

    def in_weights(n, c):
        cols = rows_of(n, 256)
        gwi[cols, :] = tn(hidden[:, cols], gp[...]).astype(bf16)
        return c

    lax.fori_loop(0, D // 256, in_weights, 0)
    gwo[...] = tn(gated[...], gb[...]).astype(bf16)
    stores += [load(gwi, gwi_o), load(gwo, gwo_o)]
    dx = gm[...] + norm_back(xr[...].astype(f32), own2[...] + ins.result())
    gr[...] = dx.astype(bf16)
    stores += [load(gr, g_out)]
    gg.drain()
    sums.drain()
    gbg.drain()
    ins.drain()
    sent_states(dp, where, zout, zin, zs, zr, False)
    for copy in stores:
        copy.wait()


def layer_backward(layer, last, first, g, x, weights, cos2, sin2, scal, saved, dp, uid):
    rows = g.shape[-2]
    total = 4 * rows
    nb = total // BLOCK
    fp = weights[3].shape[1]
    outs = [
        ((rows, D), bf16), ((D, 4 * WIDTH), bf16), ((WIDTH, D), bf16), ((2, D, fp), bf16), ((fp, D), bf16)
    ]
    scratch = [
        ((D, 4 * WIDTH), bf16), ((WIDTH, D), bf16), ((2, D, fp), bf16), ((fp, D), bf16),
        ((total, HEAD), f32), ((total, HEAD), f32), ((total, D), bf16), ((rows, D), bf16),
    ]
    scratch += [(a.shape, a.dtype) for a in saved]
    scratch += [
        ((HEADS_HERE, BLOCK, BLOCK), f32), ((HEADS_HERE, BLOCK, BLOCK), f32),
        ((HEADS_HERE, BLOCK, HEAD), f32), ((HEADS_HERE, BLOCK, HEAD), f32),
        ((nb, HEADS_HERE, HEAD, HEAD), f32), ((HEADS_HERE, HEAD, HEAD), bf16),
        ((dp, HEADS_HERE, HEAD, HEAD), bf16), ((HEADS_HERE, HEAD, HEAD), f32),
        ((2, total, fp), bf16), ((total, fp), bf16), ((total, D), bf16), ((rows, D), f32),
        ((total, WIDTH), bf16), ((total, WIDTH), bf16), ((total, WIDTH), f32), ((total, WIDTH), f32),
        ((total, 4 * WIDTH), bf16),
        ((3, rows, D), bf16), ((2, rows, D), bf16), ((2, rows // 2, D), bf16),
        ((3, rows, D), bf16), ((2, rows, D), bf16), ((2, rows // 2, D), bf16),
        ((rows, D), f32), ((rows, D), f32),
        ((D, 4 * WIDTH), bf16), ((WIDTH, D), bf16), ((2, D, fp), bf16), ((fp, D), bf16), ((rows, D), bf16),
    ]
    flops = 4 * total * D * (4 * WIDTH + WIDTH + 3 * fp)
    return pl.pallas_call(
        functools.partial(backward_kernel, dp, layer, last, first),
        out_shape=tuple(jax.ShapeDtypeStruct(a, b) for a, b in outs),
        in_specs=[ANY] * 8 + [SMEM] + [ANY] * len(saved),
        out_specs=(ANY,) * len(outs),
        scratch_shapes=[pltpu.VMEM(a, b) for a, b in scratch]
        + [
            pltpu.SemaphoreType.DMA((30,)),
            pltpu.SemaphoreType.DMA((24,)),
            pltpu.SemaphoreType.DMA((24,)),
            pltpu.SemaphoreType.DMA((dp,)),
            pltpu.SemaphoreType.DMA((dp,)),
        ],
        compiler_params=pltpu.CompilerParams(
            collective_id=uid, has_side_effects=True, vmem_limit_bytes=VMEM_BYTES
        ),
        cost_estimate=pl.CostEstimate(flops=flops, bytes_accessed=30 << 20, transcendentals=0),
        name="layer_backward",
    )(g, x, *weights, cos2, sin2, scal, *saved)


def angle_tables(starts, blocks):
    d = lax.axis_index("dp")
    at = jnp.arange(starts.shape[0], dtype=jnp.int32)
    begins = jnp.max(
        jnp.where((at[None, :] <= at[:, None]) & (starts > 0)[None, :], at[None, :], 0), axis=1
    )
    offsets = lax.dynamic_slice_in_dim((at - begins) * BLOCK, d * blocks, blocks)
    places = (offsets[:, None] + jnp.arange(BLOCK, dtype=jnp.int32)[None, :]).reshape(-1)
    lane = jnp.arange(HEAD, dtype=jnp.int32)
    frequency = 10000.0 ** (-(lane % (HEAD // 2)).astype(f32) / (HEAD // 2))
    angles = places.astype(f32)[:, None] * frequency[None, :]
    return jnp.cos(angles), jnp.where(lane < HEAD // 2, -1.0, 1.0)[None, :] * jnp.sin(angles)


def swap(x):
    return lax.ppermute(x, "section", [(0, 1), (1, 0)])


def mine_first(s, a, b):
    return jnp.where(s == 0, a, b)


def core_halves(grads, s):
    total = []
    for g in grads:
        pieces = g.reshape((2, g.shape[0] // 2) + g.shape[1:])
        keep = lax.dynamic_index_in_dim(pieces, s, 0, keepdims=False)
        give = lax.dynamic_index_in_dim(pieces, 1 - s, 0, keepdims=False)
        total.append((keep.astype(f32) + swap(give).astype(f32)).astype(bf16))
    return lax.psum(tuple(total), "dp")


def shards(tokens, cotangent, mixer_in, mixer_out, feed_in, feed_out, decay_rate, block_starts):
    s = lax.axis_index("section")
    dp = lax.axis_size("dp")
    rows = tokens.shape[1]
    blocks = 4 * rows // BLOCK
    ff = feed_out.shape[1]
    fp = -(-ff // 256) * 256
    wi = mixer_in[0].reshape(D, 4 * WIDTH)
    wfi = jnp.pad(jnp.swapaxes(feed_in[0], 0, 1), ((0, 0), (0, 0), (0, fp - ff)))
    wfo = jnp.pad(feed_out[0], ((0, fp - ff), (0, 0)))
    weights = share_weights(wi, mixer_out[0], wfi, wfo)
    other_rates = swap(decay_rate[0])
    rates = (mine_first(s, decay_rate[0], other_rates), mine_first(s, other_rates, decay_rate[0]))
    starts = lax.dynamic_index_in_dim(block_starts, s, 0, keepdims=False)
    cos2, sin2 = angle_tables(starts, blocks)
    scal = [scalar_table(starts, r, dp, blocks) for r in rates]

    y0, *saved0 = layer_forward(0, True, tokens, weights, cos2, sin2, scal[0], dp, 1)
    y1, *saved1 = layer_forward(1, False, y0, weights, cos2, sin2, scal[1], dp, 2)
    g1, *grads1 = layer_backward(1, True, False, cotangent, y0, weights, cos2, sin2, scal[1], saved1, dp, 3)
    half1 = core_halves((grads1[0], grads1[1], grads1[2], grads1[3]), s)
    g0, *grads0 = layer_backward(0, False, True, g1, tokens, weights, cos2, sin2, scal[0], saved0, dp, 4)
    half0 = core_halves((grads0[0], grads0[1], grads0[2], grads0[3]), s)

    theirs = swap(jnp.stack([mine_first(s, y1, y0), mine_first(s, g1, g0)]))
    keep_y, keep_g = mine_first(s, y0, y1), mine_first(s, g0, g1)
    outputs = jnp.stack([mine_first(s, keep_y, theirs[0]), mine_first(s, theirs[0], keep_y)])
    in_grads = jnp.stack([mine_first(s, keep_g, theirs[1]), mine_first(s, theirs[1], keep_g)])
    full = []
    for h0, h1 in zip(half0, half1):
        got = swap(mine_first(s, h1, h0))
        kept = mine_first(s, h0, h1)
        full.append(
            jnp.stack([mine_first(s, kept, got), mine_first(s, got, kept)])
            .reshape((-1,) + h0.shape[1:])
            .astype(f32)
        )
    g_in = full[0].reshape(D, 4, WIDTH)
    g_feed_in = jnp.swapaxes(full[2].reshape(2, D, fp)[:, :, :ff], 0, 1)
    return (
        outputs[None], in_grads[None], g_in[None], full[1][None], g_feed_in[None], full[3][:ff][None]
    )


def solution(mesh):
    placed = (
        P(None, ("dp", "tensor"), None),
        P(None, ("dp", "tensor"), None),
        P("section", None, None, "tensor"),
        P("section", "tensor", None),
        P("section", None, None, "tensor"),
        P("section", "tensor", None),
        P("section", "tensor"),
        P(),
    )
    return jax.shard_map(
        shards,
        mesh=mesh,
        in_specs=placed,
        out_specs=(
            P("section", None, ("dp", "tensor"), None),
            P("section", None, ("dp", "tensor"), None),
            P("section", None, None, "tensor"),
            P("section", "tensor", None),
            P("section", None, None, "tensor"),
            P("section", "tensor", None),
        ),
        check_vma=False,
    )
```

time: 1830 us -> 806 us (0.44); the launches traced: 1810 us -> 805 us
  Pallas kernels: 0 us -> 467 us
  waiting for transfers between devices: 709 us -> 253 us
  local copies, waits for them, and re-layouts: 417 us -> 36.1 us
  blocking collectives: 214 us -> 0 us
  matrix products: 206 us -> 0 us
  other arithmetic: 228 us -> 31.5 us
    pallas_call x0 -> x5, Pallas kernels: none -> 467 us  [the longest x1 227 us: share_weights(): pl.pallas_call(prep_kernel, out_shape=outs, in_specs=[ANY] * 4, out_specs...]
    reduce_scatter x12 -> x0, waiting for transfers between devices: 256 us -> none  [the longest x6 153 us: row_sums(): lax.psum_scatter(jnp.dot(left, right, preferred_element_type=jnp.float32)...]
    dot_general x69 -> x0, matrix products: 206 us -> none  [the longest x12 48.2 us: cross_dot(): lax.dot_general(left, right, (((0,), (0,)), ((), ())), preferred_element_...]
    all_gather x12 -> x0, waiting for transfers between devices: 201 us -> none  [the longest x6 128 us: gather_rows(): return lax.all_gather(values, 'tensor', axis=0, tiled=True)]
    all_gather x12 -> x0, blocking collectives: 158 us -> none  [entering_2(): lax.all_gather(part.astype(kind), axis)]
    dynamic_slice x60 -> x1, local copies, waits for them, and re-layouts: 95.6 us -> 0.07 us  [angle_tables(): lax.dynamic_slice_in_dim((at - begins) * BLOCK, d * blocks, blocks)]
    concatenate x42 -> x2, local copies, waits for them, and re-layouts: 77.9 us -> 1.2 us  [scalar_table(): jnp.concatenate([mine, rates, decay, forward.reshape(-1), backward.reshap...]
    psum x6 -> x0, blocking collectives: 55.9 us -> none  [head_sum(): return lax.psum(values, 'tensor')]
  transfers between devices with their start and end apart: 29 -> 15, of which waited for: 24 -> 2; matrix products, arithmetic and copies ran while one was open for 19% -> 5% of each run, Pallas kernels for 0% -> 28%
where the time goes in v1:
time: 806 us; the launch traced here: 805 us
  Pallas kernels  467 us (58%)
  waiting for transfers between devices  253 us (31%)
  local copies, waits for them, and re-layouts  36.1 us (4%)
  other arithmetic  31.5 us (4%)
  between operations  14.4 us (2%)
    psum x1, waiting for transfers between devices, core_halves(): return lax.psum(tuple(total), 'dp')  251 us
    pallas_call x1, Pallas kernels, share_weights(): pl.pallas_call(prep_kernel, out_shape=outs, in_specs=[ANY] * 4, out_specs...  227 us
    pallas_call x2, Pallas kernels, layer_backward(): pl.pallas_call(functools.partial(backward_kernel, dp, layer, last, first)...  136 us
    pallas_call x2, Pallas kernels, layer_forward(): pl.pallas_call(functools.partial(forward_kernel, dp, layer, first), out_s...  104 us
    unnamed x45, local copies, waits for them, and re-layouts  20.1 us
  transfers between devices with their start and end apart: 15, of which 2 were waited for; matrix products, arithmetic and copies ran while one was open for 5% of the time, Pallas kernels for 28%

profile of v1, /device:TPU:0, one launch (start us, length us, event | category | flops | bytes accessed | tf_op | source)
XLA Modules:
  0.0 804.9 jit_solution(3436211289766905484)
XLA Ops:
  9.7 3.4 copy.24
  13.1 3.1 copy.18
  16.2 2.6 pad.9.wfo
  18.8 2.0 pad.8.wfi
  20.9 2.5 fusion.7
  23.4 227.2 %share_weights.1 = (bf16[2,1024,1024]{2,1,0:T(8,128)(2,1)}, bf16[2,1024,1024]{2,1,0:T(8,128)(2,1)}, bf16[2,2,1024,768]{3,2,1,0:T(8,128)(2,1)}, bf16[2,768,1024]{2,1,0:T(8,128)(2,1)}) custom-call(bf16[1024,1024]{1,0:T(8,128)(2,1)} %bitcast.114, bf16[256,1024]{1,0:T(8,128)(2,1)} %bitcast.127, bf16[2,1024,768]{2,1,0:T(8,128)(2,1)} %pad.8.wfi, ...), custom_call_target="tpu_custom_call" | custom-call | tf_op jit(solution)/shard_map/share_weights/pallas_call | solution.py:243
  252.8 54.3 %layer_forward.2 = (bf16[192,1024]{1,0:T(8,128)(2,1)}, bf16[768,1024]{1,0:T(8,128)(2,1)}, f32[768,256]{1,0:T(8,128)}, f32[768,256]{1,0:T(8,128)}, f32[768,256]{1...) custom-call(bf16[2,192,1024]{2,1,0:T(8,128)(2,1)} %x_in.3, ...), custom_call_target="tpu_custom_call" | custom-call | flops 6845104128 | bytes 20971520 | tf_op jit(solution)/shard_map/layer_forward/pallas_call | solution.py:558
  307.1 49.2 %layer_forward.3 = (bf16[192,1024]{1,0:T(8,128)(2,1)}, bf16[768,1024]{1,0:T(8,128)(2,1)}, f32[768,256]{1,0:T(8,128)}, f32[768,256]{1,0:T(8,128)}, f32[768,256]{1...) custom-call(bf16[192,1024]{1,0:T(8,128)(2,1)} %get-tuple-element.54., ...), custom_call_target="tpu_custom_call" | custom-call | flops 6845104128 | bytes 20971520 | tf_op jit(solution)/shard_map/layer_forward/pallas_call | solution.py:558
  356.3 70.4 %layer_backward.2 = (bf16[192,1024]{1,0:T(8,128)(2,1)}, bf16[1024,1024]{1,0:T(8,128)(2,1)}, bf16[256,1024]{1,0:T(8,128)(2,1)}, bf16[2,1024,768]{2,1,0:T(8,128)(2,1)}, bf16[768,1024]{1,0:T(8,128)(2,1)}) custom-call(bf16[2,192,1024]{2,1,0:T(8,128)(2,1)} %g_in.1, bf16[192,1024]{1,0:T(8,128)(2,1)} %get-tuple-element.54.x_in, ...), custom_call_target="tpu_custom_call" | custom-call | flops 11274289152 | bytes 31457280 | tf_op jit(solution)/shard_map/layer_backward/pallas_call | solution.py:835
  427.7 65.5 %layer_backward.3 = (bf16[192,1024]{1,0:T(8,128)(2,1)}, bf16[1024,1024]{1,0:T(8,128)(2,1)}, bf16[256,1024]{1,0:T(8,128)(2,1)}, bf16[2,1024,768]{2,1,0:T(8,128)(2,1)}, bf16[768,1024]{1,0:T(8,128)(2,1)}) custom-call(bf16[192,1024]{1,0:T(8,128)(2,1)} %get-tuple-element.70.g_in, bf16[2,192,1024]{2,1,0:T(8,128)(2,1)} %x_in.3, ...), custom_call_target="tpu_custom_call" | custom-call | flops 11274289152 | bytes 31457280 | tf_op jit(solution)/shard_map/layer_backward/pallas_call | solution.py:835
  497.6 1.8 copy-done.5
  505.6 1.4 fusion.1
  507.0 1.4 fusion
  508.3 1.6 add_convert_fusion.1
  510.0 1.6 add_convert_fusion
  513.2 2.2 collective-permute-done.1
  517.5 250.7 %all-reduce.5.cloned.1.call-done = (bf16[512,1024]{1,0:T(8,128)(2,1)}, bf16[512,1024]{1,0:T(8,128)(2,1)}, bf16[128,1024]{1,0:T(8,128)(2,1)}, bf16[128,1024]{1,0:...) async-done(((bf16[512,1024]{1,0:T(8,128)(2,1)}, ...) | async-done | bytes 7340048 | tf_op jit(solution)/shard_map/psum | solution.py:885
  773.1 1.3 broadcast_select_fusion
  776.6 1.9 fusion.4
  778.7 2.3 maximum_convert_fusion
  781.0 5.6 reshape.265
  786.6 1.7 select_bitcast_fusion.1
  788.6 3.1 convert_bitcast_fusion
  791.7 6.4 copy.23
  (127 shorter events, 27.3 us)
Async XLA Ops:
  7.2 761.0 %all-reduce.5.cloned.1.call-start = ((), (), s32[]{:S(2)}) async-start(), calls=%async_computation | async-start | bytes 14680064 | tf_op jit(solution)/shard_map/psum | solution.py:885
  7.2 243.3 %collective-permute-start = (f32[2]{0:T(128)}, f32[2]{0:T(128)S(1)}, u32[]{:S(2)}, u32[]{:S(2)}) collective-permute-start(f32[2]{0:T(128)} %bitcast.132), channel_id=1, source_target_pairs={{0,16},{16,0},{1,17},{17,1},{2,18},{18,2},{3,19},{19,3},{4,20},{20... | collective-permute-start | bytes 32 | tf_op jit(solution)/shard_map/ppermute | solution.py:871
  23.4 227.2 %copy-start.20 = (f32[1,2]{1,0:T(1,128)S(1)}, f32[1,2]{1,0:T(1,128)}, u32[]{:S(2)}) copy-start(f32[1,2]{1,0:T(1,128)} %param.14) | copy-start | bytes 28
  427.7 67.0 %copy-start.10 = (bf16[768,1024]{1,0:T(8,128)(2,1)S(1)}, bf16[768,1024]{1,0:T(8,128)(2,1)}, u32[]{:S(2)}) copy-start(bf16[768,1024]{1,0:T(8,128)(2,1)} %get-tuple-element.93) | copy-start | bytes 4718596
  494.1 5.4 collective-permute-start.5
  494.2 6.8 collective-permute-start.6
  494.7 2.0 copy-start.9
  494.8 2.7 copy-start.4
  496.1 5.8 collective-permute-start.11
  496.3 8.1 %collective-permute-start.12 = (bf16[384,1024]{1,0:T(8,128)(2,1)S(1)}, bf16[384,1024]{1,0:T(8,128)(2,1)S(1)}, u32[]{:S(2)}, u32[]{:S(2)}) collective-permute-start(bf16[384,1024]{1,0:T(8,128)(2,1)S(1)} %dynamic-slice_bitcast_fusion.2), channel_id=1, source_target_pairs={{0,16},{16,0},{1,17},{17,1},{2,18},{18,2},{3,19},{19,3},{4,20},{20... | collective-permute-start | bytes 2359304 | tf_op jit(solution)/shard_map/ppermute | solution.py:871
  496.8 8.8 %collective-permute-start.2 = (bf16[512,1024]{1,0:T(8,128)(2,1)S(1)}, bf16[512,1024]{1,0:T(8,128)(2,1)S(1)}, u32[]{:S(2)}, u32[]{:S(2)}) collective-permute-start(bf16[512,1024]{1,0:T(8,128)(2,1)S(1)} %dynamic-slice_bitcast_fusion.1), channel_id=1, source_target_pairs={{0,16},{16,0},{1,17},{17,1},{2,18},{18,2},{3,19},{19,3},{4,20},{20... | collective-permute-start | bytes 3145736 | tf_op jit(solution)/shard_map/ppermute | solution.py:871
  497.5 1.9 copy-start.5
  499.5 2.9 copy-start.18
  499.5 8.8 %collective-permute-start.8 = (bf16[1,1024,768]{2,1,0:T(8,128)(2,1)S(1)}, bf16[1,1024,768]{2,1,0:T(8,128)(2,1)S(1)}, u32[]{:S(2)}, u32[]{:S(2)}) collective-permute-start(bf16[1,1024,768]{2,1,0:T(8,128)(2,1)S(1)} %constant_dynamic-slice_fusion.1), channel_id=1, source_target_pairs={{0,16},{16,0},{1,17},{17,1},{2,18},{18,2},{3,19},{19,3},{4,20},{20... | collective-permute-start | bytes 4718600 | tf_op jit(solution)/shard_map/ppermute | solution.py:871
  501.0 2.2 copy-start.11
  501.1 5.9 collective-permute-start.3
  502.0 8.0 collective-permute-start.9
  513.1 2.4 collective-permute-start.1
  768.2 3.0 copy-start.2
  768.2 3.0 copy-start.3
  769.3 5.1 collective-permute-start.7
  770.6 5.1 collective-permute-start.13
  771.3 7.2 collective-permute-start.4
  774.4 12.2 %collective-permute-start.10 = (bf16[1,1024,768]{2,1,0:T(8,128)(2,1)}, bf16[1,1024,768]{2,1,0:T(8,128)(2,1)}, u32[]{:S(2)}, u32[]{:S(2)}) collective-permute-start(bf16[1,1024,768]{2,1,0:T(8,128)(2,1)} %broadcast_select_fusion), channel_id=1, source_target_pairs={{0,16},{16,0},{1,17},{17,1},{2,18},{18,2},{3,19},{19,3},{4,20},{20... | collective-permute-start | bytes 4718600 | tf_op jit(solution)/shard_map/ppermute | solution.py:871
  (12 other events, 17.0 us)
Sparse Core Ops, SparseCore 0:
  511.8 256.3 all-reduce.4

commit v2 on v1

v2 whole, which is shorter than its diff:
```python
import functools

import jax
import jax.numpy as jnp
from jax import lax
from jax.experimental import pallas as pl
from jax.experimental.pallas import tpu as pltpu
from jax.sharding import PartitionSpec as P

D = 1024
HEAD = 128
BLOCK = 256
WIDTH = 256
HEADS_HERE = WIDTH // HEAD
norm_eps = 1e-06
MESH = pl.DeviceIdType.MESH
ANY = pl.BlockSpec(memory_space=pl.ANY)
SMEM = pl.BlockSpec(memory_space=pltpu.SMEM)
bf16, f32 = jnp.bfloat16, jnp.float32
VMEM_BYTES = 62 * 1024 * 1024


def place():
    return lax.axis_index("section"), lax.axis_index("dp"), lax.axis_index("tensor")


def partner(t, k):
    return ((t // 2 + k // 2) % 2) * 2 + (t + k) % 2


class Sems:
    def __init__(self, ref):
        self.ref, self.used = ref, 0

    def take(self):
        self.used += 1
        return self.ref.at[self.used - 1]


def remote(src, dst, send, recv, dev):
    return pltpu.make_async_remote_copy(
        src_ref=src, dst_ref=dst, send_sem=send, recv_sem=recv, device_id=dev, device_id_type=MESH
    )


def nn(a, b):
    return lax.dot_general(a, b, (((1,), (0,)), ((), ())), preferred_element_type=f32)


def nt(a, b):
    return lax.dot_general(a, b, (((1,), (1,)), ((), ())), preferred_element_type=f32)


def tn(a, b):
    return lax.dot_general(a, b, (((0,), (0,)), ((), ())), preferred_element_type=f32)


def rms_scale(v):
    return lax.rsqrt(jnp.mean(v * v, axis=-1, keepdims=True) + norm_eps)


def norm_back(v, u):
    q = rms_scale(v)
    n = v * q
    return q * (u - n * jnp.mean(u * n, axis=-1, keepdims=True))


def sig(v):
    return 1.0 / (1.0 + jnp.exp(-v))


def rows_of(p, n):
    return pl.ds(pl.multiple_of(p * n, n), n)


def entry(dp, s, d, t, core=False):
    barrier = pltpu.get_barrier_semaphore()
    count = 3
    for k in (1, 2, 3):
        pl.semaphore_signal(barrier, inc=1, device_id=(s, d, partner(t, k)), device_id_type=MESH)
    if core:
        pl.semaphore_signal(barrier, inc=1, device_id=(1 - s, d, t), device_id_type=MESH)
        count += 1
    if dp > 1:

        def greet(k, c):
            pl.semaphore_signal(
                barrier, inc=1, device_id=(s, (d + k) % dp, t), device_id_type=MESH
            )
            return c

        lax.fori_loop(1, dp, greet, 0)
        count += dp - 1
    pl.semaphore_wait(barrier, count)


class Gather:
    def __init__(self, block_at, half, ssem, rsem, base, where):
        self.at, self.half, self.ssem, self.rsem, self.base = block_at, half, ssem, rsem, base
        self.where = where

    def copy(self, n, peer, half, to):
        s, d, t = self.where
        ref = self.at(partner(t, peer), half)
        k = self.base + n
        return remote(ref, ref, self.ssem.at[k], self.rsem.at[k], (s, d, partner(t, to)))

    def mine(self, n):
        peer, half, to = ((0, 0, 1), (0, 1, 1), (0, 0, 2), (0, 1, 2), (1, 0, 2), (2, 1, 1))[n]
        return self.copy(n, peer, half, to)

    def arriving(self, n):
        s, d, t = self.where
        peer, half = ((1, 0), (1, 1), (2, 0), (2, 1), (3, 0), (3, 1))[n]
        ref = self.at(partner(t, peer), half)
        k = self.base + n
        return remote(ref, ref, self.ssem.at[k], self.rsem.at[k], (s, d, t))

    def start(self):
        self.mine(0).start()
        self.mine(3).start()
        self.mine(1).start()
        self.mine(2).start()

    def forward(self):
        self.arriving(0).wait_recv()
        self.mine(4).start()
        self.arriving(3).wait_recv()
        self.mine(5).start()

    def ready(self, k):
        if k == 1:
            self.arriving(1).wait_recv()
        elif k == 2:
            self.arriving(2).wait_recv()
        else:
            self.arriving(4).wait_recv()
            self.arriving(5).wait_recv()

    def drain(self):
        for n in range(6):
            self.mine(n).wait_send()


class Scatter:
    def __init__(self, part, got, via, rows, ssem, rsem, base, where):
        self.part, self.got, self.via, self.half = part, got, via, rows // 2
        self.ssem, self.rsem, self.base, self.where = ssem, rsem, base, where

    def copy(self, n):
        s, d, t = self.where
        h = self.half
        h0, h1 = pl.ds(0, h), pl.ds(h, h)
        src, dst, to = (
            (self.part.at[2, h0], self.via.at[0], 2),
            (self.part.at[2, h1], self.via.at[1], 1),
            (self.part.at[0, h1], self.got.at[0, h1], 1),
            (self.part.at[1, h0], self.got.at[1, h0], 2),
            (self.part.at[0, h0], self.got.at[0, h0], 1),
            (self.part.at[1, h1], self.got.at[1, h1], 2),
        )[n]
        k = self.base + n
        return remote(src, dst, self.ssem.at[k], self.rsem.at[k], (s, d, partner(t, to)))

    def put(self, k, value):
        self.part[k - 1] = value.astype(bf16)
        self.send(k)

    def send(self, k):
        if k == 3:
            self.copy(0).start()
            self.copy(1).start()
        elif k == 2:
            self.copy(3).start()
        else:
            self.copy(2).start()

    def combine(self):
        h = self.half
        self.copy(0).wait_recv()
        self.part[0, 0:h] = (self.part[0, 0:h].astype(f32) + self.via[0].astype(f32)).astype(bf16)
        self.copy(4).start()
        self.copy(1).wait_recv()
        self.part[1, h:] = (self.part[1, h:].astype(f32) + self.via[1].astype(f32)).astype(bf16)
        self.copy(5).start()

    def result(self):
        for n in (2, 3, 4, 5):
            self.copy(n).wait_recv()
        return self.got[0].astype(f32) + self.got[1].astype(f32)

    def drain(self):
        for n in range(6):
            self.copy(n).wait_send()


def scalar_table(starts, rates, dp, blocks):
    d = lax.axis_index("dp")
    survive = 1.0 - starts.astype(f32).reshape(dp, blocks)
    decay = jnp.exp(-rates * BLOCK)
    factor = jnp.prod(survive, axis=1)[:, None] * (decay**blocks)[None, :]
    at = jnp.arange(dp)
    low, high = jnp.minimum(at, d), jnp.maximum(at, d)
    between = (at[None, :] > low[:, None]) & (at[None, :] < high[:, None])
    through = jnp.prod(jnp.where(between[:, :, None], factor[None], 1.0), axis=1)
    forward = jnp.where((at < d)[:, None], through, 0.0)
    backward = jnp.where((at > d)[:, None], through, 0.0)
    mine = lax.dynamic_index_in_dim(survive, d, 0, keepdims=False)
    return jnp.concatenate([mine, rates, decay, forward.reshape(-1), backward.reshape(-1)])


def decay_fill(scal, base, nb, mask, mask_t, qd, kd):
    for h in range(HEADS_HERE):
        r = scal[base + nb + h]
        i = lax.broadcasted_iota(jnp.int32, (BLOCK, BLOCK), 0).astype(f32)
        j = lax.broadcasted_iota(jnp.int32, (BLOCK, BLOCK), 1).astype(f32)
        gap = i - j
        mask[h] = jnp.where(gap >= 0.0, jnp.exp(-r * jnp.maximum(gap, 0.0)), 0.0)
        if mask_t is not None:
            mask_t[h] = jnp.where(gap <= 0.0, jnp.exp(-r * jnp.maximum(-gap, 0.0)), 0.0)
        i = lax.broadcasted_iota(jnp.int32, (BLOCK, HEAD), 0).astype(f32)
        qd[h] = jnp.exp(-r * (i + 1.0))
        kd[h] = jnp.exp(-r * (BLOCK - 1.0 - i))


def head(h):
    return slice(h * HEAD, (h + 1) * HEAD)


def send_states(dp, where, zout, zin, zs, zr, later):
    s, d, t = where

    def each(k, c):
        to = d + k if later else d - k

        @pl.when((to < dp) if later else (to >= 0))
        def _():
            remote(zout, zin.at[d], zs.at[k], zr.at[d], (s, to, t)).start()

        return c

    lax.fori_loop(1, dp, each, 0)


def sent_states(dp, where, zout, zin, zs, zr, later):
    s, d, t = where

    def each(k, c):
        to = d + k if later else d - k

        @pl.when((to < dp) if later else (to >= 0))
        def _():
            remote(zout, zin.at[d], zs.at[k], zr.at[d], (s, to, t)).wait_send()

        return c

    lax.fori_loop(1, dp, each, 0)


def take_states(dp, where, zout, zin, zs, zr, later, scal, base, run):
    s, d, t = where
    run[...] = jnp.zeros_like(run)

    def each(k, c):
        @pl.when((k < d) if later else (k > d))
        def _():
            remote(zout, zin.at[k], zs.at[0], zr.at[k], (s, d, t)).wait_recv()
            for h in range(HEADS_HERE):
                run[h] += scal[base + 2 * k + h] * zin[k, h].astype(f32)

        return c

    lax.fori_loop(0, dp, each, 0)


class Fetch:
    def __init__(self, src, dst, owner, where, lsem, ssem, rsem):
        s, d, t = where
        self.owner = owner
        self.local = lambda: pltpu.make_async_copy(src, dst, lsem)
        self.far = lambda: remote(src, dst, ssem, rsem, (1 - s, d, t))

    def read(self):
        pl.when(self.owner)(lambda: self.local().start())

    def send(self):
        pl.when(self.owner)(lambda: self.far().start())

    def wait(self):
        pl.when(self.owner)(lambda: self.local().wait())
        pl.when(jnp.logical_not(self.owner))(lambda: self.far().wait_recv())

    def drain(self):
        pl.when(self.owner)(lambda: self.far().wait_send())


def to_owner(owner, where, src, own_dst, far_dst, lsem, ssem, rsem):
    s, d, t = where

    def far():
        return remote(src, far_dst, ssem, rsem, (1 - s, d, t))

    def local():
        return pltpu.make_async_copy(src, own_dst, lsem)

    def start():
        pl.when(owner)(lambda: local().start())
        pl.when(jnp.logical_not(owner))(lambda: far().start())

    def finish():
        @pl.when(owner)
        def _():
            local().wait()
            far().wait_recv()

        pl.when(jnp.logical_not(owner))(lambda: far().wait_send())

    return start, finish


def forward_kernel(
    dp, layer, first, x_in, my_wi, my_wo, my_wfi, my_wfo, cos2, sin2, scal,
    both_o, wi_o, wo_o, wfi_o, wfo_o, y_out, hidden_o, zq_o, zk_o, gate_o, q_o, k_o, v_o, att_o, sc_o, states_o, branch_o, mid_o,
    hid2_o, pair_o,
    wi, wo, wfi, wfo, cosv, sinv, xf, hidden, zq, zk, gate, q, k, v, att, sc, states, branch, mid, hid2,
    pair, mask, qd, kd, loc, zout, zin, run, u, y, part, got, via, ssq, own, yb,
    lsem, ssem, rsem, zs, zr, wl, ws, wr,
):
    where = s, d, t = place()
    rows = x_in.shape[-2]
    total = 4 * rows
    nb = total // BLOCK
    local = Sems(lsem)

    def load(src, dst):
        copy = pltpu.make_async_copy(src, dst, local.take())
        copy.start()
        return copy

    x_src = x_in.at[s] if first else x_in
    got_x = load(x_src, xf.at[rows_of(t, rows)])
    owner = s == layer
    ff = my_wfo.shape[0]
    pairs = (
        (my_wi, wi), (my_wo, wo.at[rows_of(t, WIDTH)]), (my_wfi, wfi), (my_wfo, wfo.at[pl.ds(0, ff)])
    )
    got_w = [
        Fetch(src, dst, owner, where, wl.at[n], ws.at[n], wr.at[n])
        for n, (src, dst) in enumerate(pairs)
    ]
    got_wi, got_wo, got_wfi, got_wfo = got_w
    got_wi.read()
    got_cos, got_sin = load(cos2, cosv), load(sin2, sinv)
    for fetch in got_w[1:]:
        fetch.read()
    wfo[ff:, :] = jnp.zeros_like(wfo[ff:, :])
    entry(dp, s, d, t, core=True)
    got_x.wait()

    half = rows // 2
    gx = Gather(
        lambda p, h: xf.at[pl.ds(pl.multiple_of(p * rows + h * half, half), half)],
        half, ssem, rsem, 0, where,
    )
    gx.start()
    for fetch in got_w:
        fetch.send()
    decay_fill(scal, 0, nb, mask, None, qd, kd)
    got_wi.wait()
    got_cos.wait()
    got_sin.wait()

    def project(i, c):
        for n in (1, 2, 3):

            @pl.when(i == n)
            def _(n=n):
                if n == 1:
                    gx.forward()
                gx.ready(n)

        r = rows_of(partner(t, i), rows)
        xv = xf[r, :].astype(f32)
        hid = (xv * rms_scale(xv)).astype(bf16)
        hidden[r, :] = hid
        cs, sn = cosv[r, :], sinv[r, :]
        for n, (pre, post) in enumerate(((zq, q), (zk, k))):
            z = nn(hid, wi[:, n * WIDTH : (n + 1) * WIDTH])
            pre[r, :] = z
            a = z * sig(z)
            for h in range(HEADS_HERE):
                ah = a[:, head(h)]
                post[r, head(h)] = (ah * cs + pltpu.roll(ah, HEAD // 2, 1) * sn).astype(bf16)
        v[r, :] = nn(hid, wi[:, 2 * WIDTH : 3 * WIDTH]).astype(bf16)
        gate[r, :] = nn(hid, wi[:, 3 * WIDTH :])
        return c

    lax.fori_loop(0, 4, project, 0)

    def wo_block(k, k_to, n, dev):
        ref = wo.at[rows_of(partner(t, k), WIDTH)]
        return remote(ref, ref, ws.at[n], wr.at[n], dev)

    def wo_out(k):
        return wo_block(0, k, 3 + k, (s, d, partner(t, k)))

    def wo_in(k):
        return wo_block(k, 0, 3 + k, (s, d, t))

    def wo_over(k):
        return wo_block(k, 0, 6 + k, (1 - s, d, t))

    @pl.when(owner)
    def _():
        got_wo.local().wait()
        for n in (1, 2, 3):
            wo_out(n).start()

    stores = [load(hidden, hidden_o), load(zq, zq_o), load(zk, zk_o), load(gate, gate_o)]
    stores += [load(q, q_o), load(k, k_o), load(v, v_o)]

    def local_state(b, c):
        r = rows_of(b, BLOCK)
        for h in range(HEADS_HERE):
            kdec = (k[r, head(h)].astype(f32) * kd[h]).astype(bf16)
            loc[b, h] = tn(kdec, v[r, head(h)])
        return c

    lax.fori_loop(0, nb, local_state, 0)
    for h in range(HEADS_HERE):
        carried = loc[0, h]
        for b in range(1, nb):
            carried = (scal[nb + 2 + h] * scal[b]) * carried + loc[b, h]
        zout[h] = carried.astype(bf16)
    send_states(dp, where, zout, zin, zs, zr, True)

    def inner(b, c):
        r = rows_of(b, BLOCK)
        for h in range(HEADS_HERE):
            w = (nt(q[r, head(h)], k[r, head(h)]) * mask[h]).astype(bf16)
            att[r, head(h)] = nn(w, v[r, head(h)])
        return c

    lax.fori_loop(0, nb, inner, 0)
    take_states(dp, where, zout, zin, zs, zr, True, scal, nb + 4, run)

    def outer(b, c):
        r = rows_of(b, BLOCK)
        for h in range(HEADS_HERE):
            entering = scal[b] * run[h]
            states[b, h] = entering
            run[h] = scal[nb + 2 + h] * entering + loc[b, h]
            qdec = (q[r, head(h)].astype(f32) * qd[h]).astype(bf16)
            a = att[r, head(h)] + nn(qdec, entering.astype(bf16))
            att[r, head(h)] = a
            u[t, r, head(h)] = (a * gate[r, head(h)]).astype(bf16)
        return c

    lax.fori_loop(0, nb, outer, 0)

    hu = total // 2
    gu = Gather(lambda p, h: u.at[p, pl.ds(h * hu, hu)], hu, ssem, rsem, 6, where)
    gu.start()
    for b in range(nb):
        a = att[b * BLOCK : (b + 1) * BLOCK, :]
        ssq[0, :, b * BLOCK : (b + 1) * BLOCK] = lax.dot_general(
            jnp.ones((8, WIDTH), f32), a * a, (((1,), (1,)), ((), ())),
            preferred_element_type=f32, precision=lax.Precision.HIGHEST,
        )
    sums = [
        remote(ssq.at[0], ssq.at[n], ssem.at[11 + n], rsem.at[11 + n], (s, d, partner(t, n)))
        for n in (1, 2, 3)
    ]
    for copy in sums:
        copy.start()
    stores += [load(att, att_o), load(states, states_o)]
    @pl.when(owner)
    def _():
        for n in (1, 2, 3):
            wo_in(n).wait_recv()
            wo_over(n).start()

    @pl.when(jnp.logical_not(owner))
    def _():
        got_wo.far().wait_recv()
        for n in (1, 2, 3):
            wo_over(n).wait_recv()

    y[...] = jnp.zeros_like(y)

    def out_project(i, c):
        for n in (1, 2, 3):

            @pl.when(i == n)
            def _(n=n):
                if n == 1:
                    gu.forward()
                gu.ready(n)

        p = partner(t, i)

        def chunk(m, c):
            r = rows_of(m, rows)
            y[r, :] += nn(u[p, r, :], wo[rows_of(p, WIDTH), :])
            return c

        return lax.fori_loop(0, 4, chunk, c)

    lax.fori_loop(0, 4, out_project, 0)
    for copy in sums:
        copy.wait_recv()
    whole = ssq[0] + ssq[1] + ssq[2] + ssq[3]
    sc[...] = jnp.transpose(lax.rsqrt(whole * (1.0 / D) + norm_eps))
    got_wfi.wait()
    got_wfo.wait()
    out = Scatter(part, got, via, rows, ssem, rsem, 15, where)

    def feed(i, c):
        e = 3 - i
        r = rows_of(partner(t, e), rows)
        br = sc[r, 0:1] * y[r, :]
        branch[r, :] = br.astype(bf16)
        m = xf[r, :].astype(f32) + br
        h2 = (m * rms_scale(m)).astype(bf16)
        hid2[r, :] = h2
        p0, p1 = nn(h2, wfi[0]), nn(h2, wfi[1])
        pair[0, r, :] = p0.astype(bf16)
        pair[1, r, :] = p1.astype(bf16)
        o = nn((p0 * p1).astype(bf16), wfo[...])
        for n in (1, 2, 3):

            @pl.when(e == n)
            def _(n=n):
                out.put(n, o)

        @pl.when(e == 0)
        def _():
            mid[...] = m
            own[...] = o + m

        return c

    lax.fori_loop(0, 4, feed, 0)
    stores += [load(sc, sc_o), load(branch, branch_o), load(mid, mid_o), load(hid2, hid2_o)]
    stores += [load(pair, pair_o), load(wi, wi_o), load(wo.at[rows_of(t, WIDTH)], wo_o)]
    stores += [load(wfi, wfi_o), load(wfo, wfo_o)]
    out.combine()
    yb[...] = (own[...] + out.result()).astype(bf16)
    stores += [load(yb, y_out)]
    start, finish = to_owner(
        owner, where, yb, both_o.at[s], both_o.at[s], wl.at[4], ws.at[10], wr.at[10]
    )
    start()
    for fetch in got_w:
        fetch.drain()

    @pl.when(owner)
    def _():
        for n in (1, 2, 3):
            wo_out(n).wait_send()
            wo_over(n).wait_send()

    finish()
    gx.drain()
    gu.drain()
    out.drain()
    for copy in sums:
        copy.wait_send()
    sent_states(dp, where, zout, zin, zs, zr, True)
    for copy in stores:
        copy.wait()


def layer_forward(layer, first, x, weights, cos2, sin2, scal, dp, uid):
    rows = x.shape[-2]
    total = 4 * rows
    nb = total // BLOCK
    fp = weights[2].shape[2]
    saved = [
        ((rows, D), bf16), ((total, D), bf16), ((total, WIDTH), f32), ((total, WIDTH), f32),
        ((total, WIDTH), f32), ((total, WIDTH), bf16), ((total, WIDTH), bf16),
        ((total, WIDTH), bf16), ((total, WIDTH), f32), ((total, 8), f32),
        ((nb, HEADS_HERE, HEAD, HEAD), f32), ((total, D), bf16), ((rows, D), f32),
        ((total, D), bf16), ((2, total, fp), bf16),
    ]
    scratch = [
        ((D, 4 * WIDTH), bf16), ((D, D), bf16), ((2, D, fp), bf16), ((fp, D), bf16),
        ((total, HEAD), f32), ((total, HEAD), f32), ((total, D), bf16),
    ]
    scratch += saved[1:]
    saved = [
        ((2, rows, D), bf16), ((D, 4 * WIDTH), bf16), ((WIDTH, D), bf16), ((2, D, fp), bf16),
        ((fp, D), bf16),
    ] + saved
    scratch += [
        ((HEADS_HERE, BLOCK, BLOCK), f32), ((HEADS_HERE, BLOCK, HEAD), f32),
        ((HEADS_HERE, BLOCK, HEAD), f32), ((nb, HEADS_HERE, HEAD, HEAD), f32),
        ((HEADS_HERE, HEAD, HEAD), bf16), ((dp, HEADS_HERE, HEAD, HEAD), bf16),
        ((HEADS_HERE, HEAD, HEAD), f32), ((4, total, WIDTH), bf16), ((total, D), f32),
        ((3, rows, D), bf16), ((2, rows, D), bf16), ((2, rows // 2, D), bf16),
        ((4, 8, total), f32), ((rows, D), f32), ((rows, D), bf16),
    ]
    flops = 2 * total * D * (4 * WIDTH + D + 3 * fp)
    return pl.pallas_call(
        functools.partial(forward_kernel, dp, layer, first),
        out_shape=tuple(jax.ShapeDtypeStruct(a, b) for a, b in saved),
        in_specs=[ANY] * 7 + [SMEM],
        out_specs=(ANY,) * len(saved),
        scratch_shapes=[pltpu.VMEM(a, b) for a, b in scratch]
        + [
            pltpu.SemaphoreType.DMA((24,)),
            pltpu.SemaphoreType.DMA((21,)),
            pltpu.SemaphoreType.DMA((21,)),
            pltpu.SemaphoreType.DMA((dp,)),
            pltpu.SemaphoreType.DMA((dp,)),
            pltpu.SemaphoreType.DMA((5,)),
            pltpu.SemaphoreType.DMA((11,)),
            pltpu.SemaphoreType.DMA((11,)),
        ],
        compiler_params=pltpu.CompilerParams(
            collective_id=uid, has_side_effects=True, vmem_limit_bytes=VMEM_BYTES
        ),
        cost_estimate=pl.CostEstimate(flops=flops, bytes_accessed=20 << 20, transcendentals=0),
        name="layer_forward",
    )(x, *weights, cos2, sin2, scal)


class LineSum:
    def __init__(self, dp, where, owner, arrays, sems):
        self.dp, self.where, self.owner, self.arrays = dp, where, owner, arrays
        self.core_s, self.core_r, self.rs, self.rr, self.gs, self.gr, self.ol, self.os, self.or_ = sems

    def each(self, fn):
        for n, array in enumerate(self.arrays):
            fn(n, *array)

    def own(self, halves, j):
        count = halves.shape[1] // self.dp
        return halves.at[self.where[0], rows_of(j, count)]

    def over(self, n, halves, from_core):
        s, d, t = self.where
        return remote(
            halves.at[1 - s], from_core, self.core_s.at[n], self.core_r.at[n], (1 - s, d, t)
        )

    def core_send(self):
        self.each(lambda n, halves, fc, land, res: self.over(n, halves, fc).start())

    def core_add(self):
        s = self.where[0]

        def one(n, halves, fc, land, res):
            self.over(n, halves, fc).wait()
            count = halves.shape[1] // self.dp

            def chunk(j, c):
                r = rows_of(j, count)
                halves[s, r, :] = (halves[s, r, :].astype(f32) + fc[r, :].astype(f32)).astype(bf16)
                return c

            lax.fori_loop(0, self.dp, chunk, 0)

        self.each(one)

    def partial(self, n, land, j, up):
        s, d, t = self.where
        to = d + 1 if up else d - 1
        slot = j if up else jnp.where(j == to, self.dp, j)
        return remote(land.at[j], land.at[slot], self.rs.at[n, j], self.rr.at[n, slot], (s, to, t))

    def landed(self, n, land, slot):
        s, d, t = self.where
        return remote(land.at[slot], land.at[slot], self.rs.at[n, 0], self.rr.at[n, slot], (s, d, t))

    def final(self, n, halves, j, up):
        s, d, t = self.where
        to = d + 1 if up else d - 1
        ref = self.own(halves, j)
        k = j if up else jnp.where(j == d, self.dp, j)
        return remote(ref, ref, self.gs.at[n, k], self.gr.at[n, j], (s, to, t))

    def arrived(self, n, halves, j):
        s, d, t = self.where
        ref = self.own(halves, j)
        return remote(ref, ref, self.gs.at[n, 0], self.gr.at[n, j], (s, d, t))

    def add(self, n, halves, land, slot, j, into_own):
        s = self.where[0]
        self.landed(n, land, slot).wait_recv()
        r = rows_of(j, halves.shape[1] // self.dp)
        total = (halves[s, r, :].astype(f32) + land[slot].astype(f32)).astype(bf16)
        if into_own:
            halves[s, r, :] = total
        else:
            land[slot] = total

    def step(self, k):
        dp = self.dp
        s, d, t = self.where
        if dp == 1:
            return
        if k < dp - 1:
            for up in (True, False):
                e = d if up else dp - 1 - d
                j = dp - 1 - k + d if up else k - (dp - 1 - d)

                def one(n, halves, fc, land, res, up=up, e=e, j=j):
                    @pl.when(e == 0)
                    def _():
                        land[j] = halves[s, rows_of(j, halves.shape[1] // dp), :]
                        self.partial(n, land, j, up).start()

                    @pl.when((e > 0) & (e <= k))
                    def _():
                        self.add(n, halves, land, j, j, False)
                        self.partial(n, land, j, up).start()

                self.each(one)
            return
        a = k - (dp - 1)
        if a == 0:

            def one(n, halves, fc, land, res):
                def sent(j, c):
                    pl.when(j > d)(lambda: self.partial(n, land, j, True).wait_send())
                    pl.when(j < d)(lambda: self.partial(n, land, j, False).wait_send())
                    return c

                @pl.when(d > 0)
                def _():
                    self.add(n, halves, land, d, d, True)

                @pl.when(d < dp - 1)
                def _():
                    self.add(n, halves, land, dp, d, True)

                lax.fori_loop(0, dp, sent, 0)
                pl.when(d < dp - 1)(lambda: self.final(n, halves, d, True).start())
                pl.when(d > 0)(lambda: self.final(n, halves, d, False).start())

            self.each(one)
            return

        def one(n, halves, fc, land, res):
            @pl.when(d - a >= 0)
            def _():
                self.arrived(n, halves, d - a).wait_recv()
                pl.when(d < dp - 1)(lambda: self.final(n, halves, d - a, True).start())

            @pl.when(d + a < dp)
            def _():
                self.arrived(n, halves, d + a).wait_recv()
                pl.when(d > 0)(lambda: self.final(n, halves, d + a, False).start())

        self.each(one)

    def results(self):
        out = []

        def one(n, halves, fc, land, res):
            s = self.where[0]
            out.append(
                to_owner(
                    self.owner, self.where, halves.at[s], res.at[s], res.at[s],
                    self.ol.at[n], self.os.at[n], self.or_.at[n],
                )
            )

        self.each(one)
        return out

    def finish(self):
        dp = self.dp
        s, d, t = self.where

        def one(n, halves, fc, land, res):
            def sent(j, c):
                @pl.when((j <= d) & (d < dp - 1))
                def _():
                    self.final(n, halves, j, True).wait_send()

                @pl.when((j >= d) & (d > 0))
                def _():
                    self.final(n, halves, j, False).wait_send()

                return c

            lax.fori_loop(0, dp, sent, 0)

        self.each(one)
        for start, _ in self.results():
            start()

    def close(self):
        for _, finish in self.results():
            finish()


def backward_kernel(
    dp, ct_in, y0_in, tok_in, cos2, sin2, scal,
    wi0, wo0, wfi0, wfo0, wi1, wo1, wfi1, wfo1, *refs,
):
    saved_i = (refs[0:14], refs[14:28])
    both_o, gwfi_o, gwfo_o, gmix_o = refs[28:32]
    (
        wi, wo, wfi, wfo, cosv, sinv, gf, xr, hidden, zq, zk, gate, q, k, v, att, sc, states, branch, mid,
        hid2, pair, mask, mask_t, qd, kd, terms, zout, zin, run, gpair, prod, gb, gm, dv, dk,
        gp, part, got, via, own, gr, gwfi, gwfo, gmix, c_fi, c_fo, c_mix, l_fi, l_fo, l_mix,
        lsem, ssem, rsem, zs, zr, ol, os, or_, core_s, core_r, ls, lr, fs, fr,
    ) = refs[32:]
    where = s, d, t = place()
    rows = y0_in.shape[0]
    total = 4 * rows
    nb = total // BLOCK
    fp = wfo.shape[0]
    half = rows // 2
    table = nb + 4 + 4 * dp
    local = Sems(lsem)
    me = rows_of(t, rows)
    gated, gatt = slice(0, WIDTH), slice(WIDTH, 2 * WIDTH)

    def gatt_head(h):
        return slice(WIDTH + h * HEAD, WIDTH + (h + 1) * HEAD)

    def load(src, dst):
        copy = pltpu.make_async_copy(src, dst, local.take())
        copy.start()
        return copy

    def block_of(ref):
        return lambda p, h: ref.at[pl.ds(pl.multiple_of(p * rows + h * half, half), half)]

    weights = ((wi0, wo0, wfi0, wfo0), (wi1, wo1, wfi1, wfo1))

    def load_feed(layer):
        keep = saved_i[layer]
        return [
            load(weights[layer][3], wfo), load(keep[13], pair), load(weights[layer][2], wfi),
            load(keep[11], mid), load(keep[12], hid2),
        ]

    def load_gates(layer):
        keep = saved_i[layer]
        return [
            load(weights[layer][1], wo), load(keep[10], branch), load(keep[8], sc), load(keep[7], att),
            load(keep[3], gate),
        ]

    def load_attn(layer):
        keep = saved_i[layer]
        pairs = ((4, q), (5, k), (6, v), (9, states), (1, zq), (2, zk))
        return [load(keep[n], ref) for n, ref in pairs]

    def load_ends(layer):
        x = tok_in.at[s] if layer == 0 else y0_in
        return [load(weights[layer][0], wi), load(saved_i[layer][0], hidden), load(x, xr)]

    def line(arrays, base, layer):
        n = len(arrays)
        at = pl.ds(base, n)
        sems = [ref.at[at] for ref in (core_s, core_r, ls, lr, fs, fr, ol, os, or_)]
        return LineSum(dp, where, s == layer, arrays, sems)

    feeds = [
        line(
            (
                (gwfi.at[layer], c_fi, l_fi, gwfi_o),
                (gwfo.at[layer], c_fo, l_fo, gwfo_o),
            ),
            3 * layer, layer,
        )
        for layer in (0, 1)
    ]
    mixes = [line(((gmix, c_mix, l_mix, gmix_o),), 3 * layer + 2, layer) for layer in (0, 1)]
    steps = 2 * dp - 1
    progress = {}

    def tick(piece, count=1):
        at = progress.get(id(piece), 0)
        for n in range(at, min(at + count, steps)):
            piece.step(n)
        progress[id(piece)] = at + count

    got_g = load(ct_in.at[s], gf.at[me])
    in_feed, in_tables = load_feed(1), [load(cos2, cosv), load(sin2, sinv)]
    in_gates, in_attn, in_ends = load_gates(1), load_attn(1), load_ends(1)
    entry(dp, s, d, t, core=True)
    got_g.wait()
    in_out = []

    for layer in (1, 0):
        offset = table * layer
        a_now, b_now = feeds[layer], mixes[layer]
        a_old, b_old = (feeds[1], mixes[1]) if layer == 0 else (None, None)
        base = 24 * layer
        gg = Gather(block_of(gf), half, ssem, rsem, base, where)
        gg.start()
        decay_fill(scal, offset, nb, mask, mask_t, qd, kd)
        if b_old is not None:
            b_old.core_add()
            tick(b_old)
        for copy in in_feed:
            copy.wait()
        sums = Scatter(part, got, via, rows, ssem, rsem, base + 6, where)

        def feed(i, c):
            for n in (1, 2, 3):

                @pl.when(i == n)
                def _(n=n):
                    if n == 1:
                        gg.forward()
                    gg.ready(n)

            r = rows_of(partner(t, i), rows)
            grad = nt(gf[r, :], wfo[...])
            p0, p1 = pair[0, r, :].astype(f32), pair[1, r, :].astype(f32)
            prod[r, :] = (p0 * p1).astype(bf16)
            g0, g1 = (grad * p1).astype(bf16), (grad * p0).astype(bf16)
            gpair[0, r, :] = g0
            gpair[1, r, :] = g1
            o = nt(g0, wfi[0]) + nt(g1, wfi[1])
            for n in (1, 2, 3):

                @pl.when(i == n)
                def _(n=n):
                    sums.put(n, o)

            @pl.when(i == 0)
            def _():
                own[...] = o

            return c

        lax.fori_loop(0, 4, feed, 0)
        sums.combine()
        if a_old is not None:
            tick(a_old)
            tick(b_old)

        def feed_weights(n, c):
            cols = rows_of(n, 256)
            a = hid2[:, cols]
            gwfi[layer, 0, cols, :] = tn(a, gpair[0]).astype(bf16)
            gwfi[layer, 1, cols, :] = tn(a, gpair[1]).astype(bf16)
            return c

        def out_weights(n, c):
            cols = rows_of(n, 256)
            a = prod[:, cols]
            gwfo[layer, 0, cols, :] = tn(a, gf[:, : D // 2]).astype(bf16)
            gwfo[layer, 1, cols, :] = tn(a, gf[:, D // 2 :]).astype(bf16)
            return c

        lax.fori_loop(0, D // 256, feed_weights, 0)
        lax.fori_loop(0, fp // 256, out_weights, 0)
        a_now.core_send()
        grad_middle = gf[me, :].astype(f32) + norm_back(mid[...], own[...] + sums.result())
        gm[...] = grad_middle
        gb[me, :] = grad_middle.astype(bf16)
        sums.drain()
        gg.drain()

        gbg = Gather(block_of(gb), half, ssem, rsem, base + 12, where)
        gbg.start()
        if layer == 1:
            in_feed = load_feed(0)
        if a_old is not None:
            tick(a_old, 1 if steps <= 7 else steps)
            tick(b_old)
        a_now.core_add()
        tick(a_now)
        for copy in in_gates:
            copy.wait()

        def gating(i, c):
            for n in (1, 2, 3):

                @pl.when(i == n)
                def _(n=n):
                    if n == 1:
                        gbg.forward()
                    gbg.ready(n)

            r = rows_of(partner(t, i), rows)
            b = gb[r, :]
            grad = nt(b, wo[...])
            dots = jnp.sum(b.astype(f32) * branch[r, :].astype(f32), axis=-1, keepdims=True) * (1.0 / D)
            scale = sc[r, 0:1]
            normed = att[r, :] * scale
            gt = gate[r, :]
            gp[r, 3 * WIDTH :] = (grad * normed).astype(bf16)
            prod[r, gated] = (normed * gt).astype(bf16)
            prod[r, gatt] = (scale * (grad * gt - normed * dots)).astype(bf16)
            return c

        lax.fori_loop(0, 4, gating, 0)
        if layer == 1:
            in_gates = load_gates(0)
        for copy in in_attn:
            copy.wait()
        if layer == 1:
            for copy in in_tables:
                copy.wait()

        def term(b, c):
            r = rows_of(b, BLOCK)
            for h in range(HEADS_HERE):
                qdec = (q[r, head(h)].astype(f32) * qd[h]).astype(bf16)
                terms[b, h] = tn(qdec, prod[r, gatt_head(h)])
            return c

        lax.fori_loop(0, nb, term, 0)
        for h in range(HEADS_HERE):
            carried = scal[offset + nb - 1] * terms[nb - 1, h]
            for b in reversed(range(nb - 1)):
                carried = scal[offset + b] * (terms[b, h] + scal[offset + nb + 2 + h] * carried)
            zout[layer, h] = carried.astype(bf16)
        z_args = (dp, where, zout.at[layer], zin.at[layer], zs.at[layer], zr.at[layer], False)
        send_states(*z_args)
        if a_old is not None:
            tick(b_old)
        tick(a_now)

        def unturn(pre, grad, r, h):
            back = grad * cosv[r, :] - pltpu.roll(grad, HEAD // 2, 1) * sinv[r, :]
            z = pre[r, head(h)]
            g = sig(z)
            return (back * (g * (1.0 + z * (1.0 - g)))).astype(bf16)

        def inner(b, c):
            r = rows_of(b, BLOCK)
            for h in range(HEADS_HERE):
                qh, kh, vh, gh = q[r, head(h)], k[r, head(h)], v[r, head(h)], prod[r, gatt_head(h)]
                w_t = (nt(kh, qh) * mask_t[h]).astype(bf16)
                dv[r, head(h)] = nn(w_t, gh)
                ds = (nt(gh, vh) * mask[h]).astype(bf16)
                ds_t = (nt(vh, gh) * mask_t[h]).astype(bf16)
                dk[r, head(h)] = nn(ds_t, qh)
                dq = nn(ds, kh) + nt(gh, states[b, h].astype(bf16)) * qd[h]
                gp[r, head(h)] = unturn(zq, dq, r, h)
            return c

        lax.fori_loop(0, nb, inner, 0)
        take_states(*z_args, scal, offset + nb + 4 + 2 * dp, run)

        def outer(i, c):
            b = nb - 1 - i
            r = rows_of(b, BLOCK)
            for h in range(HEADS_HERE):
                after = run[h]
                low = after.astype(bf16)
                run[h] = scal[offset + b] * (terms[b, h] + scal[offset + nb + 2 + h] * after)
                kdec = (k[r, head(h)].astype(f32) * kd[h]).astype(bf16)
                dkh = dk[r, head(h)] + nt(v[r, head(h)], low) * kd[h]
                k_cols = slice(WIDTH + h * HEAD, WIDTH + (h + 1) * HEAD)
                v_cols = slice(2 * WIDTH + h * HEAD, 2 * WIDTH + (h + 1) * HEAD)
                gp[r, k_cols] = unturn(zk, dkh, r, h)
                gp[r, v_cols] = (dv[r, head(h)] + nn(kdec, low)).astype(bf16)
            return c

        lax.fori_loop(0, nb, outer, 0)
        if layer == 1:
            in_attn = load_attn(0)
        for copy in in_ends:
            copy.wait()
        ins = Scatter(part, got, via, rows, ssem, rsem, base + 18, where)

        def back_in(i, c):
            e = 3 - i
            r = rows_of(partner(t, e), rows)
            o = nt(gp[r, :], wi[...])
            for n in (1, 2, 3):

                @pl.when(e == n)
                def _(n=n):
                    ins.put(n, o)

            @pl.when(e == 0)
            def _():
                own[...] = o

            return c

        lax.fori_loop(0, 4, back_in, 0)
        ins.combine()
        tick(a_now)
        if a_old is not None:
            tick(a_old, steps)
            tick(b_old, steps)
            a_old.finish()
            b_old.finish()
            b_old.close()

        def in_weights(n, c):
            cols = rows_of(n, 256)
            a = hidden[:, cols]
            gmix[0, cols, :] = tn(a, gp[:, : 2 * WIDTH]).astype(bf16)
            gmix[1, cols, :] = tn(a, gp[:, 2 * WIDTH :]).astype(bf16)
            return c

        lax.fori_loop(0, D // 256, in_weights, 0)
        gmix[0, D:, :] = tn(prod[:, gated], gb[:, : D // 2]).astype(bf16)
        gmix[1, D:, :] = tn(prod[:, gated], gb[:, D // 2 :]).astype(bf16)
        b_now.core_send()
        dx = gm[...] + norm_back(xr[...].astype(f32), own[...] + ins.result())
        gr[layer] = dx.astype(bf16)
        ins.drain()
        gbg.drain()
        sent_states(*z_args)
        start, finish = to_owner(
            s == layer, where, gr.at[layer], both_o.at[s], both_o.at[s],
            ol.at[6 + layer], os.at[6 + layer], or_.at[6 + layer],
        )
        start()
        in_out.append(finish)
        tick(a_now)
        if layer == 1:
            gf[me, :] = gr[layer]
            in_ends = load_ends(0)

    b_now.core_add()
    while progress.get(id(b_now), 0) < steps or progress.get(id(a_now), 0) < steps:
        tick(b_now)
        tick(a_now)
    a_now.finish()
    b_now.finish()
    feeds[1].close()
    a_now.close()
    b_now.close()
    for finish in in_out:
        finish()


def layers_backward(cotangent, y0, tokens, cos2, sin2, scal, weights, saved, dp, uid):
    rows = y0.shape[-2]
    total = 4 * rows
    nb = total // BLOCK
    fp = weights[0][3].shape[0]
    mixed = D + WIDTH
    outs = [
        ((2, rows, D), bf16), ((2, D, fp), bf16), ((2, fp, D // 2), bf16), ((2, mixed, D // 2), bf16)
    ]
    scratch = [
        ((D, 4 * WIDTH), bf16), ((WIDTH, D), bf16), ((2, D, fp), bf16), ((fp, D), bf16),
        ((total, HEAD), f32), ((total, HEAD), f32), ((total, D), bf16), ((rows, D), bf16),
    ]
    scratch += [(a.shape, a.dtype) for a in saved[0]]
    scratch += [
        ((HEADS_HERE, BLOCK, BLOCK), f32), ((HEADS_HERE, BLOCK, BLOCK), f32),
        ((HEADS_HERE, BLOCK, HEAD), f32), ((HEADS_HERE, BLOCK, HEAD), f32),
        ((nb, HEADS_HERE, HEAD, HEAD), f32), ((2, HEADS_HERE, HEAD, HEAD), bf16),
        ((2, dp, HEADS_HERE, HEAD, HEAD), bf16), ((HEADS_HERE, HEAD, HEAD), f32),
        ((2, total, fp), bf16), ((total, fp), bf16), ((total, D), bf16), ((rows, D), f32),
        ((total, WIDTH), f32), ((total, WIDTH), f32),
        ((total, 4 * WIDTH), bf16),
        ((3, rows, D), bf16), ((2, rows, D), bf16), ((2, rows // 2, D), bf16), ((rows, D), f32),
        ((2, rows, D), bf16),
        ((2, 2, D, fp), bf16), ((2, 2, fp, D // 2), bf16), ((2, mixed, D // 2), bf16),
        ((D, fp), bf16), ((fp, D // 2), bf16), ((mixed, D // 2), bf16),
        ((dp + 1, D // dp, fp), bf16), ((dp + 1, fp // dp, D // 2), bf16),
        ((dp + 1, mixed // dp, D // 2), bf16),
    ]
    dma = pltpu.SemaphoreType.DMA
    flops = 8 * total * D * (4 * WIDTH + WIDTH + 3 * fp)
    flat = [w for layer in weights for w in layer]
    kept = [a for layer in saved for a in layer]
    return pl.pallas_call(
        functools.partial(backward_kernel, dp),
        out_shape=tuple(jax.ShapeDtypeStruct(a, b) for a, b in outs),
        in_specs=[ANY] * 5 + [SMEM] + [ANY] * (len(flat) + len(kept)),
        out_specs=(ANY,) * len(outs),
        scratch_shapes=[pltpu.VMEM(a, b) for a, b in scratch]
        + [
            dma((48,)), dma((48,)), dma((48,)), dma((2, dp)), dma((2, dp)), dma((8,)), dma((8,)),
            dma((8,)), dma((6,)), dma((6,)), dma((6, dp)), dma((6, dp + 1)), dma((6, dp + 1)),
            dma((6, dp)),
        ],
        compiler_params=pltpu.CompilerParams(
            collective_id=uid, has_side_effects=True, vmem_limit_bytes=VMEM_BYTES
        ),
        cost_estimate=pl.CostEstimate(flops=flops, bytes_accessed=60 << 20, transcendentals=0),
        name="layers_backward",
    )(cotangent, y0, tokens, cos2, sin2, scal, *flat, *kept)


def angle_tables(starts, blocks):
    d = lax.axis_index("dp")
    at = jnp.arange(starts.shape[0], dtype=jnp.int32)
    begins = jnp.max(
        jnp.where((at[None, :] <= at[:, None]) & (starts > 0)[None, :], at[None, :], 0), axis=1
    )
    offsets = lax.dynamic_slice_in_dim((at - begins) * BLOCK, d * blocks, blocks)
    places = (offsets[:, None] + jnp.arange(BLOCK, dtype=jnp.int32)[None, :]).reshape(-1)
    lane = jnp.arange(HEAD, dtype=jnp.int32)
    frequency = 10000.0 ** (-(lane % (HEAD // 2)).astype(f32) / (HEAD // 2))
    angles = places.astype(f32)[:, None] * frequency[None, :]
    return jnp.cos(angles), jnp.where(lane < HEAD // 2, -1.0, 1.0)[None, :] * jnp.sin(angles)


def swap(x):
    return lax.ppermute(x, "section", [(0, 1), (1, 0)])


def mine_first(s, a, b):
    return jnp.where(s == 0, a, b)


def shards(tokens, cotangent, mixer_in, mixer_out, feed_in, feed_out, decay_rate, block_starts):
    s = lax.axis_index("section")
    dp = lax.axis_size("dp")
    rows = tokens.shape[1]
    blocks = 4 * rows // BLOCK
    ff = feed_out.shape[1]
    fp = -(-ff // 256) * 256
    wi = mixer_in[0].reshape(D, 4 * WIDTH)
    wfi = jnp.pad(jnp.swapaxes(feed_in[0], 0, 1), ((0, 0), (0, 0), (0, fp - ff)))
    mine = (wi, mixer_out[0], wfi, feed_out[0])
    other_rates = swap(decay_rate[0])
    rates = (mine_first(s, decay_rate[0], other_rates), mine_first(s, other_rates, decay_rate[0]))
    starts = lax.dynamic_index_in_dim(block_starts, s, 0, keepdims=False)
    cos2, sin2 = angle_tables(starts, blocks)
    scal = [scalar_table(starts, r, dp, blocks) for r in rates]

    both0, *out0 = layer_forward(0, True, tokens, mine, cos2, sin2, scal[0], dp, 1)
    weights0, y0, saved0 = out0[:4], out0[4], out0[5:]
    both1, *out1 = layer_forward(1, False, y0, mine, cos2, sin2, scal[1], dp, 2)
    weights1, saved1 = out1[:4], out1[5:]
    in_grads, g_fi, g_fo, g_mix = layers_backward(
        cotangent, y0, tokens, cos2, sin2, jnp.concatenate(scal), (weights0, weights1),
        (saved0, saved1), dp, 3,
    )
    outputs = mine_first(s, both0, both1)
    g_in = jnp.concatenate([g_mix[0, :D], g_mix[1, :D]], axis=1).astype(f32).reshape(D, 4, WIDTH)
    g_out = jnp.concatenate([g_mix[0, D:], g_mix[1, D:]], axis=1).astype(f32)
    g_feed_in = jnp.swapaxes(g_fi[:, :, :ff], 0, 1).astype(f32)
    g_feed_out = jnp.concatenate([g_fo[0, :ff], g_fo[1, :ff]], axis=1).astype(f32)
    return outputs[None], in_grads[None], g_in[None], g_out[None], g_feed_in[None], g_feed_out[None]


def solution(mesh):
    placed = (
        P(None, ("dp", "tensor"), None),
        P(None, ("dp", "tensor"), None),
        P("section", None, None, "tensor"),
        P("section", "tensor", None),
        P("section", None, None, "tensor"),
        P("section", "tensor", None),
        P("section", "tensor"),
        P(),
    )
    return jax.shard_map(
        shards,
        mesh=mesh,
        in_specs=placed,
        out_specs=(
            P("section", None, ("dp", "tensor"), None),
            P("section", None, ("dp", "tensor"), None),
            P("section", None, None, "tensor"),
            P("section", "tensor", None),
            P("section", None, None, "tensor"),
            P("section", "tensor", None),
        ),
        check_vma=False,
    )
```

time: 806 us -> 449 us (0.56)
  waiting for transfers between devices: 253 us -> 0.01 us
  Pallas kernels: 467 us -> 397 us
  other arithmetic: 31.5 us -> 17.5 us
  between operations: 14.4 us -> 1.2 us
  local copies, waits for them, and re-layouts: 36.1 us -> 24.3 us
    psum x1 -> x0, waiting for transfers between devices: 251 us -> none  [core_halves(): return lax.psum(tuple(total), 'dp')]
    pallas_call x3 -> x1, Pallas kernels: 363 us -> 264 us  [layers_backward(): pl.pallas_call(functools.partial(backward_kernel, dp), out_shape=tuple((j...]
    pallas_call x2, Pallas kernels: 104 us -> 132 us  [layer_forward(): pl.pallas_call(functools.partial(forward_kernel, dp, layer, first), out_s...]
    unnamed x45 -> x14, local copies, waits for them, and re-layouts: 20.1 us -> 14 us
  transfers between devices with their start and end apart: 15 -> 1, of which waited for: 2 -> 0; matrix products, arithmetic and copies ran while one was open for 5% -> 3% of each run, Pallas kernels for 28% -> 0%
where the time goes in v2:
time: 449 us; the launch traced here: 440 us
  Pallas kernels  397 us (88%)
  local copies, waits for them, and re-layouts  24.3 us (5%)
  other arithmetic  17.5 us (4%)
    pallas_call x1, Pallas kernels, layers_backward(): pl.pallas_call(functools.partial(backward_kernel, dp), out_shape=tuple((j...  264 us
    pallas_call x2, Pallas kernels, layer_forward(): pl.pallas_call(functools.partial(forward_kernel, dp, layer, first), out_s...  132 us
    unnamed x14, local copies, waits for them, and re-layouts  14 us
  transfers between devices with their start and end apart: 1, of which 0 were waited for; matrix products, arithmetic and copies ran while one was open for 3% of the time, Pallas kernels for 0%

profile of v2, /device:TPU:0, one launch (start us, length us, event | category | flops | bytes accessed | tf_op | source)
XLA Modules:
  0.0 440.2 jit_solution(6857095738529385537)
XLA Ops:
  0.6 0.5 collective-permute-start
  1.2 0.7 compare_bitcast_fusion
  1.8 0.7 subtract_reduce_fusion
  2.6 3.4 copy.24
  6.0 3.1 copy.18
  9.6 2.0 pad.4.my_wfi
  11.7 2.5 fusion
  15.2 0.6 concatenate.43.scal
  15.8 0.6 concatenate.44.scal
  16.4 0.6 concatenate.45.scal
  17.0 68.5 %layer_forward.2 = (bf16[2,192,1024]{2,1,0:T(8,128)(2,1)}, bf16[1024,1024]{1,0:T(8,128)(2,1)}, bf16[256,1024]{1,0:T(8,128)(2,1)}, bf16[2,1024,768]{2,1,0:T(8,128...) custom-call(bf16[2,192,1024]{2,1,0:T(8,128)(2,1)} %tok_in.1, ...), custom_call_target="tpu_custom_call" | custom-call | flops 6845104128 | bytes 20971520 | tf_op jit(solution)/shard_map/layer_forward/pallas_call | solution.py:604
  85.5 63.7 %layer_forward.3 = (bf16[2,192,1024]{2,1,0:T(8,128)(2,1)}, bf16[1024,1024]{1,0:T(8,128)(2,1)}, bf16[256,1024]{1,0:T(8,128)(2,1)}, bf16[2,1024,768]{2,1,0:T(8,128...) custom-call(bf16[192,1024]{1,0:T(8,128)(2,1)} %get-tuple-element.50., ...), custom_call_target="tpu_custom_call" | custom-call | flops 6845104128 | bytes 20971520 | tf_op jit(solution)/shard_map/layer_forward/pallas_call | solution.py:604
  149.2 264.5 %layers_backward.1 = (bf16[2,192,1024]{2,1,0:T(8,128)(2,1)}, bf16[2,1024,768]{2,1,0:T(8,128)(2,1)}, bf16[2,768,512]{2,1,0:T(8,128)(2,1)}, bf16[2,1280,512]{2,1,0:T(8,128)(2,1)}) custom-call(bf16[2,192,1024]{2,1,0:T(8,128)(2,1)} %ct_in.1, bf16[192,1024]{1,0:T(8,128)(2,1)} %get-tuple-element.50.x_in.y0_in, bf16[2,192,1024]{2,1,0:T(8,128)(2,1)} %tok_in.1, ...), custom_call_target="tpu_custom_call" | custom-call | flops 22548578304 | bytes 62914560 | tf_op jit(solution)/shard_map/layers_backward/pallas_call | solution.py:1169
  413.7 1.7 fusion.8
  415.4 1.8 fusion.7
  417.4 0.3 concatenate.46
  417.7 5.0 %convert_bitcast_fusion = f32[1,1024,2,704]{3,1,2,0:T(8,128)} fusion(bf16[2,1024,768]{2,1,0:T(8,128)(2,1)} %get-tuple-element.90), kind=kLoop, calls=%fused_computation | loop fusion | flops 1441792 | bytes 8650752 | tf_op jit(solution)/shard_map/broadcast_in_dim | solution.py:1239
  422.8 6.4 %copy.23 = f32[1,1024,2,704]{1,3,2,0:T(8,128)} copy(f32[1,1024,2,704]{3,1,2,0:T(8,128)} %convert_bitcast_fusion) | data formatting | bytes 11534336
  429.1 1.5 fusion.9
  430.9 1.0 select_bitcast_fusion
  431.9 3.9 maximum_convert_fusion
  435.8 1.1 maximum_convert_fusion.2
  436.9 2.0 maximum_convert_fusion.1
  438.9 0.9 copy.26
  (37 shorter events, 2.1 us)
Async XLA Ops:
  0.6 13.5 %collective-permute-start = (f32[2]{0:T(128)}, f32[2]{0:T(128)S(1)}, u32[]{:S(2)}, u32[]{:S(2)}) collective-permute-start(f32[2]{0:T(128)} %bitcast.29), channel_id=1, source_target_pairs={{0,16},{16,0},{1,17},{17,1},{2,18},{18,2},{3,19},{19,3},{4,20},{20... | collective-permute-start | bytes 32 | tf_op jit(solution)/shard_map/ppermute | solution.py:1203
  9.6 4.5 %copy-start.4 = (f32[1,2]{1,0:T(1,128)S(1)}, f32[1,2]{1,0:T(1,128)}, u32[]{:S(2)}) copy-start(f32[1,2]{1,0:T(1,128)} %param.14) | copy-start | bytes 28
  429.1 1.6 copy-start.1
  429.1 1.8 copy-start.2
  431.9 3.9 copy-start
  435.8 3.1 copy-start.3

commit v3 on v2

--- a/solution.py
+++ b/solution.py
@@ -17,6 +17,7 @@
 ANY = pl.BlockSpec(memory_space=pl.ANY)
 SMEM = pl.BlockSpec(memory_space=pltpu.SMEM)
 bf16, f32 = jnp.bfloat16, jnp.float32
+PIECES = 16
 VMEM_BYTES = 62 * 1024 * 1024
 
 
@@ -625,176 +626,206 @@
     )(x, *weights, cos2, sin2, scal)
 
 
+class CorePair:
+    def __init__(self, where, halves, from_core, ssem, rsem):
+        s, d, t = where
+        self.s, self.halves, self.landed = s, halves, from_core
+        self.copy = lambda: remote(halves.at[1 - s], from_core, ssem, rsem, (1 - s, d, t))
+
+    def send(self):
+        self.copy().start()
+
+    def add(self):
+        self.copy().wait()
+        rows = self.landed.shape[0]
+        step = 128
+
+        def chunk(n, c):
+            r = rows_of(n, step)
+            mine = self.halves[self.s, r, :].astype(f32)
+            self.halves[self.s, r, :] = (mine + self.landed[r, :].astype(f32)).astype(bf16)
+            return c
+
+        lax.fori_loop(0, rows // step, chunk, 0)
+
+
 class LineSum:
-    def __init__(self, dp, where, owner, arrays, sems):
-        self.dp, self.where, self.owner, self.arrays = dp, where, owner, arrays
-        self.core_s, self.core_r, self.rs, self.rr, self.gs, self.gr, self.ol, self.os, self.or_ = sems
-
-    def each(self, fn):
-        for n, array in enumerate(self.arrays):
-            fn(n, *array)
-
-    def own(self, halves, j):
-        count = halves.shape[1] // self.dp
-        return halves.at[self.where[0], rows_of(j, count)]
-
-    def over(self, n, halves, from_core):
-        s, d, t = self.where
-        return remote(
-            halves.at[1 - s], from_core, self.core_s.at[n], self.core_r.at[n], (1 - s, d, t)
+    LAG = 2
+    END = 4 * LAG
+
+    def __init__(self, dp, where, owner, halves, first, size, land, fin, result, sems, before):
+        self.dp, self.where, self.owner, self.before = dp, where, owner, before
+        self.halves, self.first, self.size, self.land, self.fin = halves, first, size, land, fin
+        self.result = result
+        self.recv, self.sent, self.free, self.ol, self.os, self.or_ = sems
+        self.age = -1
+        s, d, t = where
+        low = dp // 2 - 1
+        self.upward = d <= low
+        self.middle = (d == low) | (d == low + 1)
+        self.edge = (d == 0) | (d == dp - 1)
+        self.inner = (s, jnp.where(self.upward, d + 1, d - 1), t)
+        self.outer = (s, jnp.where(self.upward, d - 1, d + 1), t)
+        self.mine = jnp.where(self.upward, 0, 1)
+
+    def own(self, h=None):
+        return self.halves.at[self.where[0], self.rows(self.first, h)]
+
+    def rows(self, base, h=None):
+        if h is None:
+            return pl.ds(base, self.size)
+        half = self.size // 2
+        return pl.ds(pl.multiple_of(base + h * half, 16), half)
+
+    def final(self, h):
+        return self.fin.at[self.rows(self.first, h)]
+
+    def inward(self):
+        landing = self.land.at[self.rows(self.first)]
+        return remote(self.own(), landing, self.sent.at[0], self.recv.at[2], self.inner)
+
+    def swap_part(self):
+        h = 1 - self.mine
+        return remote(self.own(h), self.final(h), self.sent.at[0], self.recv.at[h], self.inner)
+
+    def swap_sum(self):
+        ref = self.final(self.mine)
+        return remote(ref, ref, self.sent.at[1], self.recv.at[self.mine], self.inner)
+
+    def outward(self, h):
+        ref = self.final(h)
+        return remote(ref, ref, self.sent.at[2 + h], self.recv.at[h], self.outer)
+
+    def sweep(self, base, size, fn):
+        unit = 32 if size % 32 == 0 else 16
+
+        def chunk(n, c):
+            fn(pl.ds(pl.multiple_of(base + n * unit, 16), unit))
+            return c
+
+        lax.fori_loop(0, size // unit, chunk, 0)
+
+    def start(self):
+        self.age = 0
+        before = self.before
+        if before is not None:
+            assert before.age >= self.END
+            before.close()
+
+            @pl.when(self.middle)
+            def _():
+                pl.semaphore_signal(
+                    self.free, inc=1, device_id=self.inner, device_id_type=MESH
+                )
+
+        if self.dp > 2:
+            pl.when(self.edge)(lambda: self.inward().start())
+
+    def tick(self):
+        self.age += 1
+        if self.dp == 1:
+            if self.age == self.END:
+                self.fin[...] = self.halves[0]
+            return
+        s = self.where[0]
+        inside = jnp.logical_not(self.edge)
+        if self.age == self.LAG:
+
+            @pl.when(inside)
+            def _():
+                self.inward().wait_recv()
+
+                def fn(r):
+                    total = self.halves[s, r, :].astype(f32) + self.land[r, :].astype(f32)
+                    self.halves[s, r, :] = total.astype(bf16)
+
+                self.sweep(self.first, self.size, fn)
+                pl.when(jnp.logical_not(self.middle))(lambda: self.inward().start())
+
+            @pl.when(self.middle)
+            def _():
+                if self.before is not None:
+                    pl.semaphore_wait(self.free, 1)
+                self.swap_part().start()
+
+        if self.age == 2 * self.LAG:
+
+            @pl.when(self.middle)
+            def _():
+                h = self.mine
+                half = self.size // 2
+                self.arrived(h)
+
+                def fn(r):
+                    total = self.halves[s, r, :].astype(f32) + self.fin[r, :].astype(f32)
+                    self.fin[r, :] = total.astype(bf16)
+
+                self.sweep(self.first + h * half, half, fn)
+                self.swap_sum().start()
+                pl.when(inside)(lambda: self.outward(h).start())
+                self.swap_part().wait_send()
+
+            pl.when(jnp.logical_not(self.middle))(lambda: self.inward().wait_send())
+
+        if self.age == 3 * self.LAG:
+
+            @pl.when(self.middle)
+            def _():
+                self.arrived(1 - self.mine)
+                pl.when(inside)(lambda: self.outward(1 - self.mine).start())
+
+        if self.age == self.END:
+
+            @pl.when(jnp.logical_not(self.middle))
+            def _():
+                for h in (0, 1):
+                    self.arrived(h)
+                    pl.when(inside)(lambda h=h: self.outward(h).start())
+
+            pl.when(self.middle)(lambda: self.swap_sum().wait_send())
+
+            @pl.when(inside)
+            def _():
+                for h in (0, 1):
+                    self.outward(h).wait_send()
+
+            self.to_result()[0]()
+
+    def arrived(self, h):
+        ref = self.final(h)
+        remote(ref, ref, self.sent.at[0], self.recv.at[h], self.where).wait_recv()
+
+    def to_result(self):
+        s = self.where[0]
+        part = self.rows(self.first)
+        target = self.result.at[s, part]
+        return to_owner(
+            self.owner, self.where, self.fin.at[part], target, target, self.ol, self.os, self.or_
         )
 
-    def core_send(self):
-        self.each(lambda n, halves, fc, land, res: self.over(n, halves, fc).start())
-
-    def core_add(self):
-        s = self.where[0]
-
-        def one(n, halves, fc, land, res):
-            self.over(n, halves, fc).wait()
-            count = halves.shape[1] // self.dp
-
-            def chunk(j, c):
-                r = rows_of(j, count)
-                halves[s, r, :] = (halves[s, r, :].astype(f32) + fc[r, :].astype(f32)).astype(bf16)
-                return c
-
-            lax.fori_loop(0, self.dp, chunk, 0)
-
-        self.each(one)
-
-    def partial(self, n, land, j, up):
-        s, d, t = self.where
-        to = d + 1 if up else d - 1
-        slot = j if up else jnp.where(j == to, self.dp, j)
-        return remote(land.at[j], land.at[slot], self.rs.at[n, j], self.rr.at[n, slot], (s, to, t))
-
-    def landed(self, n, land, slot):
-        s, d, t = self.where
-        return remote(land.at[slot], land.at[slot], self.rs.at[n, 0], self.rr.at[n, slot], (s, d, t))
-
-    def final(self, n, halves, j, up):
-        s, d, t = self.where
-        to = d + 1 if up else d - 1
-        ref = self.own(halves, j)
-        k = j if up else jnp.where(j == d, self.dp, j)
-        return remote(ref, ref, self.gs.at[n, k], self.gr.at[n, j], (s, to, t))
-
-    def arrived(self, n, halves, j):
-        s, d, t = self.where
-        ref = self.own(halves, j)
-        return remote(ref, ref, self.gs.at[n, 0], self.gr.at[n, j], (s, d, t))
-
-    def add(self, n, halves, land, slot, j, into_own):
-        s = self.where[0]
-        self.landed(n, land, slot).wait_recv()
-        r = rows_of(j, halves.shape[1] // self.dp)
-        total = (halves[s, r, :].astype(f32) + land[slot].astype(f32)).astype(bf16)
-        if into_own:
-            halves[s, r, :] = total
-        else:
-            land[slot] = total
-
-    def step(self, k):
-        dp = self.dp
-        s, d, t = self.where
-        if dp == 1:
-            return
-        if k < dp - 1:
-            for up in (True, False):
-                e = d if up else dp - 1 - d
-                j = dp - 1 - k + d if up else k - (dp - 1 - d)
-
-                def one(n, halves, fc, land, res, up=up, e=e, j=j):
-                    @pl.when(e == 0)
-                    def _():
-                        land[j] = halves[s, rows_of(j, halves.shape[1] // dp), :]
-                        self.partial(n, land, j, up).start()
-
-                    @pl.when((e > 0) & (e <= k))
-                    def _():
-                        self.add(n, halves, land, j, j, False)
-                        self.partial(n, land, j, up).start()
-
-                self.each(one)
-            return
-        a = k - (dp - 1)
-        if a == 0:
-
-            def one(n, halves, fc, land, res):
-                def sent(j, c):
-                    pl.when(j > d)(lambda: self.partial(n, land, j, True).wait_send())
-                    pl.when(j < d)(lambda: self.partial(n, land, j, False).wait_send())
-                    return c
-
-                @pl.when(d > 0)
-                def _():
-                    self.add(n, halves, land, d, d, True)
-
-                @pl.when(d < dp - 1)
-                def _():
-                    self.add(n, halves, land, dp, d, True)
-
-                lax.fori_loop(0, dp, sent, 0)
-                pl.when(d < dp - 1)(lambda: self.final(n, halves, d, True).start())
-                pl.when(d > 0)(lambda: self.final(n, halves, d, False).start())
-
-            self.each(one)
-            return
-
-        def one(n, halves, fc, land, res):
-            @pl.when(d - a >= 0)
-            def _():
-                self.arrived(n, halves, d - a).wait_recv()
-                pl.when(d < dp - 1)(lambda: self.final(n, halves, d - a, True).start())
-
-            @pl.when(d + a < dp)
-            def _():
-                self.arrived(n, halves, d + a).wait_recv()
-                pl.when(d > 0)(lambda: self.final(n, halves, d + a, False).start())
-
-        self.each(one)
-
-    def results(self):
-        out = []
-
-        def one(n, halves, fc, land, res):
-            s = self.where[0]
-            out.append(
-                to_owner(
-                    self.owner, self.where, halves.at[s], res.at[s], res.at[s],
-                    self.ol.at[n], self.os.at[n], self.or_.at[n],
-                )
-            )
-
-        self.each(one)
-        return out
-
-    def finish(self):
-        dp = self.dp
-        s, d, t = self.where
-
-        def one(n, halves, fc, land, res):
-            def sent(j, c):
-                @pl.when((j <= d) & (d < dp - 1))
-                def _():
-                    self.final(n, halves, j, True).wait_send()
-
-                @pl.when((j >= d) & (d > 0))
-                def _():
-                    self.final(n, halves, j, False).wait_send()
-
-                return c
-
-            lax.fori_loop(0, dp, sent, 0)
-
-        self.each(one)
-        for start, _ in self.results():
-            start()
-
     def close(self):
-        for _, finish in self.results():
-            finish()
+        self.to_result()[1]()
+
+
+class Background:
+    def __init__(self):
+        self.queue, self.active = [], []
+
+    def put(self, pieces):
+        self.queue += pieces
+
+    def tick(self):
+        for piece in self.active:
+            piece.tick()
+        self.active = [piece for piece in self.active if piece.age < piece.END]
+        if self.queue:
+            piece = self.queue.pop(0)
+            piece.start()
+            self.active.append(piece)
+
+    def until(self, pieces, age):
+        while any(piece.age < age for piece in pieces):
+            self.tick()
 
 
 def backward_kernel(
@@ -807,7 +838,7 @@
         wi, wo, wfi, wfo, cosv, sinv, gf, xr, hidden, zq, zk, gate, q, k, v, att, sc, states, branch, mid,
         hid2, pair, mask, mask_t, qd, kd, terms, zout, zin, run, gpair, prod, gb, gm, dv, dk,
         gp, part, got, via, own, gr, gwfi, gwfo, gmix, c_fi, c_fo, c_mix, l_fi, l_fo, l_mix,
-        lsem, ssem, rsem, zs, zr, ol, os, or_, core_s, core_r, ls, lr, fs, fr,
+        f_fi, f_fo, f_mix, lsem, ssem, rsem, zs, zr, ol, os, or_, core_s, core_r, ls, lr, free,
     ) = refs[32:]
     where = s, d, t = place()
     rows = y0_in.shape[0]
@@ -856,31 +887,28 @@
         x = tok_in.at[s] if layer == 0 else y0_in
         return [load(weights[layer][0], wi), load(saved_i[layer][0], hidden), load(x, xr)]
 
-    def line(arrays, base, layer):
-        n = len(arrays)
-        at = pl.ds(base, n)
-        sems = [ref.at[at] for ref in (core_s, core_r, ls, lr, fs, fr, ol, os, or_)]
-        return LineSum(dp, where, s == layer, arrays, sems)
-
-    feeds = [
-        line(
-            (
-                (gwfi.at[layer], c_fi, l_fi, gwfi_o),
-                (gwfo.at[layer], c_fo, l_fo, gwfo_o),
-            ),
-            3 * layer, layer,
-        )
-        for layer in (0, 1)
-    ]
-    mixes = [line(((gmix, c_mix, l_mix, gmix_o),), 3 * layer + 2, layer) for layer in (0, 1)]
-    steps = 2 * dp - 1
-    progress = {}
-
-    def tick(piece, count=1):
-        at = progress.get(id(piece), 0)
-        for n in range(at, min(at + count, steps)):
-            piece.step(n)
-        progress[id(piece)] = at + count
+
+    ff = l_fo.shape[0]
+    pieces, pairs = {}, {}
+    for layer in (1, 0):
+        cuts = [(gwfo, 256 * n, min(256, ff - 256 * n), l_fo, f_fo, gwfo_o) for n in range(-(-ff // 256))]
+        cuts += [(gwfi, 128 * n, 128, l_fi, f_fi, gwfi_o) for n in range(D // 128)]
+        cuts += [(gmix, 256 * n, 256, l_mix, f_mix, gmix_o) for n in range((D + WIDTH) // 256)]
+        made = []
+        for n, cut in enumerate(cuts):
+            slot = PIECES * layer + n
+            sems = [ref.at[slot] for ref in (lr, ls)] + [free.at[n]]
+            sems += [ref.at[slot] for ref in (ol, os, or_)]
+            before = pieces[1][n] if layer == 0 else None
+            made.append(LineSum(dp, where, s == layer, *cut, sems, before))
+        pieces[layer] = made
+        pairs[layer] = [
+            CorePair(where, halves, landed, core_s.at[3 * layer + n], core_r.at[3 * layer + n])
+            for n, (halves, landed) in enumerate(((gwfo, c_fo), (gwfi, c_fi), (gmix, c_mix)))
+        ]
+    n_out, n_feed = -(-ff // 256), -(-ff // 256) + D // 128
+    work = Background()
+    tick = work.tick
 
     got_g = load(ct_in.at[s], gf.at[me])
     in_feed, in_tables = load_feed(1), [load(cos2, cosv), load(sin2, sinv)]
@@ -891,15 +919,15 @@
 
     for layer in (1, 0):
         offset = table * layer
-        a_now, b_now = feeds[layer], mixes[layer]
-        a_old, b_old = (feeds[1], mixes[1]) if layer == 0 else (None, None)
+        pair_fo, pair_fi, pair_mix = pairs[layer]
         base = 24 * layer
         gg = Gather(block_of(gf), half, ssem, rsem, base, where)
         gg.start()
         decay_fill(scal, offset, nb, mask, mask_t, qd, kd)
-        if b_old is not None:
-            b_old.core_add()
-            tick(b_old)
+        if layer == 0:
+            pairs[1][2].add()
+            work.put(pieces[1][n_feed:])
+        tick()
         for copy in in_feed:
             copy.wait()
         sums = Scatter(part, got, via, rows, ssem, rsem, base + 6, where)
@@ -911,6 +939,8 @@
                 def _(n=n):
                     if n == 1:
                         gg.forward()
+                    if n == 3:
+                        tick()
                     gg.ready(n)
 
             r = rows_of(partner(t, i), rows)
@@ -934,28 +964,34 @@
             return c
 
         lax.fori_loop(0, 4, feed, 0)
-        sums.combine()
-        if a_old is not None:
-            tick(a_old)
-            tick(b_old)
 
         def feed_weights(n, c):
             cols = rows_of(n, 256)
             a = hid2[:, cols]
-            gwfi[layer, 0, cols, :] = tn(a, gpair[0]).astype(bf16)
-            gwfi[layer, 1, cols, :] = tn(a, gpair[1]).astype(bf16)
+            gwfi[0, cols, :] = tn(a, gpair[0]).astype(bf16)
+            gwfi[1, cols, :] = tn(a, gpair[1]).astype(bf16)
             return c
 
         def out_weights(n, c):
             cols = rows_of(n, 256)
             a = prod[:, cols]
-            gwfo[layer, 0, cols, :] = tn(a, gf[:, : D // 2]).astype(bf16)
-            gwfo[layer, 1, cols, :] = tn(a, gf[:, D // 2 :]).astype(bf16)
+            gwfo[0, cols, :] = tn(a, gf[:, : D // 2]).astype(bf16)
+            gwfo[1, cols, :] = tn(a, gf[:, D // 2 :]).astype(bf16)
             return c
 
+        if layer == 0:
+            work.until(pieces[1][:n_feed], 2 * LineSum.LAG)
+        lax.fori_loop(0, fp // 256, out_weights, 0)
+        pair_fo.send()
         lax.fori_loop(0, D // 256, feed_weights, 0)
-        lax.fori_loop(0, fp // 256, out_weights, 0)
-        a_now.core_send()
+        pair_fi.send()
+        tick()
+        sums.combine()
+        pair_fo.add()
+        work.put(pieces[layer][:n_out])
+        tick()
+        pair_fi.add()
+        work.put(pieces[layer][n_out:n_feed])
         grad_middle = gf[me, :].astype(f32) + norm_back(mid[...], own[...] + sums.result())
         gm[...] = grad_middle
         gb[me, :] = grad_middle.astype(bf16)
@@ -966,11 +1002,7 @@
         gbg.start()
         if layer == 1:
             in_feed = load_feed(0)
-        if a_old is not None:
-            tick(a_old, 1 if steps <= 7 else steps)
-            tick(b_old)
-        a_now.core_add()
-        tick(a_now)
+        tick()
         for copy in in_gates:
             copy.wait()
 
@@ -981,6 +1013,8 @@
                 def _(n=n):
                     if n == 1:
                         gbg.forward()
+                    if n == 3:
+                        tick()
                     gbg.ready(n)
 
             r = rows_of(partner(t, i), rows)
@@ -1019,9 +1053,7 @@
             zout[layer, h] = carried.astype(bf16)
         z_args = (dp, where, zout.at[layer], zin.at[layer], zs.at[layer], zr.at[layer], False)
         send_states(*z_args)
-        if a_old is not None:
-            tick(b_old)
-        tick(a_now)
+        tick()
 
         def unturn(pre, grad, r, h):
             back = grad * cosv[r, :] - pltpu.roll(grad, HEAD // 2, 1) * sinv[r, :]
@@ -1043,6 +1075,7 @@
             return c
 
         lax.fori_loop(0, nb, inner, 0)
+        tick()
         take_states(*z_args, scal, offset + nb + 4 + 2 * dp, run)
 
         def outer(i, c):
@@ -1061,6 +1094,7 @@
             return c
 
         lax.fori_loop(0, nb, outer, 0)
+        tick()
         if layer == 1:
             in_attn = load_attn(0)
         for copy in in_ends:
@@ -1084,14 +1118,9 @@
             return c
 
         lax.fori_loop(0, 4, back_in, 0)
-        ins.combine()
-        tick(a_now)
-        if a_old is not None:
-            tick(a_old, steps)
-            tick(b_old, steps)
-            a_old.finish()
-            b_old.finish()
-            b_old.close()
+        tick()
+        if layer == 0:
+            work.until(pieces[1], 2 * LineSum.LAG)
 
         def in_weights(n, c):
             cols = rows_of(n, 256)
@@ -1103,7 +1132,9 @@
         lax.fori_loop(0, D // 256, in_weights, 0)
         gmix[0, D:, :] = tn(prod[:, gated], gb[:, : D // 2]).astype(bf16)
         gmix[1, D:, :] = tn(prod[:, gated], gb[:, D // 2 :]).astype(bf16)
-        b_now.core_send()
+        pair_mix.send()
+        ins.combine()
+        tick()
         dx = gm[...] + norm_back(xr[...].astype(f32), own[...] + ins.result())
         gr[layer] = dx.astype(bf16)
         ins.drain()
@@ -1111,29 +1142,24 @@
         sent_states(*z_args)
         start, finish = to_owner(
             s == layer, where, gr.at[layer], both_o.at[s], both_o.at[s],
-            ol.at[6 + layer], os.at[6 + layer], or_.at[6 + layer],
+            ol.at[2 * PIECES + layer], os.at[2 * PIECES + layer], or_.at[2 * PIECES + layer],
         )
         start()
         in_out.append(finish)
-        tick(a_now)
         if layer == 1:
             gf[me, :] = gr[layer]
             in_ends = load_ends(0)
 
-    b_now.core_add()
-    while progress.get(id(b_now), 0) < steps or progress.get(id(a_now), 0) < steps:
-        tick(b_now)
-        tick(a_now)
-    a_now.finish()
-    b_now.finish()
-    feeds[1].close()
-    a_now.close()
-    b_now.close()
+    pairs[0][2].add()
+    work.put(pieces[0][n_feed:])
+    work.until(pieces[0], LineSum.END)
+    for piece in pieces[0]:
+        piece.close()
     for finish in in_out:
         finish()
 
 
-def layers_backward(cotangent, y0, tokens, cos2, sin2, scal, weights, saved, dp, uid):
+def layers_backward(cotangent, y0, tokens, cos2, sin2, scal, weights, saved, dp, ff, uid):
     rows = y0.shape[-2]
     total = 4 * rows
     nb = total // BLOCK
@@ -1157,11 +1183,12 @@
         ((total, 4 * WIDTH), bf16),
         ((3, rows, D), bf16), ((2, rows, D), bf16), ((2, rows // 2, D), bf16), ((rows, D), f32),
         ((2, rows, D), bf16),
-        ((2, 2, D, fp), bf16), ((2, 2, fp, D // 2), bf16), ((2, mixed, D // 2), bf16),
+        ((2, D, fp), bf16), ((2, fp, D // 2), bf16), ((2, mixed, D // 2), bf16),
         ((D, fp), bf16), ((fp, D // 2), bf16), ((mixed, D // 2), bf16),
-        ((dp + 1, D // dp, fp), bf16), ((dp + 1, fp // dp, D // 2), bf16),
-        ((dp + 1, mixed // dp, D // 2), bf16),
+        ((D, fp), bf16), ((ff, D // 2), bf16), ((mixed, D // 2), bf16),
+        ((D, fp), bf16), ((ff, D // 2), bf16), ((mixed, D // 2), bf16),
     ]
+    count = 2 * PIECES
     dma = pltpu.SemaphoreType.DMA
     flops = 8 * total * D * (4 * WIDTH + WIDTH + 3 * fp)
     flat = [w for layer in weights for w in layer]
@@ -1173,9 +1200,9 @@
         out_specs=(ANY,) * len(outs),
         scratch_shapes=[pltpu.VMEM(a, b) for a, b in scratch]
         + [
-            dma((48,)), dma((48,)), dma((48,)), dma((2, dp)), dma((2, dp)), dma((8,)), dma((8,)),
-            dma((8,)), dma((6,)), dma((6,)), dma((6, dp)), dma((6, dp + 1)), dma((6, dp + 1)),
-            dma((6, dp)),
+            dma((48,)), dma((48,)), dma((48,)), dma((2, dp)), dma((2, dp)), dma((count + 2,)),
+            dma((count + 2,)), dma((count + 2,)), dma((6,)), dma((6,)), dma((count, 4)),
+            dma((count, 3)), pltpu.SemaphoreType.REGULAR((PIECES,)),
         ],
         compiler_params=pltpu.CompilerParams(
             collective_id=uid, has_side_effects=True, vmem_limit_bytes=VMEM_BYTES
@@ -1229,7 +1256,7 @@
     weights1, saved1 = out1[:4], out1[5:]
     in_grads, g_fi, g_fo, g_mix = layers_backward(
         cotangent, y0, tokens, cos2, sin2, jnp.concatenate(scal), (weights0, weights1),
-        (saved0, saved1), dp, 3,
+        (saved0, saved1), dp, ff, 3,
     )
     outputs = mine_first(s, both0, both1)
     g_in = jnp.concatenate([g_mix[0, :D], g_mix[1, :D]], axis=1).astype(f32).reshape(D, 4, WIDTH)

time: 449 us -> 409 us (0.911); the launches traced: 440 us -> 409 us
  Pallas kernels: 397 us -> 366 us
    pallas_call x1, Pallas kernels: 264 us -> 233 us  [layers_backward(): pl.pallas_call(functools.partial(backward_kernel, dp), out_shape=tuple((j...]
where the time goes in v3:
time: 409 us
  Pallas kernels  366 us (89%)
  local copies, waits for them, and re-layouts  24.3 us (6%)
  other arithmetic  17.5 us (4%)
    pallas_call x1, Pallas kernels, layers_backward(): pl.pallas_call(functools.partial(backward_kernel, dp), out_shape=tuple((j...  233 us
    pallas_call x2, Pallas kernels, layer_forward(): pl.pallas_call(functools.partial(forward_kernel, dp, layer, first), out_s...  132 us
    unnamed x14, local copies, waits for them, and re-layouts  14 us
  transfers between devices with their start and end apart: 1, of which 0 were waited for; matrix products, arithmetic and copies ran while one was open for 3% of the time, Pallas kernels for 0%

profile of v3, /device:TPU:0, one launch (start us, length us, event | category | flops | bytes accessed | tf_op | source)
XLA Modules:
  0.0 408.7 jit_solution(1930637262134337128)
XLA Ops:
  0.6 0.5 collective-permute-start
  1.2 0.7 compare_bitcast_fusion
  1.8 0.7 subtract_reduce_fusion
  2.6 3.4 copy.24
  6.0 3.1 copy.18
  9.6 2.0 pad.4.my_wfi
  11.7 2.5 fusion
  15.2 0.6 concatenate.43.scal
  15.8 0.6 concatenate.44.scal
  16.4 0.6 concatenate.45.scal
  17.0 68.5 %layer_forward.2 = (bf16[2,192,1024]{2,1,0:T(8,128)(2,1)}, bf16[1024,1024]{1,0:T(8,128)(2,1)}, bf16[256,1024]{1,0:T(8,128)(2,1)}, bf16[2,1024,768]{2,1,0:T(8,128...) custom-call(bf16[2,192,1024]{2,1,0:T(8,128)(2,1)} %tok_in.1, ...), custom_call_target="tpu_custom_call" | custom-call | flops 6845104128 | bytes 20971520 | tf_op jit(solution)/shard_map/layer_forward/pallas_call | solution.py:605
  85.5 63.7 %layer_forward.3 = (bf16[2,192,1024]{2,1,0:T(8,128)(2,1)}, bf16[1024,1024]{1,0:T(8,128)(2,1)}, bf16[256,1024]{1,0:T(8,128)(2,1)}, bf16[2,1024,768]{2,1,0:T(8,128...) custom-call(bf16[192,1024]{1,0:T(8,128)(2,1)} %get-tuple-element.50., ...), custom_call_target="tpu_custom_call" | custom-call | flops 6845104128 | bytes 20971520 | tf_op jit(solution)/shard_map/layer_forward/pallas_call | solution.py:605
  149.2 233.4 %layers_backward.1 = (bf16[2,192,1024]{2,1,0:T(8,128)(2,1)}, bf16[2,1024,768]{2,1,0:T(8,128)(2,1)}, bf16[2,768,512]{2,1,0:T(8,128)(2,1)}, bf16[2,1280,512]{2,1,0:T(8,128)(2,1)}) custom-call(bf16[2,192,1024]{2,1,0:T(8,128)(2,1)} %ct_in.1, bf16[192,1024]{1,0:T(8,128)(2,1)} %get-tuple-element.50.x_in.y0_in, bf16[2,192,1024]{2,1,0:T(8,128)(2,1)} %tok_in.1, ...), custom_call_target="tpu_custom_call" | custom-call | flops 22548578304 | bytes 62914560 | tf_op jit(solution)/shard_map/layers_backward/pallas_call | solution.py:1196
  382.6 1.7 fusion.8
  384.3 1.8 fusion.7
  386.3 0.3 concatenate.46
  386.6 5.0 %convert_bitcast_fusion = f32[1,1024,2,704]{3,1,2,0:T(8,128)} fusion(bf16[2,1024,768]{2,1,0:T(8,128)(2,1)} %get-tuple-element.90), kind=kLoop, calls=%fused_computation | loop fusion | flops 1441792 | bytes 8650752 | tf_op jit(solution)/shard_map/broadcast_in_dim | solution.py:1266
  391.7 6.4 %copy.23 = f32[1,1024,2,704]{1,3,2,0:T(8,128)} copy(f32[1,1024,2,704]{3,1,2,0:T(8,128)} %convert_bitcast_fusion) | data formatting | bytes 11534336
  398.0 1.5 fusion.9
  399.8 1.0 select_bitcast_fusion
  400.8 3.9 maximum_convert_fusion
  404.7 1.1 maximum_convert_fusion.2
  405.8 2.0 maximum_convert_fusion.1
  407.8 0.9 copy.26
  (37 shorter events, 2.1 us)
Async XLA Ops:
  0.6 13.5 %collective-permute-start = (f32[2]{0:T(128)}, f32[2]{0:T(128)S(1)}, u32[]{:S(2)}, u32[]{:S(2)}) collective-permute-start(f32[2]{0:T(128)} %bitcast.29), channel_id=1, source_target_pairs={{0,16},{16,0},{1,17},{17,1},{2,18},{18,2},{3,19},{19,3},{4,20},{20... | collective-permute-start | bytes 32 | tf_op jit(solution)/shard_map/ppermute | solution.py:1230
  9.6 4.5 %copy-start.4 = (f32[1,2]{1,0:T(1,128)S(1)}, f32[1,2]{1,0:T(1,128)}, u32[]{:S(2)}) copy-start(f32[1,2]{1,0:T(1,128)} %param.14) | copy-start | bytes 28
  398.0 1.6 copy-start.1
  398.0 1.8 copy-start.2
  400.8 3.9 copy-start
  404.7 3.1 copy-start.3

commit v4 on v3

--- a/solution.py
+++ b/solution.py
@@ -207,7 +207,7 @@
     forward = jnp.where((at < d)[:, None], through, 0.0)
     backward = jnp.where((at > d)[:, None], through, 0.0)
     mine = lax.dynamic_index_in_dim(survive, d, 0, keepdims=False)
-    return jnp.concatenate([mine, rates, decay, forward.reshape(-1), backward.reshape(-1)])
+    return [mine, rates, decay, forward.reshape(-1), backward.reshape(-1)]
 
 
 def decay_fill(scal, base, nb, mask, mask_t, qd, kd):
@@ -331,6 +331,7 @@
     rows = x_in.shape[-2]
     total = 4 * rows
     nb = total // BLOCK
+    at = layer * (nb + 4 + 4 * dp)
     local = Sems(lsem)
 
     def load(src, dst):
@@ -343,7 +344,8 @@
     owner = s == layer
     ff = my_wfo.shape[0]
     pairs = (
-        (my_wi, wi), (my_wo, wo.at[rows_of(t, WIDTH)]), (my_wfi, wfi), (my_wfo, wfo.at[pl.ds(0, ff)])
+        (my_wi, wi), (my_wo, wo.at[rows_of(t, WIDTH)]), (my_wfi, wfi.at[:, pl.ds(0, ff)]),
+        (my_wfo, wfo.at[pl.ds(0, ff)]),
     )
     got_w = [
         Fetch(src, dst, owner, where, wl.at[n], ws.at[n], wr.at[n])
@@ -354,6 +356,7 @@
     got_cos, got_sin = load(cos2, cosv), load(sin2, sinv)
     for fetch in got_w[1:]:
         fetch.read()
+    wfi[:, ff:, :] = jnp.zeros_like(wfi[:, ff:, :])
     wfo[ff:, :] = jnp.zeros_like(wfo[ff:, :])
     entry(dp, s, d, t, core=True)
     got_x.wait()
@@ -363,10 +366,20 @@
         lambda p, h: xf.at[pl.ds(pl.multiple_of(p * rows + h * half, half), half)],
         half, ssem, rsem, 0, where,
     )
+    quarter = WIDTH // 2
+    gw = Gather(
+        lambda p, h: wo.at[pl.ds(pl.multiple_of(p * WIDTH + h * quarter, quarter), quarter)],
+        quarter, ws, wr, 4, where,
+    )
+
+    def wo_over(k):
+        ref = wo.at[rows_of(partner(t, k), WIDTH)]
+        return remote(ref, ref, ws.at[10 + k], wr.at[10 + k], (1 - s, d, t))
+
     gx.start()
     for fetch in got_w:
         fetch.send()
-    decay_fill(scal, 0, nb, mask, None, qd, kd)
+    decay_fill(scal, at, nb, mask, None, qd, kd)
     got_wi.wait()
     got_cos.wait()
     got_sin.wait()
@@ -378,6 +391,12 @@
             def _(n=n):
                 if n == 1:
                     gx.forward()
+
+                    @pl.when(owner)
+                    def _():
+                        got_wo.local().wait()
+                        gw.start()
+
                 gx.ready(n)
 
         r = rows_of(partner(t, i), rows)
@@ -398,25 +417,6 @@
 
     lax.fori_loop(0, 4, project, 0)
 
-    def wo_block(k, k_to, n, dev):
-        ref = wo.at[rows_of(partner(t, k), WIDTH)]
-        return remote(ref, ref, ws.at[n], wr.at[n], dev)
-
-    def wo_out(k):
-        return wo_block(0, k, 3 + k, (s, d, partner(t, k)))
-
-    def wo_in(k):
-        return wo_block(k, 0, 3 + k, (s, d, t))
-
-    def wo_over(k):
-        return wo_block(k, 0, 6 + k, (1 - s, d, t))
-
-    @pl.when(owner)
-    def _():
-        got_wo.local().wait()
-        for n in (1, 2, 3):
-            wo_out(n).start()
-
     stores = [load(hidden, hidden_o), load(zq, zq_o), load(zk, zk_o), load(gate, gate_o)]
     stores += [load(q, q_o), load(k, k_o), load(v, v_o)]
 
@@ -428,10 +428,11 @@
         return c
 
     lax.fori_loop(0, nb, local_state, 0)
+    pl.when(owner)(gw.forward)
     for h in range(HEADS_HERE):
         carried = loc[0, h]
         for b in range(1, nb):
-            carried = (scal[nb + 2 + h] * scal[b]) * carried + loc[b, h]
+            carried = (scal[at + nb + 2 + h] * scal[at + b]) * carried + loc[b, h]
         zout[h] = carried.astype(bf16)
     send_states(dp, where, zout, zin, zs, zr, True)
 
@@ -443,14 +444,14 @@
         return c
 
     lax.fori_loop(0, nb, inner, 0)
-    take_states(dp, where, zout, zin, zs, zr, True, scal, nb + 4, run)
+    take_states(dp, where, zout, zin, zs, zr, True, scal, at + nb + 4, run)
 
     def outer(b, c):
         r = rows_of(b, BLOCK)
         for h in range(HEADS_HERE):
-            entering = scal[b] * run[h]
+            entering = scal[at + b] * run[h]
             states[b, h] = entering
-            run[h] = scal[nb + 2 + h] * entering + loc[b, h]
+            run[h] = scal[at + nb + 2 + h] * entering + loc[b, h]
             qdec = (q[r, head(h)].astype(f32) * qd[h]).astype(bf16)
             a = att[r, head(h)] + nn(qdec, entering.astype(bf16))
             att[r, head(h)] = a
@@ -478,7 +479,7 @@
     @pl.when(owner)
     def _():
         for n in (1, 2, 3):
-            wo_in(n).wait_recv()
+            gw.ready(n)
             wo_over(n).start()
 
     @pl.when(jnp.logical_not(owner))
@@ -524,7 +525,7 @@
         m = xf[r, :].astype(f32) + br
         h2 = (m * rms_scale(m)).astype(bf16)
         hid2[r, :] = h2
-        p0, p1 = nn(h2, wfi[0]), nn(h2, wfi[1])
+        p0, p1 = nt(h2, wfi[0]), nt(h2, wfi[1])
         pair[0, r, :] = p0.astype(bf16)
         pair[1, r, :] = p1.astype(bf16)
         o = nn((p0 * p1).astype(bf16), wfo[...])
@@ -549,7 +550,7 @@
     yb[...] = (own[...] + out.result()).astype(bf16)
     stores += [load(yb, y_out)]
     start, finish = to_owner(
-        owner, where, yb, both_o.at[s], both_o.at[s], wl.at[4], ws.at[10], wr.at[10]
+        owner, where, yb, both_o.at[s], both_o.at[s], wl.at[4], ws.at[14], wr.at[14]
     )
     start()
     for fetch in got_w:
@@ -558,8 +559,8 @@
     @pl.when(owner)
     def _():
         for n in (1, 2, 3):
-            wo_out(n).wait_send()
             wo_over(n).wait_send()
+        gw.drain()
 
     finish()
     gx.drain()
@@ -576,7 +577,7 @@
     rows = x.shape[-2]
     total = 4 * rows
     nb = total // BLOCK
-    fp = weights[2].shape[2]
+    fp = -(-weights[3].shape[0] // 256) * 256
     saved = [
         ((rows, D), bf16), ((total, D), bf16), ((total, WIDTH), f32), ((total, WIDTH), f32),
         ((total, WIDTH), f32), ((total, WIDTH), bf16), ((total, WIDTH), bf16),
@@ -585,12 +586,12 @@
         ((total, D), bf16), ((2, total, fp), bf16),
     ]
     scratch = [
-        ((D, 4 * WIDTH), bf16), ((D, D), bf16), ((2, D, fp), bf16), ((fp, D), bf16),
+        ((D, 4 * WIDTH), bf16), ((D, D), bf16), ((2, fp, D), bf16), ((fp, D), bf16),
         ((total, HEAD), f32), ((total, HEAD), f32), ((total, D), bf16),
     ]
     scratch += saved[1:]
     saved = [
-        ((2, rows, D), bf16), ((D, 4 * WIDTH), bf16), ((WIDTH, D), bf16), ((2, D, fp), bf16),
+        ((2, rows, D), bf16), ((D, 4 * WIDTH), bf16), ((WIDTH, D), bf16), ((2, fp, D), bf16),
         ((fp, D), bf16),
     ] + saved
     scratch += [
@@ -615,8 +616,8 @@
             pltpu.SemaphoreType.DMA((dp,)),
             pltpu.SemaphoreType.DMA((dp,)),
             pltpu.SemaphoreType.DMA((5,)),
-            pltpu.SemaphoreType.DMA((11,)),
-            pltpu.SemaphoreType.DMA((11,)),
+            pltpu.SemaphoreType.DMA((15,)),
+            pltpu.SemaphoreType.DMA((15,)),
         ],
         compiler_params=pltpu.CompilerParams(
             collective_id=uid, has_side_effects=True, vmem_limit_bytes=VMEM_BYTES
@@ -892,7 +893,7 @@
     pieces, pairs = {}, {}
     for layer in (1, 0):
         cuts = [(gwfo, 256 * n, min(256, ff - 256 * n), l_fo, f_fo, gwfo_o) for n in range(-(-ff // 256))]
-        cuts += [(gwfi, 128 * n, 128, l_fi, f_fi, gwfi_o) for n in range(D // 128)]
+        cuts += [(gwfi, 128 * n, min(128, ff - 128 * n), l_fi, f_fi, gwfi_o) for n in range(-(-ff // 128))]
         cuts += [(gmix, 256 * n, 256, l_mix, f_mix, gmix_o) for n in range((D + WIDTH) // 256)]
         made = []
         for n, cut in enumerate(cuts):
@@ -906,7 +907,7 @@
             CorePair(where, halves, landed, core_s.at[3 * layer + n], core_r.at[3 * layer + n])
             for n, (halves, landed) in enumerate(((gwfo, c_fo), (gwfi, c_fi), (gmix, c_mix)))
         ]
-    n_out, n_feed = -(-ff // 256), -(-ff // 256) + D // 128
+    n_out, n_feed = -(-ff // 256), -(-ff // 256) + -(-ff // 128)
     work = Background()
     tick = work.tick
 
@@ -950,7 +951,7 @@
             g0, g1 = (grad * p1).astype(bf16), (grad * p0).astype(bf16)
             gpair[0, r, :] = g0
             gpair[1, r, :] = g1
-            o = nt(g0, wfi[0]) + nt(g1, wfi[1])
+            o = nn(g0, wfi[0]) + nn(g1, wfi[1])
             for n in (1, 2, 3):
 
                 @pl.when(i == n)
@@ -967,9 +968,8 @@
 
         def feed_weights(n, c):
             cols = rows_of(n, 256)
-            a = hid2[:, cols]
-            gwfi[0, cols, :] = tn(a, gpair[0]).astype(bf16)
-            gwfi[1, cols, :] = tn(a, gpair[1]).astype(bf16)
+            for part_of in (0, 1):
+                gwfi[part_of, cols, :] = tn(gpair[part_of, :, cols], hid2[...]).astype(bf16)
             return c
 
         def out_weights(n, c):
@@ -983,7 +983,7 @@
             work.until(pieces[1][:n_feed], 2 * LineSum.LAG)
         lax.fori_loop(0, fp // 256, out_weights, 0)
         pair_fo.send()
-        lax.fori_loop(0, D // 256, feed_weights, 0)
+        lax.fori_loop(0, fp // 256, feed_weights, 0)
         pair_fi.send()
         tick()
         sums.combine()
@@ -1166,10 +1166,10 @@
     fp = weights[0][3].shape[0]
     mixed = D + WIDTH
     outs = [
-        ((2, rows, D), bf16), ((2, D, fp), bf16), ((2, fp, D // 2), bf16), ((2, mixed, D // 2), bf16)
+        ((2, rows, D), bf16), ((2, fp, D), bf16), ((2, fp, D // 2), bf16), ((2, mixed, D // 2), bf16)
     ]
     scratch = [
-        ((D, 4 * WIDTH), bf16), ((WIDTH, D), bf16), ((2, D, fp), bf16), ((fp, D), bf16),
+        ((D, 4 * WIDTH), bf16), ((WIDTH, D), bf16), ((2, fp, D), bf16), ((fp, D), bf16),
         ((total, HEAD), f32), ((total, HEAD), f32), ((total, D), bf16), ((rows, D), bf16),
     ]
     scratch += [(a.shape, a.dtype) for a in saved[0]]
@@ -1183,10 +1183,10 @@
         ((total, 4 * WIDTH), bf16),
         ((3, rows, D), bf16), ((2, rows, D), bf16), ((2, rows // 2, D), bf16), ((rows, D), f32),
         ((2, rows, D), bf16),
-        ((2, D, fp), bf16), ((2, fp, D // 2), bf16), ((2, mixed, D // 2), bf16),
-        ((D, fp), bf16), ((fp, D // 2), bf16), ((mixed, D // 2), bf16),
-        ((D, fp), bf16), ((ff, D // 2), bf16), ((mixed, D // 2), bf16),
-        ((D, fp), bf16), ((ff, D // 2), bf16), ((mixed, D // 2), bf16),
+        ((2, fp, D), bf16), ((2, fp, D // 2), bf16), ((2, mixed, D // 2), bf16),
+        ((fp, D), bf16), ((fp, D // 2), bf16), ((mixed, D // 2), bf16),
+        ((ff, D), bf16), ((ff, D // 2), bf16), ((mixed, D // 2), bf16),
+        ((ff, D), bf16), ((ff, D // 2), bf16), ((mixed, D // 2), bf16),
     ]
     count = 2 * PIECES
     dma = pltpu.SemaphoreType.DMA
@@ -1212,6 +1212,60 @@
     )(cotangent, y0, tokens, cos2, sin2, scal, *flat, *kept)
 
 
+def widen_kernel(section, fi, fo, mix, mix_out, both0, both1, g_in, g_fi, g_out, g_fo, outputs):
+    for n in range(4):
+        lanes = slice((n % 2) * WIDTH, (n % 2 + 1) * WIDTH)
+        g_in[:, n, :] = mix[n // 2, :, lanes].astype(f32)
+    for n in range(2):
+        half = slice(n * (D // 2), (n + 1) * (D // 2))
+        g_fi[n] = fi[n].astype(f32)
+        g_out[:, half] = mix_out[n].astype(f32)
+        g_fo[:, half] = fo[n].astype(f32)
+
+    @pl.when(section[0] == 0)
+    def _():
+        outputs[...] = both0[...]
+
+    @pl.when(section[0] != 0)
+    def _():
+        outputs[...] = both1[...]
+
+
+def widen(s, g_fi, g_fo, g_mix, both0, both1, ff):
+    cuts = 4
+    rows = both0.shape[1]
+    n = D // cuts
+    ahead = D // (WIDTH // cuts)
+    shapes = ((D, 4, WIDTH), (2, ff, D), (WIDTH, D), (ff, D))
+    per_row = lambda *shape: pl.BlockSpec(shape, lambda i, _: (i,) + (0,) * (len(shape) - 1))
+    halves = lambda *shape: pl.BlockSpec(shape, lambda i, _: (0, i, 0))
+    return pl.pallas_call(
+        widen_kernel,
+        out_shape=tuple(jax.ShapeDtypeStruct(a, f32) for a in shapes)
+        + (jax.ShapeDtypeStruct(both0.shape, bf16),),
+        grid_spec=pltpu.PrefetchScalarGridSpec(
+            num_scalar_prefetch=1,
+            grid=(cuts,),
+            in_specs=[
+                halves(2, ff // cuts, D),
+                halves(2, ff // cuts, D // 2),
+                halves(2, n, D // 2),
+                pl.BlockSpec((2, WIDTH // cuts, D // 2), lambda i, _: (0, ahead + i, 0)),
+                halves(2, rows // cuts, D),
+                halves(2, rows // cuts, D),
+            ],
+            out_specs=(
+                per_row(n, 4, WIDTH), halves(2, ff // cuts, D), per_row(WIDTH // cuts, D),
+                per_row(ff // cuts, D),
+                halves(2, rows // cuts, D),
+            ),
+        ),
+        compiler_params=pltpu.CompilerParams(vmem_limit_bytes=VMEM_BYTES),
+        cost_estimate=pl.CostEstimate(flops=0, bytes_accessed=24 << 20, transcendentals=0),
+        name="widen",
+    )(s.reshape(1), g_fi, g_fo, g_mix, g_mix, both0, both1)
+
+
 def angle_tables(starts, blocks):
     d = lax.axis_index("dp")
     at = jnp.arange(starts.shape[0], dtype=jnp.int32)
@@ -1240,29 +1294,25 @@
     rows = tokens.shape[1]
     blocks = 4 * rows // BLOCK
     ff = feed_out.shape[1]
-    fp = -(-ff // 256) * 256
     wi = mixer_in[0].reshape(D, 4 * WIDTH)
-    wfi = jnp.pad(jnp.swapaxes(feed_in[0], 0, 1), ((0, 0), (0, 0), (0, fp - ff)))
+    wfi = jnp.transpose(feed_in[0], (1, 2, 0))
     mine = (wi, mixer_out[0], wfi, feed_out[0])
     other_rates = swap(decay_rate[0])
     rates = (mine_first(s, decay_rate[0], other_rates), mine_first(s, other_rates, decay_rate[0]))
     starts = lax.dynamic_index_in_dim(block_starts, s, 0, keepdims=False)
     cos2, sin2 = angle_tables(starts, blocks)
-    scal = [scalar_table(starts, r, dp, blocks) for r in rates]
-
-    both0, *out0 = layer_forward(0, True, tokens, mine, cos2, sin2, scal[0], dp, 1)
+    scal = jnp.concatenate([row for r in rates for row in scalar_table(starts, r, dp, blocks)])
+
+    both0, *out0 = layer_forward(0, True, tokens, mine, cos2, sin2, scal, dp, 1)
     weights0, y0, saved0 = out0[:4], out0[4], out0[5:]
-    both1, *out1 = layer_forward(1, False, y0, mine, cos2, sin2, scal[1], dp, 2)
+    both1, *out1 = layer_forward(1, False, y0, mine, cos2, sin2, scal, dp, 2)
     weights1, saved1 = out1[:4], out1[5:]
     in_grads, g_fi, g_fo, g_mix = layers_backward(
-        cotangent, y0, tokens, cos2, sin2, jnp.concatenate(scal), (weights0, weights1),
+        cotangent, y0, tokens, cos2, sin2, scal, (weights0, weights1),
         (saved0, saved1), dp, ff, 3,
     )
-    outputs = mine_first(s, both0, both1)
-    g_in = jnp.concatenate([g_mix[0, :D], g_mix[1, :D]], axis=1).astype(f32).reshape(D, 4, WIDTH)
-    g_out = jnp.concatenate([g_mix[0, D:], g_mix[1, D:]], axis=1).astype(f32)
-    g_feed_in = jnp.swapaxes(g_fi[:, :, :ff], 0, 1).astype(f32)
-    g_feed_out = jnp.concatenate([g_fo[0, :ff], g_fo[1, :ff]], axis=1).astype(f32)
+    g_in, g_feed_in, g_out, g_feed_out, outputs = widen(s, g_fi, g_fo, g_mix, both0, both1, ff)
+    g_feed_in = jnp.transpose(g_feed_in, (2, 0, 1))
     return outputs[None], in_grads[None], g_in[None], g_out[None], g_feed_in[None], g_feed_out[None]
 
 

time: 409 us -> 367 us (0.90)
  local copies, waits for them, and re-layouts: 24.3 us -> 5.81 us
  other arithmetic: 17.5 us -> 4.54 us
  Pallas kernels: 366 us -> 356 us
    pallas_call x2, Pallas kernels: 132 us -> 121 us  [layer_forward(): pl.pallas_call(functools.partial(forward_kernel, dp, layer, first), out_s...]
    unnamed x14 -> x6, local copies, waits for them, and re-layouts: 14 us -> 4.31 us
    pallas_call x0 -> x1, Pallas kernels: none -> 9.71 us  [widen(): pl.pallas_call(widen_kernel, out_shape=tuple((jax.ShapeDtypeStruct(a, f32...]
    pallas_call x1, Pallas kernels: 233 us -> 225 us  [layers_backward(): pl.pallas_call(functools.partial(backward_kernel, dp), out_shape=tuple((j...]
    convert_element_type x3 -> x0, other arithmetic: 6.96 us -> none  [the longest x1 3.9 us: shards(): jnp.concatenate([g_mix[0, :D], g_mix[1, :D]], axis=1).astype(f32)]
    broadcast_in_dim x2 -> x0, other arithmetic: 6 us -> none  [the longest x1 5.04 us: shards(): g_feed_in[None]]
    slice x3 -> x0, local copies, waits for them, and re-layouts: 4.98 us -> none  [the longest x1 1.77 us: shards(): g_out = jnp.concatenate([g_mix[0, D:], g_mix[1, D:]], axis=1).astype(f32)]
  transfers between devices with their start and end apart: 1 -> 1, of which waited for: 0 -> 0; matrix products, arithmetic and copies ran while one was open for 3% -> 2% of each run, Pallas kernels for 0% -> 0%
where the time goes in v4:
time: 367 us
  Pallas kernels  356 us (97%)
  local copies, waits for them, and re-layouts  5.81 us (2%)
  other arithmetic  4.54 us (1%)
    pallas_call x1, Pallas kernels, layers_backward(): pl.pallas_call(functools.partial(backward_kernel, dp), out_shape=tuple((j...  225 us
    pallas_call x2, Pallas kernels, layer_forward(): pl.pallas_call(functools.partial(forward_kernel, dp, layer, first), out_s...  121 us
    pallas_call x1, Pallas kernels, widen(): pl.pallas_call(widen_kernel, out_shape=tuple((jax.ShapeDtypeStruct(a, f32...  9.71 us
  transfers between devices with their start and end apart: 1, of which 0 were waited for; matrix products, arithmetic and copies ran while one was open for 2% of the time, Pallas kernels for 0%

profile of v4, /device:TPU:0, one launch (start us, length us, event | category | flops | bytes accessed | tf_op | source)
XLA Modules:
  0.0 367.2 jit_solution(16922907437953773178)
XLA Ops:
  0.6 0.5 collective-permute-start
  1.1 0.7 subtract_reduce_fusion
  1.8 0.7 compare_bitcast_fusion
  2.6 0.1 select_reduce_fusion
  2.7 0.1 sub.16
  2.8 0.1 reduce_prod.27
  3.0 0.1 add_convert_fusion
  3.1 3.4 copy.18
  6.6 2.5 fusion
  9.2 0.1 select_reduce_fusion.1
  9.3 0.1 copy.15
  9.4 0.1 select_n.95
  9.5 0.1 copy.14
  9.6 0.1 select_n.93
  9.7 0.1 copy.16
  9.8 0.1 select_n.99
  9.9 0.1 copy.17
  10.0 0.1 select_n.101
  10.1 0.6 concatenate.3.scal
  10.7 61.4 %layer_forward.2 = (bf16[2,192,1024]{2,1,0:T(8,128)(2,1)}, bf16[1024,1024]{1,0:T(8,128)(2,1)}, bf16[256,1024]{1,0:T(8,128)(2,1)}, bf16[2,768,1024]{2,1,0:T(8,128...) custom-call(bf16[2,192,1024]{2,1,0:T(8,128)(2,1)} %tok_in.1, ...), custom_call_target="tpu_custom_call" | custom-call | flops 6845104128 | bytes 20971520 | tf_op jit(solution)/shard_map/layer_forward/pallas_call | solution.py:606
  72.0 59.3 %layer_forward.3 = (bf16[2,192,1024]{2,1,0:T(8,128)(2,1)}, bf16[1024,1024]{1,0:T(8,128)(2,1)}, bf16[256,1024]{1,0:T(8,128)(2,1)}, bf16[2,768,1024]{2,1,0:T(8,128...) custom-call(bf16[192,1024]{1,0:T(8,128)(2,1)} %get-tuple-element.54., ...), custom_call_target="tpu_custom_call" | custom-call | flops 6845104128 | bytes 20971520 | tf_op jit(solution)/shard_map/layer_forward/pallas_call | solution.py:606
  131.4 225.2 %layers_backward.1 = (bf16[2,192,1024]{2,1,0:T(8,128)(2,1)}, bf16[2,768,1024]{2,1,0:T(8,128)(2,1)}, bf16[2,768,512]{2,1,0:T(8,128)(2,1)}, bf16[2,1280,512]{2,1,0:T(8,128)(2,1)}) custom-call(bf16[2,192,1024]{2,1,0:T(8,128)(2,1)} %ct_in.1, bf16[192,1024]{1,0:T(8,128)(2,1)} %get-tuple-element.54.x_in.y0_in, bf16[2,192,1024]{2,1,0:T(8,128)(2,1)} %tok_in.1, ...), custom_call_target="tpu_custom_call" | custom-call | flops 22548578304 | bytes 62914560 | tf_op jit(solution)/shard_map/layers_backward/pallas_call | solution.py:1196
  356.6 9.7 %widen.1 = (f32[1024,4,256]{2,1,0:T(4,128)}, f32[2,704,1024]{2,1,0:T(8,128)}, f32[256,1024]{1,0:T(8,128)}, f32[704,1024]{1,0:T(8,128)}, bf16[2,192,1024]{2,1,0:T(8,128)(2,1)}) custom-call(s32[1]{0:T(128)} %bitcast.section, bf16[2,768,1024]{2,1,0:T(8,128)(2,1)} %get-tuple-element.91.fi, bf16[2,768,512]{2,1,0:T(8,128)(2,1)} %get-tuple-element.92.fo, ...), custom_call_target="tpu_custom_call" | custom-call | bytes 25165824 | tf_op jit(solution)/shard_map/widen/pallas_call | solution.py:1242
  366.3 0.9 copy.20
  (17 shorter events, 0.3 us)
Async XLA Ops:
  0.6 8.4 %collective-permute-start = (f32[2]{0:T(128)}, f32[2]{0:T(128)S(1)}, u32[]{:S(2)}, u32[]{:S(2)}) collective-permute-start(f32[2]{0:T(128)} %bitcast.30), channel_id=1, source_target_pairs={{0,16},{16,0},{1,17},{17,1},{2,18},{18,2},{3,19},{19,3},{4,20},{20... | collective-permute-start | bytes 32 | tf_op jit(solution)/shard_map/ppermute | solution.py:1284
  3.1 6.0 %copy-start.1 = (f32[1,2]{1,0:T(1,128)S(1)}, f32[1,2]{1,0:T(1,128)}, u32[]{:S(2)}) copy-start(f32[1,2]{1,0:T(1,128)} %param.14) | copy-start | bytes 28
  356.6 9.7 %copy-start = (bf16[2,192,1024]{2,1,0:T(8,128)(2,1)S(1)}, bf16[2,192,1024]{2,1,0:T(8,128)(2,1)}, u32[]{:S(2)}) copy-start(bf16[2,192,1024]{2,1,0:T(8,128)(2,1)} %get-tuple-element.97) | copy-start | bytes 2359300

commit v5 on v4

--- a/solution.py
+++ b/solution.py
@@ -2,6 +2,7 @@
 
 import jax
 import jax.numpy as jnp
+import numpy as np
 from jax import lax
 from jax.experimental import pallas as pl
 from jax.experimental.pallas import tpu as pltpu
@@ -207,7 +208,12 @@
     forward = jnp.where((at < d)[:, None], through, 0.0)
     backward = jnp.where((at > d)[:, None], through, 0.0)
     mine = lax.dynamic_index_in_dim(survive, d, 0, keepdims=False)
-    return [mine, rates, decay, forward.reshape(-1), backward.reshape(-1)]
+    index = jnp.arange(starts.shape[0], dtype=jnp.int32)
+    begins = jnp.max(
+        jnp.where((index[None, :] <= index[:, None]) & (starts > 0)[None, :], index[None, :], 0), axis=1
+    )
+    offsets = lax.dynamic_slice_in_dim((index - begins) * BLOCK, d * blocks, blocks).astype(f32)
+    return [mine, rates, decay, forward.reshape(-1), backward.reshape(-1), offsets]
 
 
 def decay_fill(scal, base, nb, mask, mask_t, qd, kd):
@@ -320,10 +326,10 @@
 
 
 def forward_kernel(
-    dp, layer, first, x_in, my_wi, my_wo, my_wfi, my_wfo, cos2, sin2, scal,
-    both_o, wi_o, wo_o, wfi_o, wfo_o, y_out, hidden_o, zq_o, zk_o, gate_o, q_o, k_o, v_o, att_o, sc_o, states_o, branch_o, mid_o,
+    dp, layer, first, x_in, my_wi, my_wo, my_wfi, my_wfo, turn_in, scal,
+    both_o, turn_o, wi_o, wo_o, wfi_o, wfo_o, y_out, hidden_o, zq_o, zk_o, gate_o, q_o, k_o, v_o, att_o, sc_o, states_o, branch_o, mid_o,
     hid2_o, pair_o,
-    wi, wo, wfi, wfo, cosv, sinv, xf, hidden, zq, zk, gate, q, k, v, att, sc, states, branch, mid, hid2,
+    raw, wi, wo, wfi, wfo, turn, xf, hidden, zq, zk, gate, q, k, v, att, sc, states, branch, mid, hid2,
     pair, mask, qd, kd, loc, zout, zin, run, u, y, part, got, via, ssq, own, yb,
     lsem, ssem, rsem, zs, zr, wl, ws, wr,
 ):
@@ -331,7 +337,7 @@
     rows = x_in.shape[-2]
     total = 4 * rows
     nb = total // BLOCK
-    at = layer * (nb + 4 + 4 * dp)
+    at = layer * (2 * nb + 4 + 4 * dp)
     local = Sems(lsem)
 
     def load(src, dst):
@@ -344,7 +350,7 @@
     owner = s == layer
     ff = my_wfo.shape[0]
     pairs = (
-        (my_wi, wi), (my_wo, wo.at[rows_of(t, WIDTH)]), (my_wfi, wfi.at[:, pl.ds(0, ff)]),
+        (wi, wi), (my_wo, wo.at[rows_of(t, WIDTH)]), (my_wfi, wfi.at[:, pl.ds(0, ff)]),
         (my_wfo, wfo.at[pl.ds(0, ff)]),
     )
     got_w = [
@@ -352,8 +358,9 @@
         for n, (src, dst) in enumerate(pairs)
     ]
     got_wi, got_wo, got_wfi, got_wfo = got_w
-    got_wi.read()
-    got_cos, got_sin = load(cos2, cosv), load(sin2, sinv)
+    got_raw = pltpu.make_async_copy(my_wi, raw, wl.at[0])
+    pl.when(owner)(lambda: got_raw.start())
+    got_turn = load(turn_in, turn.at[0, pl.ds(0, 8)] if first else turn)
     for fetch in got_w[1:]:
         fetch.read()
     wfi[:, ff:, :] = jnp.zeros_like(wfi[:, ff:, :])
@@ -377,12 +384,39 @@
         return remote(ref, ref, ws.at[10 + k], wr.at[10 + k], (1 - s, d, t))
 
     gx.start()
-    for fetch in got_w:
+    for fetch in got_w[1:]:
         fetch.send()
+
+    @pl.when(owner)
+    def _():
+        got_raw.wait()
+
+        def chunk(n, c):
+            r = rows_of(n, 128)
+            wi[r, :] = raw[r].reshape(128, 4 * WIDTH)
+            return c
+
+        lax.fori_loop(0, D // 128, chunk, 0)
+        got_wi.far().start()
+
+    got_turn.wait()
+    stores = []
+    if first:
+        frequency = turn[0, 0:1, :]
+        sign = jnp.where(lax.broadcasted_iota(jnp.int32, (1, HEAD), 1) < HEAD // 2, -1.0, 1.0)
+
+        def angles(b, c):
+            steps_in = lax.broadcasted_iota(jnp.int32, (BLOCK, HEAD), 0).astype(f32)
+            angle = (scal[at + nb + 4 + 4 * dp + b] + steps_in) * frequency
+            r = rows_of(b, BLOCK)
+            turn[0, r, :] = jnp.cos(angle)
+            turn[1, r, :] = sign * jnp.sin(angle)
+            return c
+
+        lax.fori_loop(0, nb, angles, 0)
+        stores.append(load(turn, turn_o))
     decay_fill(scal, at, nb, mask, None, qd, kd)
-    got_wi.wait()
-    got_cos.wait()
-    got_sin.wait()
+    pl.when(jnp.logical_not(owner))(lambda: got_wi.far().wait_recv())
 
     def project(i, c):
         for n in (1, 2, 3):
@@ -403,7 +437,7 @@
         xv = xf[r, :].astype(f32)
         hid = (xv * rms_scale(xv)).astype(bf16)
         hidden[r, :] = hid
-        cs, sn = cosv[r, :], sinv[r, :]
+        cs, sn = turn[0, r, :], turn[1, r, :]
         for n, (pre, post) in enumerate(((zq, q), (zk, k))):
             z = nn(hid, wi[:, n * WIDTH : (n + 1) * WIDTH])
             pre[r, :] = z
@@ -417,7 +451,7 @@
 
     lax.fori_loop(0, 4, project, 0)
 
-    stores = [load(hidden, hidden_o), load(zq, zq_o), load(zk, zk_o), load(gate, gate_o)]
+    stores += [load(hidden, hidden_o), load(zq, zq_o), load(zk, zk_o), load(gate, gate_o)]
     stores += [load(q, q_o), load(k, k_o), load(v, v_o)]
 
     def local_state(b, c):
@@ -573,7 +607,7 @@
         copy.wait()
 
 
-def layer_forward(layer, first, x, weights, cos2, sin2, scal, dp, uid):
+def layer_forward(layer, first, x, weights, turn, scal, dp, uid):
     rows = x.shape[-2]
     total = 4 * rows
     nb = total // BLOCK
@@ -586,12 +620,13 @@
         ((total, D), bf16), ((2, total, fp), bf16),
     ]
     scratch = [
-        ((D, 4 * WIDTH), bf16), ((D, D), bf16), ((2, fp, D), bf16), ((fp, D), bf16),
-        ((total, HEAD), f32), ((total, HEAD), f32), ((total, D), bf16),
+        ((D, 4, WIDTH), bf16), ((D, 4 * WIDTH), bf16), ((D, D), bf16), ((2, fp, D), bf16), ((fp, D), bf16),
+        ((2, total, HEAD), f32), ((total, D), bf16),
     ]
     scratch += saved[1:]
     saved = [
-        ((2, rows, D), bf16), ((D, 4 * WIDTH), bf16), ((WIDTH, D), bf16), ((2, fp, D), bf16),
+        ((2, rows, D), bf16), ((2, total, HEAD) if first else (8, 128), f32),
+        ((D, 4 * WIDTH), bf16), ((WIDTH, D), bf16), ((2, fp, D), bf16),
         ((fp, D), bf16),
     ] + saved
     scratch += [
@@ -606,7 +641,7 @@
     return pl.pallas_call(
         functools.partial(forward_kernel, dp, layer, first),
         out_shape=tuple(jax.ShapeDtypeStruct(a, b) for a, b in saved),
-        in_specs=[ANY] * 7 + [SMEM],
+        in_specs=[ANY] * 6 + [SMEM],
         out_specs=(ANY,) * len(saved),
         scratch_shapes=[pltpu.VMEM(a, b) for a, b in scratch]
         + [
@@ -624,7 +659,7 @@
         ),
         cost_estimate=pl.CostEstimate(flops=flops, bytes_accessed=20 << 20, transcendentals=0),
         name="layer_forward",
-    )(x, *weights, cos2, sin2, scal)
+    )(x, *weights, turn, scal)
 
 
 class CorePair:
@@ -652,7 +687,7 @@
 
 class LineSum:
     LAG = 2
-    END = 4 * LAG
+    END = 5 * LAG
 
     def __init__(self, dp, where, owner, halves, first, size, land, fin, result, sems, before):
         self.dp, self.where, self.owner, self.before = dp, where, owner, before
@@ -830,13 +865,13 @@
 
 
 def backward_kernel(
-    dp, ct_in, y0_in, tok_in, cos2, sin2, scal,
+    dp, ct_in, y0_in, tok_in, turn_in, scal,
     wi0, wo0, wfi0, wfo0, wi1, wo1, wfi1, wfo1, *refs,
 ):
     saved_i = (refs[0:14], refs[14:28])
     both_o, gwfi_o, gwfo_o, gmix_o = refs[28:32]
     (
-        wi, wo, wfi, wfo, cosv, sinv, gf, xr, hidden, zq, zk, gate, q, k, v, att, sc, states, branch, mid,
+        wi, wo, wfi, wfo, turn, gf, xr, hidden, zq, zk, gate, q, k, v, att, sc, states, branch, mid,
         hid2, pair, mask, mask_t, qd, kd, terms, zout, zin, run, gpair, prod, gb, gm, dv, dk,
         gp, part, got, via, own, gr, gwfi, gwfo, gmix, c_fi, c_fo, c_mix, l_fi, l_fo, l_mix,
         f_fi, f_fo, f_mix, lsem, ssem, rsem, zs, zr, ol, os, or_, core_s, core_r, ls, lr, free,
@@ -847,7 +882,7 @@
     nb = total // BLOCK
     fp = wfo.shape[0]
     half = rows // 2
-    table = nb + 4 + 4 * dp
+    table = 2 * nb + 4 + 4 * dp
     local = Sems(lsem)
     me = rows_of(t, rows)
     gated, gatt = slice(0, WIDTH), slice(WIDTH, 2 * WIDTH)
@@ -893,7 +928,7 @@
     pieces, pairs = {}, {}
     for layer in (1, 0):
         cuts = [(gwfo, 256 * n, min(256, ff - 256 * n), l_fo, f_fo, gwfo_o) for n in range(-(-ff // 256))]
-        cuts += [(gwfi, 128 * n, min(128, ff - 128 * n), l_fi, f_fi, gwfi_o) for n in range(-(-ff // 128))]
+        cuts += [(gwfi, 96 * n, min(96, ff - 96 * n), l_fi, f_fi, gwfi_o) for n in range(-(-ff // 96))]
         cuts += [(gmix, 256 * n, 256, l_mix, f_mix, gmix_o) for n in range((D + WIDTH) // 256)]
         made = []
         for n, cut in enumerate(cuts):
@@ -907,12 +942,12 @@
             CorePair(where, halves, landed, core_s.at[3 * layer + n], core_r.at[3 * layer + n])
             for n, (halves, landed) in enumerate(((gwfo, c_fo), (gwfi, c_fi), (gmix, c_mix)))
         ]
-    n_out, n_feed = -(-ff // 256), -(-ff // 256) + -(-ff // 128)
+    n_out, n_feed = -(-ff // 256), -(-ff // 256) + -(-ff // 96)
     work = Background()
     tick = work.tick
 
     got_g = load(ct_in.at[s], gf.at[me])
-    in_feed, in_tables = load_feed(1), [load(cos2, cosv), load(sin2, sinv)]
+    in_feed, in_tables = load_feed(1), [load(turn_in, turn)]
     in_gates, in_attn, in_ends = load_gates(1), load_attn(1), load_ends(1)
     entry(dp, s, d, t, core=True)
     got_g.wait()
@@ -925,9 +960,6 @@
         gg = Gather(block_of(gf), half, ssem, rsem, base, where)
         gg.start()
         decay_fill(scal, offset, nb, mask, mask_t, qd, kd)
-        if layer == 0:
-            pairs[1][2].add()
-            work.put(pieces[1][n_feed:])
         tick()
         for copy in in_feed:
             copy.wait()
@@ -940,8 +972,7 @@
                 def _(n=n):
                     if n == 1:
                         gg.forward()
-                    if n == 3:
-                        tick()
+                    tick()
                     gg.ready(n)
 
             r = rows_of(partner(t, i), rows)
@@ -965,6 +996,7 @@
             return c
 
         lax.fori_loop(0, 4, feed, 0)
+        tick()
 
         def feed_weights(n, c):
             cols = rows_of(n, 256)
@@ -1013,8 +1045,7 @@
                 def _(n=n):
                     if n == 1:
                         gbg.forward()
-                    if n == 3:
-                        tick()
+                    tick()
                     gbg.ready(n)
 
             r = rows_of(partner(t, i), rows)
@@ -1030,6 +1061,7 @@
             return c
 
         lax.fori_loop(0, 4, gating, 0)
+        tick()
         if layer == 1:
             in_gates = load_gates(0)
         for copy in in_attn:
@@ -1056,7 +1088,7 @@
         tick()
 
         def unturn(pre, grad, r, h):
-            back = grad * cosv[r, :] - pltpu.roll(grad, HEAD // 2, 1) * sinv[r, :]
+            back = grad * turn[0, r, :] - pltpu.roll(grad, HEAD // 2, 1) * turn[1, r, :]
             z = pre[r, head(h)]
             g = sig(z)
             return (back * (g * (1.0 + z * (1.0 - g)))).astype(bf16)
@@ -1134,6 +1166,9 @@
         gmix[1, D:, :] = tn(prod[:, gated], gb[:, D // 2 :]).astype(bf16)
         pair_mix.send()
         ins.combine()
+        tick()
+        pair_mix.add()
+        work.put(pieces[layer][n_feed:])
         tick()
         dx = gm[...] + norm_back(xr[...].astype(f32), own[...] + ins.result())
         gr[layer] = dx.astype(bf16)
@@ -1150,8 +1185,6 @@
             gf[me, :] = gr[layer]
             in_ends = load_ends(0)
 
-    pairs[0][2].add()
-    work.put(pieces[0][n_feed:])
     work.until(pieces[0], LineSum.END)
     for piece in pieces[0]:
         piece.close()
@@ -1159,7 +1192,7 @@
         finish()
 
 
-def layers_backward(cotangent, y0, tokens, cos2, sin2, scal, weights, saved, dp, ff, uid):
+def layers_backward(cotangent, y0, tokens, turn, scal, weights, saved, dp, ff, uid):
     rows = y0.shape[-2]
     total = 4 * rows
     nb = total // BLOCK
@@ -1170,7 +1203,7 @@
     ]
     scratch = [
         ((D, 4 * WIDTH), bf16), ((WIDTH, D), bf16), ((2, fp, D), bf16), ((fp, D), bf16),
-        ((total, HEAD), f32), ((total, HEAD), f32), ((total, D), bf16), ((rows, D), bf16),
+        ((2, total, HEAD), f32), ((total, D), bf16), ((rows, D), bf16),
     ]
     scratch += [(a.shape, a.dtype) for a in saved[0]]
     scratch += [
@@ -1196,7 +1229,7 @@
     return pl.pallas_call(
         functools.partial(backward_kernel, dp),
         out_shape=tuple(jax.ShapeDtypeStruct(a, b) for a, b in outs),
-        in_specs=[ANY] * 5 + [SMEM] + [ANY] * (len(flat) + len(kept)),
+        in_specs=[ANY] * 4 + [SMEM] + [ANY] * (len(flat) + len(kept)),
         out_specs=(ANY,) * len(outs),
         scratch_shapes=[pltpu.VMEM(a, b) for a, b in scratch]
         + [
@@ -1209,7 +1242,7 @@
         ),
         cost_estimate=pl.CostEstimate(flops=flops, bytes_accessed=60 << 20, transcendentals=0),
         name="layers_backward",
-    )(cotangent, y0, tokens, cos2, sin2, scal, *flat, *kept)
+    )(cotangent, y0, tokens, turn, scal, *flat, *kept)
 
 
 def widen_kernel(section, fi, fo, mix, mix_out, both0, both1, g_in, g_fi, g_out, g_fo, outputs):
@@ -1266,18 +1299,10 @@
     )(s.reshape(1), g_fi, g_fo, g_mix, g_mix, both0, both1)
 
 
-def angle_tables(starts, blocks):
-    d = lax.axis_index("dp")
-    at = jnp.arange(starts.shape[0], dtype=jnp.int32)
-    begins = jnp.max(
-        jnp.where((at[None, :] <= at[:, None]) & (starts > 0)[None, :], at[None, :], 0), axis=1
-    )
-    offsets = lax.dynamic_slice_in_dim((at - begins) * BLOCK, d * blocks, blocks)
-    places = (offsets[:, None] + jnp.arange(BLOCK, dtype=jnp.int32)[None, :]).reshape(-1)
-    lane = jnp.arange(HEAD, dtype=jnp.int32)
-    frequency = 10000.0 ** (-(lane % (HEAD // 2)).astype(f32) / (HEAD // 2))
-    angles = places.astype(f32)[:, None] * frequency[None, :]
-    return jnp.cos(angles), jnp.where(lane < HEAD // 2, -1.0, 1.0)[None, :] * jnp.sin(angles)
+def frequencies():
+    lane = np.arange(HEAD) % (HEAD // 2)
+    row = np.float32(10000.0) ** (-lane.astype(np.float32) / np.float32(HEAD // 2))
+    return np.broadcast_to(row.astype(np.float32), (8, HEAD))
 
 
 def swap(x):
@@ -1294,21 +1319,19 @@
     rows = tokens.shape[1]
     blocks = 4 * rows // BLOCK
     ff = feed_out.shape[1]
-    wi = mixer_in[0].reshape(D, 4 * WIDTH)
     wfi = jnp.transpose(feed_in[0], (1, 2, 0))
-    mine = (wi, mixer_out[0], wfi, feed_out[0])
+    mine = (mixer_in[0], mixer_out[0], wfi, feed_out[0])
     other_rates = swap(decay_rate[0])
     rates = (mine_first(s, decay_rate[0], other_rates), mine_first(s, other_rates, decay_rate[0]))
     starts = lax.dynamic_index_in_dim(block_starts, s, 0, keepdims=False)
-    cos2, sin2 = angle_tables(starts, blocks)
     scal = jnp.concatenate([row for r in rates for row in scalar_table(starts, r, dp, blocks)])
 
-    both0, *out0 = layer_forward(0, True, tokens, mine, cos2, sin2, scal, dp, 1)
-    weights0, y0, saved0 = out0[:4], out0[4], out0[5:]
-    both1, *out1 = layer_forward(1, False, y0, mine, cos2, sin2, scal, dp, 2)
-    weights1, saved1 = out1[:4], out1[5:]
+    both0, *out0 = layer_forward(0, True, tokens, mine, frequencies(), scal, dp, 1)
+    turn, weights0, y0, saved0 = out0[0], out0[1:5], out0[5], out0[6:]
+    both1, *out1 = layer_forward(1, False, y0, mine, turn, scal, dp, 2)
+    weights1, saved1 = out1[1:5], out1[6:]
     in_grads, g_fi, g_fo, g_mix = layers_backward(
-        cotangent, y0, tokens, cos2, sin2, scal, (weights0, weights1),
+        cotangent, y0, tokens, turn, scal, (weights0, weights1),
         (saved0, saved1), dp, ff, 3,
     )
     g_in, g_feed_in, g_out, g_feed_out, outputs = widen(s, g_fi, g_fo, g_mix, both0, both1, ff)

time: 367 us -> 358 us (0.975)
  Pallas kernels: 356 us -> 350 us
    pallas_call x1, Pallas kernels: 225 us -> 219 us  [layers_backward(): pl.pallas_call(functools.partial(backward_kernel, dp), out_shape=tuple((j...]
  transfers between devices with their start and end apart: 1 -> 1, of which waited for: 0 -> 0; matrix products, arithmetic and copies ran while one was open for 2% -> 1% of each run, Pallas kernels for 0% -> 0%
where the time goes in v5:
time: 358 us; the launch traced here: 357 us
  Pallas kernels  350 us (98%)
    pallas_call x1, Pallas kernels, layers_backward(): pl.pallas_call(functools.partial(backward_kernel, dp), out_shape=tuple((j...  219 us
    pallas_call x2, Pallas kernels, layer_forward(): pl.pallas_call(functools.partial(forward_kernel, dp, layer, first), out_s...  121 us
    pallas_call x1, Pallas kernels, widen(): pl.pallas_call(widen_kernel, out_shape=tuple((jax.ShapeDtypeStruct(a, f32...  9.71 us
  transfers between devices with their start and end apart: 1, of which 0 were waited for; matrix products, arithmetic and copies ran while one was open for 1% of the time, Pallas kernels for 0%

profile of v5, /device:TPU:0, one launch (start us, length us, event | category | flops | bytes accessed | tf_op | source)
XLA Modules:
  0.0 357.4 jit_solution(3072123115760910988)
XLA Ops:
  0.6 0.5 collective-permute-start
  1.1 0.7 compare_bitcast_fusion
  1.8 0.7 subtract_reduce_fusion
  2.6 0.1 select_reduce_fusion
  2.7 0.1 sub.16
  2.8 0.1 reduce_prod.27
  2.9 0.1 dynamic-slice_convert_fusion
  3.0 0.7 multiply_exponential_fusion
  3.8 0.2 select_reduce_fusion.1
  4.0 0.1 copy.16
  4.1 0.1 select_n.74
  4.2 0.1 copy.15
  4.2 0.1 select_n.72
  4.3 0.1 copy.17
  4.4 0.1 select_n.80
  4.5 0.1 copy.18
  4.6 0.1 select_n.82
  4.7 0.6 concatenate.3.scal
  5.3 1.2 jit_solution_.3.turn_in
  6.5 61.4 %layer_forward.2 = (bf16[2,192,1024]{2,1,0:T(8,128)(2,1)}, f32[2,768,128]{2,1,0:T(8,128)}, bf16[1024,1024]{1,0:T(8,128)(2,1)}, bf16[256,1024]{1,0:T(8,128)(2,1)}...) custom-call(bf16[2,192,1024]{2,1,0:T(8,128)(2,1)} %tok_in.1, ...), custom_call_target="tpu_custom_call" | custom-call | flops 6845104128 | bytes 20971520 | tf_op jit(solution)/shard_map/layer_forward/pallas_call | solution.py:641
  67.9 59.8 %layer_forward.3 = (bf16[2,192,1024]{2,1,0:T(8,128)(2,1)}, f32[8,128]{1,0:T(8,128)}, bf16[1024,1024]{1,0:T(8,128)(2,1)}, bf16[256,1024]{1,0:T(8,128)(2,1)}, bf16...) custom-call(bf16[192,1024]{1,0:T(8,128)(2,1)} %get-tuple-element.55., ...), custom_call_target="tpu_custom_call" | custom-call | flops 6845104128 | bytes 20971520 | tf_op jit(solution)/shard_map/layer_forward/pallas_call | solution.py:641
  127.7 219.0 %layers_backward.1 = (bf16[2,192,1024]{2,1,0:T(8,128)(2,1)}, bf16[2,768,1024]{2,1,0:T(8,128)(2,1)}, bf16[2,768,512]{2,1,0:T(8,128)(2,1)}, bf16[2,1280,512]{2,1,0:T(8,128)(2,1)}) custom-call(bf16[2,192,1024]{2,1,0:T(8,128)(2,1)} %ct_in.1, bf16[192,1024]{1,0:T(8,128)(2,1)} %get-tuple-element.55.x_in.y0_in, bf16[2,192,1024]{2,1,0:T(8,128)(2,1)} %tok_in.1, ...), custom_call_target="tpu_custom_call" | custom-call | flops 22548578304 | bytes 62914560 | tf_op jit(solution)/shard_map/layers_backward/pallas_call | solution.py:1229
  346.8 9.7 %widen.1 = (f32[1024,4,256]{2,1,0:T(4,128)}, f32[2,704,1024]{2,1,0:T(8,128)}, f32[256,1024]{1,0:T(8,128)}, f32[704,1024]{1,0:T(8,128)}, bf16[2,192,1024]{2,1,0:T(8,128)(2,1)}) custom-call(s32[1]{0:T(128)} %bitcast.section, bf16[2,768,1024]{2,1,0:T(8,128)(2,1)} %get-tuple-element.93.fi, bf16[2,768,512]{2,1,0:T(8,128)(2,1)} %get-tuple-element.94.fo, ...), custom_call_target="tpu_custom_call" | custom-call | bytes 25165824 | tf_op jit(solution)/shard_map/widen/pallas_call | solution.py:1275
  356.5 0.9 copy.20
  (11 shorter events, 0.2 us)
Async XLA Ops:
  0.6 2.4 collective-permute-start
  346.8 9.7 %copy-start = (bf16[2,192,1024]{2,1,0:T(8,128)(2,1)S(1)}, bf16[2,192,1024]{2,1,0:T(8,128)(2,1)}, u32[]{:S(2)}) copy-start(bf16[2,192,1024]{2,1,0:T(8,128)(2,1)} %get-tuple-element.99) | copy-start | bytes 2359300

commit v6 on v5

--- a/solution.py
+++ b/solution.py
@@ -280,27 +280,6 @@
     lax.fori_loop(0, dp, each, 0)
 
 
-class Fetch:
-    def __init__(self, src, dst, owner, where, lsem, ssem, rsem):
-        s, d, t = where
-        self.owner = owner
-        self.local = lambda: pltpu.make_async_copy(src, dst, lsem)
-        self.far = lambda: remote(src, dst, ssem, rsem, (1 - s, d, t))
-
-    def read(self):
-        pl.when(self.owner)(lambda: self.local().start())
-
-    def send(self):
-        pl.when(self.owner)(lambda: self.far().start())
-
-    def wait(self):
-        pl.when(self.owner)(lambda: self.local().wait())
-        pl.when(jnp.logical_not(self.owner))(lambda: self.far().wait_recv())
-
-    def drain(self):
-        pl.when(self.owner)(lambda: self.far().wait_send())
-
-
 def to_owner(owner, where, src, own_dst, far_dst, lsem, ssem, rsem):
     s, d, t = where
 
@@ -326,340 +305,366 @@
 
 
 def forward_kernel(
-    dp, layer, first, x_in, my_wi, my_wo, my_wfi, my_wfo, turn_in, scal,
-    both_o, turn_o, wi_o, wo_o, wfi_o, wfo_o, y_out, hidden_o, zq_o, zk_o, gate_o, q_o, k_o, v_o, att_o, sc_o, states_o, branch_o, mid_o,
-    hid2_o, pair_o,
-    raw, wi, wo, wfi, wfo, turn, xf, hidden, zq, zk, gate, q, k, v, att, sc, states, branch, mid, hid2,
-    pair, mask, qd, kd, loc, zout, zin, run, u, y, part, got, via, ssq, own, yb,
-    lsem, ssem, rsem, zs, zr, wl, ws, wr,
+    dp, tok_in, ct_in, my_wi, my_wo, my_wfi, my_wfo, turn_in, scal,
+    both0_o, both1_o, turn_o, gf_o, y_out, *refs,
 ):
+    outs = (refs[0:18], refs[18:36])
+    (
+        raw, wi2, wo2, wfi2, wfo2, turn, gf, xf, hidden, zq, zk, gate, q, k, v, att, sc, states, branch, mid,
+        hid2, pair, mask, qd, kd, loc, zout2, zin2, run, u, y, part, got, via, ssq, own, yb2,
+        lsem, ssem, rsem, zs2, zr2, wl, ws, wr,
+    ) = refs[36:]
     where = s, d, t = place()
-    rows = x_in.shape[-2]
+    rows = tok_in.shape[-2]
     total = 4 * rows
     nb = total // BLOCK
-    at = layer * (2 * nb + 4 + 4 * dp)
     local = Sems(lsem)
+    me = rows_of(t, rows)
 
     def load(src, dst):
         copy = pltpu.make_async_copy(src, dst, local.take())
         copy.start()
         return copy
 
-    x_src = x_in.at[s] if first else x_in
-    got_x = load(x_src, xf.at[rows_of(t, rows)])
-    owner = s == layer
+    got_x = load(tok_in.at[s], xf.at[me])
+    got_raw = load(my_wi, raw)
+    got_turn = load(turn_in, turn.at[0, pl.ds(0, 8)])
+    got_ct = load(ct_in.at[s], gf.at[me])
     ff = my_wfo.shape[0]
     pairs = (
-        (wi, wi), (my_wo, wo.at[rows_of(t, WIDTH)]), (my_wfi, wfi.at[:, pl.ds(0, ff)]),
-        (my_wfo, wfo.at[pl.ds(0, ff)]),
+        (wi2.at[s], wi2.at[s]), (my_wo, wo2.at[s, rows_of(t, WIDTH)]),
+        (my_wfi, wfi2.at[s, :, pl.ds(0, ff)]), (my_wfo, wfo2.at[s, pl.ds(0, ff)]),
     )
-    got_w = [
-        Fetch(src, dst, owner, where, wl.at[n], ws.at[n], wr.at[n])
-        for n, (src, dst) in enumerate(pairs)
-    ]
-    got_wi, got_wo, got_wfi, got_wfo = got_w
-    got_raw = pltpu.make_async_copy(my_wi, raw, wl.at[0])
-    pl.when(owner)(lambda: got_raw.start())
-    got_turn = load(turn_in, turn.at[0, pl.ds(0, 8)] if first else turn)
-    for fetch in got_w[1:]:
-        fetch.read()
-    wfi[:, ff:, :] = jnp.zeros_like(wfi[:, ff:, :])
-    wfo[ff:, :] = jnp.zeros_like(wfo[ff:, :])
+
+    def mine(n):
+        return pltpu.make_async_copy(*pairs[n], wl.at[n])
+
+    def over(n):
+        return remote(*pairs[n], ws.at[n], wr.at[n], (1 - s, d, t))
+
+    def await_weight(n, owner):
+        if n > 0:
+            pl.when(owner)(lambda: mine(n).wait())
+        pl.when(jnp.logical_not(owner))(lambda: over(n).wait_recv())
+
+    for n in (1, 2, 3):
+        mine(n).start()
+    wfi2[:, :, ff:, :] = jnp.zeros_like(wfi2[:, :, ff:, :])
+    wfo2[:, ff:, :] = jnp.zeros_like(wfo2[:, ff:, :])
     entry(dp, s, d, t, core=True)
     got_x.wait()
-
+    got_ct.wait()
     half = rows // 2
-    gx = Gather(
-        lambda p, h: xf.at[pl.ds(pl.multiple_of(p * rows + h * half, half), half)],
-        half, ssem, rsem, 0, where,
-    )
+
+    def block_of(ref):
+        return lambda p, h: ref.at[pl.ds(pl.multiple_of(p * rows + h * half, half), half)]
+
+    gg = Gather(block_of(gf), half, ssem, rsem, 42, where)
     quarter = WIDTH // 2
     gw = Gather(
-        lambda p, h: wo.at[pl.ds(pl.multiple_of(p * WIDTH + h * quarter, quarter), quarter)],
+        lambda p, h: wo2.at[s, pl.ds(pl.multiple_of(p * WIDTH + h * quarter, quarter), quarter)],
         quarter, ws, wr, 4, where,
     )
 
-    def wo_over(k):
-        ref = wo.at[rows_of(partner(t, k), WIDTH)]
+    def wo_over(k, slot):
+        ref = wo2.at[slot, rows_of(partner(t, k), WIDTH)]
         return remote(ref, ref, ws.at[10 + k], wr.at[10 + k], (1 - s, d, t))
 
-    gx.start()
-    for fetch in got_w[1:]:
-        fetch.send()
-
-    @pl.when(owner)
-    def _():
-        got_raw.wait()
-
-        def chunk(n, c):
-            r = rows_of(n, 128)
-            wi[r, :] = raw[r].reshape(128, 4 * WIDTH)
-            return c
-
-        lax.fori_loop(0, D // 128, chunk, 0)
-        got_wi.far().start()
-
-    got_turn.wait()
-    stores = []
-    if first:
-        frequency = turn[0, 0:1, :]
-        sign = jnp.where(lax.broadcasted_iota(jnp.int32, (1, HEAD), 1) < HEAD // 2, -1.0, 1.0)
-
-        def angles(b, c):
-            steps_in = lax.broadcasted_iota(jnp.int32, (BLOCK, HEAD), 0).astype(f32)
-            angle = (scal[at + nb + 4 + 4 * dp + b] + steps_in) * frequency
+    stores, finishes = [], []
+    for layer in (0, 1):
+        (
+            wi_o, wo_o, wfi_o, wfo_o, hidden_o, zq_o, zk_o, gate_o, q_o, k_o, v_o, att_o, sc_o, states_o,
+            branch_o, mid_o, hid2_o, pair_o,
+        ) = outs[layer]
+        wi, wo, wfi, wfo = wi2.at[layer], wo2.at[layer], wfi2.at[layer], wfo2.at[layer]
+        zout, zin, zs, zr = zout2.at[layer], zin2.at[layer], zs2.at[layer], zr2.at[layer]
+        yb = yb2.at[layer]
+        both_o = (both0_o, both1_o)[layer]
+        owner = s == layer
+        at = layer * (2 * nb + 4 + 4 * dp)
+        base = 21 * layer
+        gx = Gather(block_of(xf), half, ssem, rsem, base, where)
+        gx.start()
+        if layer == 0:
+            for n in (1, 2, 3):
+                over(n).start()
+            got_raw.wait()
+
+            def chunk(n, c):
+                r = rows_of(n, 128)
+                wi2[s, r, :] = raw[r].reshape(128, 4 * WIDTH)
+                return c
+
+            lax.fori_loop(0, D // 128, chunk, 0)
+            over(0).start()
+            got_turn.wait()
+            frequency = turn[0, 0:1, :]
+            sign = jnp.where(lax.broadcasted_iota(jnp.int32, (1, HEAD), 1) < HEAD // 2, -1.0, 1.0)
+
+            def angles(b, c):
+                steps_in = lax.broadcasted_iota(jnp.int32, (BLOCK, HEAD), 0).astype(f32)
+                angle = (scal[at + nb + 4 + 4 * dp + b] + steps_in) * frequency
+                r = rows_of(b, BLOCK)
+                turn[0, r, :] = jnp.cos(angle)
+                turn[1, r, :] = sign * jnp.sin(angle)
+                return c
+
+            lax.fori_loop(0, nb, angles, 0)
+            stores.append(load(turn, turn_o))
+        decay_fill(scal, at, nb, mask, None, qd, kd)
+        await_weight(0, owner)
+        if layer == 1:
+            for copy in stores:
+                copy.wait()
+            stores = []
+
+        def project(i, c):
+            for n in (1, 2, 3):
+
+                @pl.when(i == n)
+                def _(n=n):
+                    if n == 1:
+                        gx.forward()
+
+                        @pl.when(owner)
+                        def _():
+                            mine(1).wait()
+                            gw.start()
+
+                    gx.ready(n)
+
+            r = rows_of(partner(t, i), rows)
+            xv = xf[r, :].astype(f32)
+            hid = (xv * rms_scale(xv)).astype(bf16)
+            hidden[r, :] = hid
+            cs, sn = turn[0, r, :], turn[1, r, :]
+            for n, (pre, post) in enumerate(((zq, q), (zk, k))):
+                z = nn(hid, wi[:, n * WIDTH : (n + 1) * WIDTH])
+                pre[r, :] = z
+                a = z * sig(z)
+                for h in range(HEADS_HERE):
+                    ah = a[:, head(h)]
+                    post[r, head(h)] = (ah * cs + pltpu.roll(ah, HEAD // 2, 1) * sn).astype(bf16)
+            v[r, :] = nn(hid, wi[:, 2 * WIDTH : 3 * WIDTH]).astype(bf16)
+            gate[r, :] = nn(hid, wi[:, 3 * WIDTH :])
+            return c
+
+        lax.fori_loop(0, 4, project, 0)
+
+        stores += [load(hidden, hidden_o), load(zq, zq_o), load(zk, zk_o), load(gate, gate_o)]
+        stores += [load(q, q_o), load(k, k_o), load(v, v_o)]
+
+        def local_state(b, c):
             r = rows_of(b, BLOCK)
-            turn[0, r, :] = jnp.cos(angle)
-            turn[1, r, :] = sign * jnp.sin(angle)
-            return c
-
-        lax.fori_loop(0, nb, angles, 0)
-        stores.append(load(turn, turn_o))
-    decay_fill(scal, at, nb, mask, None, qd, kd)
-    pl.when(jnp.logical_not(owner))(lambda: got_wi.far().wait_recv())
-
-    def project(i, c):
-        for n in (1, 2, 3):
-
-            @pl.when(i == n)
-            def _(n=n):
-                if n == 1:
-                    gx.forward()
-
-                    @pl.when(owner)
-                    def _():
-                        got_wo.local().wait()
-                        gw.start()
-
-                gx.ready(n)
-
-        r = rows_of(partner(t, i), rows)
-        xv = xf[r, :].astype(f32)
-        hid = (xv * rms_scale(xv)).astype(bf16)
-        hidden[r, :] = hid
-        cs, sn = turn[0, r, :], turn[1, r, :]
-        for n, (pre, post) in enumerate(((zq, q), (zk, k))):
-            z = nn(hid, wi[:, n * WIDTH : (n + 1) * WIDTH])
-            pre[r, :] = z
-            a = z * sig(z)
             for h in range(HEADS_HERE):
-                ah = a[:, head(h)]
-                post[r, head(h)] = (ah * cs + pltpu.roll(ah, HEAD // 2, 1) * sn).astype(bf16)
-        v[r, :] = nn(hid, wi[:, 2 * WIDTH : 3 * WIDTH]).astype(bf16)
-        gate[r, :] = nn(hid, wi[:, 3 * WIDTH :])
-        return c
-
-    lax.fori_loop(0, 4, project, 0)
-
-    stores += [load(hidden, hidden_o), load(zq, zq_o), load(zk, zk_o), load(gate, gate_o)]
-    stores += [load(q, q_o), load(k, k_o), load(v, v_o)]
-
-    def local_state(b, c):
-        r = rows_of(b, BLOCK)
+                kdec = (k[r, head(h)].astype(f32) * kd[h]).astype(bf16)
+                loc[b, h] = tn(kdec, v[r, head(h)])
+            return c
+
+        lax.fori_loop(0, nb, local_state, 0)
+        pl.when(owner)(gw.forward)
+        if layer == 1:
+            gg.forward()
         for h in range(HEADS_HERE):
-            kdec = (k[r, head(h)].astype(f32) * kd[h]).astype(bf16)
-            loc[b, h] = tn(kdec, v[r, head(h)])
-        return c
-
-    lax.fori_loop(0, nb, local_state, 0)
-    pl.when(owner)(gw.forward)
-    for h in range(HEADS_HERE):
-        carried = loc[0, h]
-        for b in range(1, nb):
-            carried = (scal[at + nb + 2 + h] * scal[at + b]) * carried + loc[b, h]
-        zout[h] = carried.astype(bf16)
-    send_states(dp, where, zout, zin, zs, zr, True)
-
-    def inner(b, c):
-        r = rows_of(b, BLOCK)
-        for h in range(HEADS_HERE):
-            w = (nt(q[r, head(h)], k[r, head(h)]) * mask[h]).astype(bf16)
-            att[r, head(h)] = nn(w, v[r, head(h)])
-        return c
-
-    lax.fori_loop(0, nb, inner, 0)
-    take_states(dp, where, zout, zin, zs, zr, True, scal, at + nb + 4, run)
-
-    def outer(b, c):
-        r = rows_of(b, BLOCK)
-        for h in range(HEADS_HERE):
-            entering = scal[at + b] * run[h]
-            states[b, h] = entering
-            run[h] = scal[at + nb + 2 + h] * entering + loc[b, h]
-            qdec = (q[r, head(h)].astype(f32) * qd[h]).astype(bf16)
-            a = att[r, head(h)] + nn(qdec, entering.astype(bf16))
-            att[r, head(h)] = a
-            u[t, r, head(h)] = (a * gate[r, head(h)]).astype(bf16)
-        return c
-
-    lax.fori_loop(0, nb, outer, 0)
-
-    hu = total // 2
-    gu = Gather(lambda p, h: u.at[p, pl.ds(h * hu, hu)], hu, ssem, rsem, 6, where)
-    gu.start()
-    for b in range(nb):
-        a = att[b * BLOCK : (b + 1) * BLOCK, :]
-        ssq[0, :, b * BLOCK : (b + 1) * BLOCK] = lax.dot_general(
-            jnp.ones((8, WIDTH), f32), a * a, (((1,), (1,)), ((), ())),
-            preferred_element_type=f32, precision=lax.Precision.HIGHEST,
+            carried = loc[0, h]
+            for b in range(1, nb):
+                carried = (scal[at + nb + 2 + h] * scal[at + b]) * carried + loc[b, h]
+            zout[h] = carried.astype(bf16)
+        send_states(dp, where, zout, zin, zs, zr, True)
+
+        def inner(b, c):
+            r = rows_of(b, BLOCK)
+            for h in range(HEADS_HERE):
+                w = (nt(q[r, head(h)], k[r, head(h)]) * mask[h]).astype(bf16)
+                att[r, head(h)] = nn(w, v[r, head(h)])
+            return c
+
+        lax.fori_loop(0, nb, inner, 0)
+        take_states(dp, where, zout, zin, zs, zr, True, scal, at + nb + 4, run)
+
+        def outer(b, c):
+            r = rows_of(b, BLOCK)
+            for h in range(HEADS_HERE):
+                entering = scal[at + b] * run[h]
+                states[b, h] = entering
+                run[h] = scal[at + nb + 2 + h] * entering + loc[b, h]
+                qdec = (q[r, head(h)].astype(f32) * qd[h]).astype(bf16)
+                a = att[r, head(h)] + nn(qdec, entering.astype(bf16))
+                att[r, head(h)] = a
+                u[t, r, head(h)] = (a * gate[r, head(h)]).astype(bf16)
+            return c
+
+        lax.fori_loop(0, nb, outer, 0)
+
+        hu = total // 2
+        gu = Gather(lambda p, h: u.at[p, pl.ds(h * hu, hu)], hu, ssem, rsem, base + 6, where)
+        gu.start()
+        for b in range(nb):
+            a = att[b * BLOCK : (b + 1) * BLOCK, :]
+            ssq[0, :, b * BLOCK : (b + 1) * BLOCK] = lax.dot_general(
+                jnp.ones((8, WIDTH), f32), a * a, (((1,), (1,)), ((), ())),
+                preferred_element_type=f32, precision=lax.Precision.HIGHEST,
+            )
+        sums = [
+            remote(
+                ssq.at[0], ssq.at[n], ssem.at[base + 11 + n], rsem.at[base + 11 + n], (s, d, partner(t, n))
+            )
+            for n in (1, 2, 3)
+        ]
+        for copy in sums:
+            copy.start()
+        stores += [load(att, att_o), load(states, states_o)]
+
+        @pl.when(owner)
+        def _():
+            for n in (1, 2, 3):
+                gw.ready(n)
+                wo_over(n, layer).start()
+
+        @pl.when(jnp.logical_not(owner))
+        def _():
+            over(1).wait_recv()
+            for n in (1, 2, 3):
+                wo_over(n, layer).wait_recv()
+
+        y[...] = jnp.zeros_like(y)
+
+        def out_project(i, c):
+            for n in (1, 2, 3):
+
+                @pl.when(i == n)
+                def _(n=n):
+                    if n == 1:
+                        gu.forward()
+                        gg.mine(layer).start()
+                        gg.mine(3 - layer).start()
+                    gu.ready(n)
+
+            p = partner(t, i)
+
+            def chunk(m, c):
+                r = rows_of(m, rows)
+                y[r, :] += nn(u[p, r, :], wo[rows_of(p, WIDTH), :])
+                return c
+
+            return lax.fori_loop(0, 4, chunk, c)
+
+        lax.fori_loop(0, 4, out_project, 0)
+        for copy in sums:
+            copy.wait_recv()
+        whole = ssq[0] + ssq[1] + ssq[2] + ssq[3]
+        sc[...] = jnp.transpose(lax.rsqrt(whole * (1.0 / D) + norm_eps))
+        await_weight(2, owner)
+        await_weight(3, owner)
+        out = Scatter(part, got, via, rows, ssem, rsem, base + 15, where)
+
+        def feed(i, c):
+            e = 3 - i
+            r = rows_of(partner(t, e), rows)
+            br = sc[r, 0:1] * y[r, :]
+            m = xf[r, :].astype(f32) + br
+            h2 = (m * rms_scale(m)).astype(bf16)
+            hid2[r, :] = h2
+            p0, p1 = nt(h2, wfi[0]), nt(h2, wfi[1])
+            pair[0, r, :] = p0.astype(bf16)
+            pair[1, r, :] = p1.astype(bf16)
+            o = nn((p0 * p1).astype(bf16), wfo[...])
+            for n in (1, 2, 3):
+
+                @pl.when(e == n)
+                def _(n=n):
+                    out.put(n, o)
+
+            @pl.when(e == 0)
+            def _():
+                branch[...] = br.astype(bf16)
+                mid[...] = m
+                own[...] = o + m
+
+            return c
+
+        lax.fori_loop(0, 4, feed, 0)
+        stores += [load(sc, sc_o), load(branch, branch_o), load(mid, mid_o), load(hid2, hid2_o)]
+        stores += [load(pair, pair_o), load(wi, wi_o), load(wo, wo_o)]
+        stores += [load(wfi, wfi_o), load(wfo, wfo_o)]
+        gx.drain()
+        gu.drain()
+        for copy in sums:
+            copy.wait_send()
+        out.combine()
+        yv = (own[...] + out.result()).astype(bf16)
+        yb[...] = yv
+        out.drain()
+        sent_states(dp, where, zout, zin, zs, zr, True)
+        start, finish = to_owner(
+            owner, where, yb, both_o.at[s], both_o.at[s], wl.at[4 + layer], ws.at[14 + layer],
+            wr.at[14 + layer],
         )
-    sums = [
-        remote(ssq.at[0], ssq.at[n], ssem.at[11 + n], rsem.at[11 + n], (s, d, partner(t, n)))
-        for n in (1, 2, 3)
-    ]
-    for copy in sums:
-        copy.start()
-    stores += [load(att, att_o), load(states, states_o)]
-    @pl.when(owner)
-    def _():
-        for n in (1, 2, 3):
-            gw.ready(n)
-            wo_over(n).start()
-
-    @pl.when(jnp.logical_not(owner))
-    def _():
-        got_wo.far().wait_recv()
-        for n in (1, 2, 3):
-            wo_over(n).wait_recv()
-
-    y[...] = jnp.zeros_like(y)
-
-    def out_project(i, c):
-        for n in (1, 2, 3):
-
-            @pl.when(i == n)
-            def _(n=n):
-                if n == 1:
-                    gu.forward()
-                gu.ready(n)
-
-        p = partner(t, i)
-
-        def chunk(m, c):
-            r = rows_of(m, rows)
-            y[r, :] += nn(u[p, r, :], wo[rows_of(p, WIDTH), :])
-            return c
-
-        return lax.fori_loop(0, 4, chunk, c)
-
-    lax.fori_loop(0, 4, out_project, 0)
-    for copy in sums:
-        copy.wait_recv()
-    whole = ssq[0] + ssq[1] + ssq[2] + ssq[3]
-    sc[...] = jnp.transpose(lax.rsqrt(whole * (1.0 / D) + norm_eps))
-    got_wfi.wait()
-    got_wfo.wait()
-    out = Scatter(part, got, via, rows, ssem, rsem, 15, where)
-
-    def feed(i, c):
-        e = 3 - i
-        r = rows_of(partner(t, e), rows)
-        br = sc[r, 0:1] * y[r, :]
-        branch[r, :] = br.astype(bf16)
-        m = xf[r, :].astype(f32) + br
-        h2 = (m * rms_scale(m)).astype(bf16)
-        hid2[r, :] = h2
-        p0, p1 = nt(h2, wfi[0]), nt(h2, wfi[1])
-        pair[0, r, :] = p0.astype(bf16)
-        pair[1, r, :] = p1.astype(bf16)
-        o = nn((p0 * p1).astype(bf16), wfo[...])
-        for n in (1, 2, 3):
-
-            @pl.when(e == n)
-            def _(n=n):
-                out.put(n, o)
-
-        @pl.when(e == 0)
-        def _():
-            mid[...] = m
-            own[...] = o + m
-
-        return c
-
-    lax.fori_loop(0, 4, feed, 0)
-    stores += [load(sc, sc_o), load(branch, branch_o), load(mid, mid_o), load(hid2, hid2_o)]
-    stores += [load(pair, pair_o), load(wi, wi_o), load(wo.at[rows_of(t, WIDTH)], wo_o)]
-    stores += [load(wfi, wfi_o), load(wfo, wfo_o)]
-    out.combine()
-    yb[...] = (own[...] + out.result()).astype(bf16)
-    stores += [load(yb, y_out)]
-    start, finish = to_owner(
-        owner, where, yb, both_o.at[s], both_o.at[s], wl.at[4], ws.at[14], wr.at[14]
-    )
-    start()
-    for fetch in got_w:
-        fetch.drain()
-
-    @pl.when(owner)
-    def _():
-        for n in (1, 2, 3):
-            wo_over(n).wait_send()
-        gw.drain()
-
-    finish()
-    gx.drain()
-    gu.drain()
-    out.drain()
-    for copy in sums:
-        copy.wait_send()
-    sent_states(dp, where, zout, zin, zs, zr, True)
+        start()
+        finishes.append(finish)
+        if layer == 0:
+            stores.append(load(yb, y_out))
+            xf[me, :] = yv
+
+
+    for n in (1, 2, 3):
+        gg.ready(n)
+    stores.append(load(gf, gf_o))
+    for n in range(4):
+        over(n).wait_send()
+    for n in (1, 2, 3):
+        wo_over(n, s).wait_send()
+    gw.drain()
+    gg.drain()
+    for finish in finishes:
+        finish()
     for copy in stores:
         copy.wait()
 
 
-def layer_forward(layer, first, x, weights, turn, scal, dp, uid):
-    rows = x.shape[-2]
+def layers_forward(tokens, cotangent, weights, frequency, scal, dp, uid):
+    rows = tokens.shape[-2]
     total = 4 * rows
     nb = total // BLOCK
     fp = -(-weights[3].shape[0] // 256) * 256
     saved = [
-        ((rows, D), bf16), ((total, D), bf16), ((total, WIDTH), f32), ((total, WIDTH), f32),
-        ((total, WIDTH), f32), ((total, WIDTH), bf16), ((total, WIDTH), bf16),
-        ((total, WIDTH), bf16), ((total, WIDTH), f32), ((total, 8), f32),
-        ((nb, HEADS_HERE, HEAD, HEAD), f32), ((total, D), bf16), ((rows, D), f32),
+        ((total, D), bf16), ((total, WIDTH), f32), ((total, WIDTH), f32), ((total, WIDTH), f32),
+        ((total, WIDTH), bf16), ((total, WIDTH), bf16), ((total, WIDTH), bf16), ((total, WIDTH), f32),
+        ((total, 8), f32), ((nb, HEADS_HERE, HEAD, HEAD), f32), ((rows, D), bf16), ((rows, D), f32),
         ((total, D), bf16), ((2, total, fp), bf16),
     ]
-    scratch = [
-        ((D, 4, WIDTH), bf16), ((D, 4 * WIDTH), bf16), ((D, D), bf16), ((2, fp, D), bf16), ((fp, D), bf16),
-        ((2, total, HEAD), f32), ((total, D), bf16),
-    ]
-    scratch += saved[1:]
-    saved = [
-        ((2, rows, D), bf16), ((2, total, HEAD) if first else (8, 128), f32),
-        ((D, 4 * WIDTH), bf16), ((WIDTH, D), bf16), ((2, fp, D), bf16),
-        ((fp, D), bf16),
-    ] + saved
+    kept = [((D, 4 * WIDTH), bf16), ((D, D), bf16), ((2, fp, D), bf16), ((fp, D), bf16)]
+    scratch = [((D, 4, WIDTH), bf16)] + [((2,) + a, b) for a, b in kept]
+    scratch += [((2, total, HEAD), f32), ((total, D), bf16), ((total, D), bf16)] + saved
     scratch += [
         ((HEADS_HERE, BLOCK, BLOCK), f32), ((HEADS_HERE, BLOCK, HEAD), f32),
         ((HEADS_HERE, BLOCK, HEAD), f32), ((nb, HEADS_HERE, HEAD, HEAD), f32),
-        ((HEADS_HERE, HEAD, HEAD), bf16), ((dp, HEADS_HERE, HEAD, HEAD), bf16),
+        ((2, HEADS_HERE, HEAD, HEAD), bf16), ((2, dp, HEADS_HERE, HEAD, HEAD), bf16),
         ((HEADS_HERE, HEAD, HEAD), f32), ((4, total, WIDTH), bf16), ((total, D), f32),
         ((3, rows, D), bf16), ((2, rows, D), bf16), ((2, rows // 2, D), bf16),
-        ((4, 8, total), f32), ((rows, D), f32), ((rows, D), bf16),
+        ((4, 8, total), f32), ((rows, D), f32), ((2, rows, D), bf16),
     ]
-    flops = 2 * total * D * (4 * WIDTH + D + 3 * fp)
+    both = ((2, rows, D), bf16)
+    outs = [both, both, ((2, total, HEAD), f32), ((total, D), bf16), ((rows, D), bf16)]
+    outs += (kept + saved) * 2
+    dma = pltpu.SemaphoreType.DMA
+    flops = 4 * total * D * (4 * WIDTH + D + 3 * fp)
     return pl.pallas_call(
-        functools.partial(forward_kernel, dp, layer, first),
-        out_shape=tuple(jax.ShapeDtypeStruct(a, b) for a, b in saved),
-        in_specs=[ANY] * 6 + [SMEM],
-        out_specs=(ANY,) * len(saved),
+        functools.partial(forward_kernel, dp),
+        out_shape=tuple(jax.ShapeDtypeStruct(a, b) for a, b in outs),
+        in_specs=[ANY] * 7 + [SMEM],
+        out_specs=(ANY,) * len(outs),
         scratch_shapes=[pltpu.VMEM(a, b) for a, b in scratch]
         + [
-            pltpu.SemaphoreType.DMA((24,)),
-            pltpu.SemaphoreType.DMA((21,)),
-            pltpu.SemaphoreType.DMA((21,)),
-            pltpu.SemaphoreType.DMA((dp,)),
-            pltpu.SemaphoreType.DMA((dp,)),
-            pltpu.SemaphoreType.DMA((5,)),
-            pltpu.SemaphoreType.DMA((15,)),
-            pltpu.SemaphoreType.DMA((15,)),
+            dma((48,)), dma((48,)), dma((48,)), dma((2, dp)), dma((2, dp)), dma((6,)), dma((16,)),
+            dma((16,)),
         ],
         compiler_params=pltpu.CompilerParams(
             collective_id=uid, has_side_effects=True, vmem_limit_bytes=VMEM_BYTES
         ),
-        cost_estimate=pl.CostEstimate(flops=flops, bytes_accessed=20 << 20, transcendentals=0),
-        name="layer_forward",
-    )(x, *weights, turn, scal)
+        cost_estimate=pl.CostEstimate(flops=flops, bytes_accessed=60 << 20, transcendentals=0),
+        name="layers_forward",
+    )(tokens, cotangent, *weights, frequency, scal)
 
 
 class CorePair:
@@ -865,14 +870,14 @@
 
 
 def backward_kernel(
-    dp, ct_in, y0_in, tok_in, turn_in, scal,
+    dp, gf_in, y0_in, tok_in, turn_in, scal,
     wi0, wo0, wfi0, wfo0, wi1, wo1, wfi1, wfo1, *refs,
 ):
     saved_i = (refs[0:14], refs[14:28])
     both_o, gwfi_o, gwfo_o, gmix_o = refs[28:32]
     (
         wi, wo, wfi, wfo, turn, gf, xr, hidden, zq, zk, gate, q, k, v, att, sc, states, branch, mid,
-        hid2, pair, mask, mask_t, qd, kd, terms, zout, zin, run, gpair, prod, gb, gm, dv, dk,
+        hid2, pair, mask, mask_t, qd, kd, terms, zout, zin, run, gpair, prod, gb, gsend, grecv, dots, gm, dv, dk,
         gp, part, got, via, own, gr, gwfi, gwfo, gmix, c_fi, c_fo, c_mix, l_fi, l_fo, l_mix,
         f_fi, f_fo, f_mix, lsem, ssem, rsem, zs, zr, ol, os, or_, core_s, core_r, ls, lr, free,
     ) = refs[32:]
@@ -946,7 +951,7 @@
     work = Background()
     tick = work.tick
 
-    got_g = load(ct_in.at[s], gf.at[me])
+    got_g = load(gf_in, gf)
     in_feed, in_tables = load_feed(1), [load(turn_in, turn)]
     in_gates, in_attn, in_ends = load_gates(1), load_attn(1), load_ends(1)
     entry(dp, s, d, t, core=True)
@@ -956,9 +961,10 @@
     for layer in (1, 0):
         offset = table * layer
         pair_fo, pair_fi, pair_mix = pairs[layer]
-        base = 24 * layer
-        gg = Gather(block_of(gf), half, ssem, rsem, base, where)
-        gg.start()
+        base = 30 * layer
+        gg = Gather(block_of(gf), half, ssem, rsem, base, where) if layer == 0 else None
+        if gg is not None:
+            gg.start()
         decay_fill(scal, offset, nb, mask, mask_t, qd, kd)
         tick()
         for copy in in_feed:
@@ -966,7 +972,7 @@
         sums = Scatter(part, got, via, rows, ssem, rsem, base + 6, where)
 
         def feed(i, c):
-            for n in (1, 2, 3):
+            for n in (1, 2, 3) if gg is not None else ():
 
                 @pl.when(i == n)
                 def _(n=n):
@@ -1028,36 +1034,56 @@
         gm[...] = grad_middle
         gb[me, :] = grad_middle.astype(bf16)
         sums.drain()
-        gg.drain()
-
+        if gg is not None:
+            gg.drain()
+
+        for copy in in_gates:
+            copy.wait()
+        mine = gb[me, :]
+        for p in range(4):
+            gsend[p] = nt(mine, wo[p * WIDTH : (p + 1) * WIDTH, :]).astype(bf16)
+        grecv[t] = gsend[t]
+        dots[t, :, 0:rows] = lax.dot_general(
+            jnp.ones((8, D), f32), mine.astype(f32) * branch[...].astype(f32), (((1,), (1,)), ((), ())),
+            preferred_element_type=f32, precision=lax.Precision.HIGHEST,
+        ) * (1.0 / D)
+
+        def turned(k, into):
+            dev = (s, d, partner(t, k))
+            slot = partner(t, k) if into else t
+            n = base + 24 + 2 * k
+            return (
+                remote(gsend.at[partner(t, k)], grecv.at[slot], ssem.at[n - 2], rsem.at[n - 2], dev),
+                remote(dots.at[t], dots.at[slot], ssem.at[n - 1], rsem.at[n - 1], dev),
+            )
+
+        for n in (3, 1, 2):
+            for copy in turned(n, False):
+                copy.start()
         gbg = Gather(block_of(gb), half, ssem, rsem, base + 12, where)
         gbg.start()
         if layer == 1:
             in_feed = load_feed(0)
         tick()
-        for copy in in_gates:
-            copy.wait()
 
         def gating(i, c):
             for n in (1, 2, 3):
 
                 @pl.when(i == n)
                 def _(n=n):
-                    if n == 1:
-                        gbg.forward()
-                    tick()
-                    gbg.ready(n)
-
-            r = rows_of(partner(t, i), rows)
-            b = gb[r, :]
-            grad = nt(b, wo[...])
-            dots = jnp.sum(b.astype(f32) * branch[r, :].astype(f32), axis=-1, keepdims=True) * (1.0 / D)
+                    for copy in turned(n, True):
+                        copy.wait_recv()
+
+            p = partner(t, i)
+            r = rows_of(p, rows)
+            grad = grecv[p].astype(f32)
+            inner_sum = jnp.transpose(dots[p])[0:rows, 0:1]
             scale = sc[r, 0:1]
             normed = att[r, :] * scale
             gt = gate[r, :]
             gp[r, 3 * WIDTH :] = (grad * normed).astype(bf16)
             prod[r, gated] = (normed * gt).astype(bf16)
-            prod[r, gatt] = (scale * (grad * gt - normed * dots)).astype(bf16)
+            prod[r, gatt] = (scale * (grad * gt - normed * inner_sum)).astype(bf16)
             return c
 
         lax.fori_loop(0, 4, gating, 0)
@@ -1086,6 +1112,7 @@
         z_args = (dp, where, zout.at[layer], zin.at[layer], zs.at[layer], zr.at[layer], False)
         send_states(*z_args)
         tick()
+        gbg.forward()
 
         def unturn(pre, grad, r, h):
             back = grad * turn[0, r, :] - pltpu.roll(grad, HEAD // 2, 1) * turn[1, r, :]
@@ -1162,6 +1189,8 @@
             return c
 
         lax.fori_loop(0, D // 256, in_weights, 0)
+        for n in (1, 2, 3):
+            gbg.ready(n)
         gmix[0, D:, :] = tn(prod[:, gated], gb[:, : D // 2]).astype(bf16)
         gmix[1, D:, :] = tn(prod[:, gated], gb[:, D // 2 :]).astype(bf16)
         pair_mix.send()
@@ -1174,6 +1203,9 @@
         gr[layer] = dx.astype(bf16)
         ins.drain()
         gbg.drain()
+        for n in (1, 2, 3):
+            for copy in turned(n, False):
+                copy.wait_send()
         sent_states(*z_args)
         start, finish = to_owner(
             s == layer, where, gr.at[layer], both_o.at[s], both_o.at[s],
@@ -1192,7 +1224,7 @@
         finish()
 
 
-def layers_backward(cotangent, y0, tokens, turn, scal, weights, saved, dp, ff, uid):
+def layers_backward(gathered, y0, tokens, turn, scal, weights, saved, dp, ff, uid):
     rows = y0.shape[-2]
     total = 4 * rows
     nb = total // BLOCK
@@ -1202,7 +1234,7 @@
         ((2, rows, D), bf16), ((2, fp, D), bf16), ((2, fp, D // 2), bf16), ((2, mixed, D // 2), bf16)
     ]
     scratch = [
-        ((D, 4 * WIDTH), bf16), ((WIDTH, D), bf16), ((2, fp, D), bf16), ((fp, D), bf16),
+        ((D, 4 * WIDTH), bf16), ((D, D), bf16), ((2, fp, D), bf16), ((fp, D), bf16),
         ((2, total, HEAD), f32), ((total, D), bf16), ((rows, D), bf16),
     ]
     scratch += [(a.shape, a.dtype) for a in saved[0]]
@@ -1211,7 +1243,8 @@
         ((HEADS_HERE, BLOCK, HEAD), f32), ((HEADS_HERE, BLOCK, HEAD), f32),
         ((nb, HEADS_HERE, HEAD, HEAD), f32), ((2, HEADS_HERE, HEAD, HEAD), bf16),
         ((2, dp, HEADS_HERE, HEAD, HEAD), bf16), ((HEADS_HERE, HEAD, HEAD), f32),
-        ((2, total, fp), bf16), ((total, fp), bf16), ((total, D), bf16), ((rows, D), f32),
+        ((2, total, fp), bf16), ((total, fp), bf16), ((total, D), bf16), ((4, rows, WIDTH), bf16),
+        ((4, rows, WIDTH), bf16), ((4, 8, -(-rows // 128) * 128), f32), ((rows, D), f32),
         ((total, WIDTH), f32), ((total, WIDTH), f32),
         ((total, 4 * WIDTH), bf16),
         ((3, rows, D), bf16), ((2, rows, D), bf16), ((2, rows // 2, D), bf16), ((rows, D), f32),
@@ -1233,7 +1266,7 @@
         out_specs=(ANY,) * len(outs),
         scratch_shapes=[pltpu.VMEM(a, b) for a, b in scratch]
         + [
-            dma((48,)), dma((48,)), dma((48,)), dma((2, dp)), dma((2, dp)), dma((count + 2,)),
+            dma((48,)), dma((60,)), dma((60,)), dma((2, dp)), dma((2, dp)), dma((count + 2,)),
             dma((count + 2,)), dma((count + 2,)), dma((6,)), dma((6,)), dma((count, 4)),
             dma((count, 3)), pltpu.SemaphoreType.REGULAR((PIECES,)),
         ],
@@ -1242,7 +1275,7 @@
         ),
         cost_estimate=pl.CostEstimate(flops=flops, bytes_accessed=60 << 20, transcendentals=0),
         name="layers_backward",
-    )(cotangent, y0, tokens, turn, scal, *flat, *kept)
+    )(gathered, y0, tokens, turn, scal, *flat, *kept)
 
 
 def widen_kernel(section, fi, fo, mix, mix_out, both0, both1, g_in, g_fi, g_out, g_fo, outputs):
@@ -1326,13 +1359,13 @@
     starts = lax.dynamic_index_in_dim(block_starts, s, 0, keepdims=False)
     scal = jnp.concatenate([row for r in rates for row in scalar_table(starts, r, dp, blocks)])
 
-    both0, *out0 = layer_forward(0, True, tokens, mine, frequencies(), scal, dp, 1)
-    turn, weights0, y0, saved0 = out0[0], out0[1:5], out0[5], out0[6:]
-    both1, *out1 = layer_forward(1, False, y0, mine, turn, scal, dp, 2)
-    weights1, saved1 = out1[1:5], out1[6:]
+    both0, both1, turn, gf, y0, *kept = layers_forward(
+        tokens, cotangent, mine, frequencies(), scal, dp, 1
+    )
+    weights0, saved0, weights1, saved1 = kept[:4], kept[4:18], kept[18:22], kept[22:]
     in_grads, g_fi, g_fo, g_mix = layers_backward(
-        cotangent, y0, tokens, turn, scal, (weights0, weights1),
-        (saved0, saved1), dp, ff, 3,
+        gf, y0, tokens, turn, scal, (weights0, weights1),
+        (saved0, saved1), dp, ff, 2,
     )
     g_in, g_feed_in, g_out, g_feed_out, outputs = widen(s, g_fi, g_fo, g_mix, both0, both1, ff)
     g_feed_in = jnp.transpose(g_feed_in, (2, 0, 1))

time: 358 us -> 348 us (0.972)
  Pallas kernels: 350 us -> 340 us
    pallas_call x1, Pallas kernels: 219 us -> 212 us  [layers_backward(): pl.pallas_call(functools.partial(backward_kernel, dp), out_shape=tuple((j...]
    pallas_call x2 -> x1, Pallas kernels: 121 us -> 119 us  [layers_forward(): pl.pallas_call(functools.partial(forward_kernel, dp), out_shape=tuple((ja...]
where the time goes in v6:
time: 348 us
  Pallas kernels  340 us (98%)
  local copies, waits for them, and re-layouts  3.55 us (1%)
    pallas_call x1, Pallas kernels, layers_backward(): pl.pallas_call(functools.partial(backward_kernel, dp), out_shape=tuple((j...  212 us
    pallas_call x1, Pallas kernels, layers_forward(): pl.pallas_call(functools.partial(forward_kernel, dp), out_shape=tuple((ja...  119 us
    pallas_call x1, Pallas kernels, widen(): pl.pallas_call(widen_kernel, out_shape=tuple((jax.ShapeDtypeStruct(a, f32...  9.71 us
  transfers between devices with their start and end apart: 1, of which 0 were waited for; matrix products, arithmetic and copies ran while one was open for 1% of the time, Pallas kernels for 0%

profile of v6, /device:TPU:0, one launch (start us, length us, event | category | flops | bytes accessed | tf_op | source)
XLA Modules:
  0.0 347.9 jit_solution(8169227892361319548)
XLA Ops:
  0.6 0.5 collective-permute-start
  1.1 0.7 compare_bitcast_fusion
  1.8 0.7 subtract_reduce_fusion
  2.6 0.1 select_reduce_fusion
  2.7 0.1 sub.16
  2.8 0.1 reduce_prod.27
  2.9 0.1 dynamic-slice_convert_fusion
  3.0 0.1 fusion.1
  3.0 0.7 multiply_exponential_fusion
  3.8 0.2 select_reduce_fusion.1
  4.0 0.1 copy.16
  4.1 0.1 select_n.74
  4.2 0.1 copy.15
  4.2 0.1 select_n.72
  4.3 0.1 copy.17
  4.4 0.1 select_n.80
  4.5 0.1 copy.18
  4.6 0.1 select_n.82
  4.7 0.6 concatenate.3.scal
  5.3 1.2 jit_solution_.3.turn_in
  6.5 119.0 %layers_forward.1 = (bf16[2,192,1024]{2,1,0:T(8,128)(2,1)}, bf16[2,192,1024]{2,1,0:T(8,128)(2,1)}, f32[2,768,128]{2,1,0:T(8,128)}, bf16[768,1024]{1,0:T(8,128)(2...) custom-call(bf16[2,192,1024]{2,1,0:T(8,128)(2,1)} %tok_in.3, ...), custom_call_target="tpu_custom_call" | custom-call | flops 13690208256 | bytes 62914560 | tf_op jit(solution)/shard_map/layers_forward/pallas_call | solution.py:652
  125.5 211.8 %layers_backward.1 = (bf16[2,192,1024]{2,1,0:T(8,128)(2,1)}, bf16[2,768,1024]{2,1,0:T(8,128)(2,1)}, bf16[2,768,512]{2,1,0:T(8,128)(2,1)}, bf16[2,1280,512]{2,1,0:T(8,128)(2,1)}) custom-call(bf16[768,1024]{1,0:T(8,128)(2,1)} %get-tuple-element.56.gf_in, bf16[192,1024]{1,0:T(8,128)(2,1)} %get-tuple-element.57.y0_in, bf16[2,192,1024]{2,1,0:T(8,128)(2,1)} %tok_in.3, ...), custom_call_target="tpu_custom_call" | custom-call | flops 22548578304 | bytes 62914560 | tf_op jit(solution)/shard_map/layers_backward/pallas_call | solution.py:1262
  337.3 9.7 %widen.1 = (f32[1024,4,256]{2,1,0:T(4,128)}, f32[2,704,1024]{2,1,0:T(8,128)}, f32[256,1024]{1,0:T(8,128)}, f32[704,1024]{1,0:T(8,128)}, bf16[2,192,1024]{2,1,0:T(8,128)(2,1)}) custom-call(s32[1]{0:T(128)} %bitcast.section, bf16[2,768,1024]{2,1,0:T(8,128)(2,1)} %get-tuple-element.95.fi, bf16[2,768,512]{2,1,0:T(8,128)(2,1)} %get-tuple-element.96.fo, ...), custom_call_target="tpu_custom_call" | custom-call | bytes 25165824 | tf_op jit(solution)/shard_map/widen/pallas_call | solution.py:1308
  347.1 0.9 copy.20
  (10 shorter events, 0.1 us)
Async XLA Ops:
  0.6 2.4 collective-permute-start
  337.3 9.7 %copy-start = (bf16[2,192,1024]{2,1,0:T(8,128)(2,1)S(1)}, bf16[2,192,1024]{2,1,0:T(8,128)(2,1)}, u32[]{:S(2)}) copy-start(bf16[2,192,1024]{2,1,0:T(8,128)(2,1)} %get-tuple-element.101) | copy-start | bytes 2359300

commit v7 on v6

--- a/solution.py
+++ b/solution.py
@@ -971,7 +971,34 @@
             copy.wait()
         sums = Scatter(part, got, via, rows, ssem, rsem, base + 6, where)
 
+        def out_weights(n, c):
+            cols = rows_of(n, 256)
+            a = prod[:, cols]
+            gwfo[0, cols, :] = tn(a, gf[:, : D // 2]).astype(bf16)
+            gwfo[1, cols, :] = tn(a, gf[:, D // 2 :]).astype(bf16)
+            return c
+
+        if layer == 1:
+
+            def products(i, c):
+                r = rows_of(i, rows)
+                prod[r, :] = (pair[0, r, :].astype(f32) * pair[1, r, :].astype(f32)).astype(bf16)
+                return c
+
+            lax.fori_loop(0, 4, products, 0)
+            lax.fori_loop(0, fp // 256, out_weights, 0)
+            pair_fo.send()
+
         def feed(i, c):
+            for n in (1, 2, 3) if layer == 1 else ():
+
+                @pl.when(i == n)
+                def _(n=n):
+                    if n == 1:
+                        pair_fo.add()
+                        work.put(pieces[layer][:n_out])
+                    tick()
+
             for n in (1, 2, 3) if gg is not None else ():
 
                 @pl.when(i == n)
@@ -984,7 +1011,8 @@
             r = rows_of(partner(t, i), rows)
             grad = nt(gf[r, :], wfo[...])
             p0, p1 = pair[0, r, :].astype(f32), pair[1, r, :].astype(f32)
-            prod[r, :] = (p0 * p1).astype(bf16)
+            if layer == 0:
+                prod[r, :] = (p0 * p1).astype(bf16)
             g0, g1 = (grad * p1).astype(bf16), (grad * p0).astype(bf16)
             gpair[0, r, :] = g0
             gpair[1, r, :] = g1
@@ -1010,29 +1038,25 @@
                 gwfi[part_of, cols, :] = tn(gpair[part_of, :, cols], hid2[...]).astype(bf16)
             return c
 
-        def out_weights(n, c):
-            cols = rows_of(n, 256)
-            a = prod[:, cols]
-            gwfo[0, cols, :] = tn(a, gf[:, : D // 2]).astype(bf16)
-            gwfo[1, cols, :] = tn(a, gf[:, D // 2 :]).astype(bf16)
-            return c
-
         if layer == 0:
             work.until(pieces[1][:n_feed], 2 * LineSum.LAG)
-        lax.fori_loop(0, fp // 256, out_weights, 0)
-        pair_fo.send()
+            lax.fori_loop(0, fp // 256, out_weights, 0)
+            pair_fo.send()
         lax.fori_loop(0, fp // 256, feed_weights, 0)
         pair_fi.send()
         tick()
         sums.combine()
-        pair_fo.add()
-        work.put(pieces[layer][:n_out])
+        if layer == 0:
+            pair_fo.add()
+            work.put(pieces[layer][:n_out])
         tick()
         pair_fi.add()
         work.put(pieces[layer][n_out:n_feed])
+        tick()
         grad_middle = gf[me, :].astype(f32) + norm_back(mid[...], own[...] + sums.result())
         gm[...] = grad_middle
         gb[me, :] = grad_middle.astype(bf16)
+        tick()
         sums.drain()
         if gg is not None:
             gg.drain()

time: 348 us -> 340 us (0.977)
  Pallas kernels: 340 us -> 333 us
    pallas_call x1, Pallas kernels: 212 us -> 204 us  [layers_backward(): pl.pallas_call(functools.partial(backward_kernel, dp), out_shape=tuple((j...]
where the time goes in v7:
time: 340 us
  Pallas kernels  333 us (98%)
  local copies, waits for them, and re-layouts  3.55 us (1%)
    pallas_call x1, Pallas kernels, layers_backward(): pl.pallas_call(functools.partial(backward_kernel, dp), out_shape=tuple((j...  204 us
    pallas_call x1, Pallas kernels, layers_forward(): pl.pallas_call(functools.partial(forward_kernel, dp), out_shape=tuple((ja...  119 us
    pallas_call x1, Pallas kernels, widen(): pl.pallas_call(widen_kernel, out_shape=tuple((jax.ShapeDtypeStruct(a, f32...  9.71 us
  transfers between devices with their start and end apart: 1, of which 0 were waited for; matrix products, arithmetic and copies ran while one was open for 1% of the time, Pallas kernels for 0%

profile of v7, /device:TPU:0, one launch (start us, length us, event | category | flops | bytes accessed | tf_op | source)
XLA Modules:
  0.0 340.1 jit_solution(3457374187513501591)
XLA Ops:
  0.6 0.5 collective-permute-start
  1.1 0.7 compare_bitcast_fusion
  1.8 0.7 subtract_reduce_fusion
  2.6 0.1 select_reduce_fusion
  2.7 0.1 sub.16
  2.8 0.1 reduce_prod.27
  2.9 0.1 dynamic-slice_convert_fusion
  3.0 0.1 fusion.1
  3.0 0.7 multiply_exponential_fusion
  3.8 0.2 select_reduce_fusion.1
  4.0 0.1 copy.16
  4.1 0.1 select_n.74
  4.2 0.1 copy.15
  4.2 0.1 select_n.72
  4.3 0.1 copy.17
  4.4 0.1 select_n.80
  4.5 0.1 copy.18
  4.6 0.1 select_n.82
  4.7 0.6 concatenate.3.scal
  5.3 1.2 jit_solution_.3.turn_in
  6.5 119.0 %layers_forward.1 = (bf16[2,192,1024]{2,1,0:T(8,128)(2,1)}, bf16[2,192,1024]{2,1,0:T(8,128)(2,1)}, f32[2,768,128]{2,1,0:T(8,128)}, bf16[768,1024]{1,0:T(8,128)(2...) custom-call(bf16[2,192,1024]{2,1,0:T(8,128)(2,1)} %tok_in.3, ...), custom_call_target="tpu_custom_call" | custom-call | flops 13690208256 | bytes 62914560 | tf_op jit(solution)/shard_map/layers_forward/pallas_call | solution.py:652
  125.5 204.0 %layers_backward.1 = (bf16[2,192,1024]{2,1,0:T(8,128)(2,1)}, bf16[2,768,1024]{2,1,0:T(8,128)(2,1)}, bf16[2,768,512]{2,1,0:T(8,128)(2,1)}, bf16[2,1280,512]{2,1,0:T(8,128)(2,1)}) custom-call(bf16[768,1024]{1,0:T(8,128)(2,1)} %get-tuple-element.56.gf_in, bf16[192,1024]{1,0:T(8,128)(2,1)} %get-tuple-element.57.y0_in, bf16[2,192,1024]{2,1,0:T(8,128)(2,1)} %tok_in.3, ...), custom_call_target="tpu_custom_call" | custom-call | flops 22548578304 | bytes 62914560 | tf_op jit(solution)/shard_map/layers_backward/pallas_call | solution.py:1286
  329.6 9.7 %widen.1 = (f32[1024,4,256]{2,1,0:T(4,128)}, f32[2,704,1024]{2,1,0:T(8,128)}, f32[256,1024]{1,0:T(8,128)}, f32[704,1024]{1,0:T(8,128)}, bf16[2,192,1024]{2,1,0:T(8,128)(2,1)}) custom-call(s32[1]{0:T(128)} %bitcast.section, bf16[2,768,1024]{2,1,0:T(8,128)(2,1)} %get-tuple-element.95.fi, bf16[2,768,512]{2,1,0:T(8,128)(2,1)} %get-tuple-element.96.fo, ...), custom_call_target="tpu_custom_call" | custom-call | bytes 25165824 | tf_op jit(solution)/shard_map/widen/pallas_call | solution.py:1332
  339.3 0.9 copy.20
  (10 shorter events, 0.1 us)
Async XLA Ops:
  0.6 2.4 collective-permute-start
  329.5 9.7 %copy-start = (bf16[2,192,1024]{2,1,0:T(8,128)(2,1)S(1)}, bf16[2,192,1024]{2,1,0:T(8,128)(2,1)}, u32[]{:S(2)}) copy-start(bf16[2,192,1024]{2,1,0:T(8,128)(2,1)} %get-tuple-element.101) | copy-start | bytes 2359300

commit v8 on v7

--- a/solution.py
+++ b/solution.py
@@ -305,7 +305,7 @@
 
 
 def forward_kernel(
-    dp, tok_in, ct_in, my_wi, my_wo, my_wfi, my_wfo, turn_in, scal,
+    dp, tok_in, ct_in, my_wi, my_wo, my_wfi, my_wfo, scal,
     both0_o, both1_o, turn_o, gf_o, y_out, *refs,
 ):
     outs = (refs[0:18], refs[18:36])
@@ -328,7 +328,6 @@
 
     got_x = load(tok_in.at[s], xf.at[me])
     got_raw = load(my_wi, raw)
-    got_turn = load(turn_in, turn.at[0, pl.ds(0, 8)])
     got_ct = load(ct_in.at[s], gf.at[me])
     ff = my_wfo.shape[0]
     pairs = (
@@ -397,9 +396,12 @@
 
             lax.fori_loop(0, D // 128, chunk, 0)
             over(0).start()
-            got_turn.wait()
-            frequency = turn[0, 0:1, :]
-            sign = jnp.where(lax.broadcasted_iota(jnp.int32, (1, HEAD), 1) < HEAD // 2, -1.0, 1.0)
+            lane = lax.broadcasted_iota(jnp.int32, (1, HEAD), 1)
+            sign = jnp.where(lane < HEAD // 2, -1.0, 1.0)
+            frequency = jnp.zeros((1, HEAD), f32)
+            for n in range(HEAD // 2):
+                value = scal[2 * (2 * nb + 4 + 4 * dp) + n]
+                frequency = jnp.where(lax.rem(lane, HEAD // 2) == n, value, frequency)
 
             def angles(b, c):
                 steps_in = lax.broadcasted_iota(jnp.int32, (BLOCK, HEAD), 0).astype(f32)
@@ -622,7 +624,7 @@
         copy.wait()
 
 
-def layers_forward(tokens, cotangent, weights, frequency, scal, dp, uid):
+def layers_forward(tokens, cotangent, weights, scal, dp, uid):
     rows = tokens.shape[-2]
     total = 4 * rows
     nb = total // BLOCK
@@ -652,7 +654,7 @@
     return pl.pallas_call(
         functools.partial(forward_kernel, dp),
         out_shape=tuple(jax.ShapeDtypeStruct(a, b) for a, b in outs),
-        in_specs=[ANY] * 7 + [SMEM],
+        in_specs=[ANY] * 6 + [SMEM],
         out_specs=(ANY,) * len(outs),
         scratch_shapes=[pltpu.VMEM(a, b) for a, b in scratch]
         + [
@@ -664,7 +666,7 @@
         ),
         cost_estimate=pl.CostEstimate(flops=flops, bytes_accessed=60 << 20, transcendentals=0),
         name="layers_forward",
-    )(tokens, cotangent, *weights, frequency, scal)
+    )(tokens, cotangent, *weights, scal)
 
 
 class CorePair:
@@ -1322,7 +1324,7 @@
 
 
 def widen(s, g_fi, g_fo, g_mix, both0, both1, ff):
-    cuts = 4
+    cuts = 2
     rows = both0.shape[1]
     n = D // cuts
     ahead = D // (WIDTH // cuts)
@@ -1359,7 +1361,7 @@
 def frequencies():
     lane = np.arange(HEAD) % (HEAD // 2)
     row = np.float32(10000.0) ** (-lane.astype(np.float32) / np.float32(HEAD // 2))
-    return np.broadcast_to(row.astype(np.float32), (8, HEAD))
+    return row[: HEAD // 2].astype(np.float32)
 
 
 def swap(x):
@@ -1381,10 +1383,10 @@
     other_rates = swap(decay_rate[0])
     rates = (mine_first(s, decay_rate[0], other_rates), mine_first(s, other_rates, decay_rate[0]))
     starts = lax.dynamic_index_in_dim(block_starts, s, 0, keepdims=False)
-    scal = jnp.concatenate([row for r in rates for row in scalar_table(starts, r, dp, blocks)])
+    scal = jnp.concatenate([row for r in rates for row in scalar_table(starts, r, dp, blocks)] + [frequencies()])
 
     both0, both1, turn, gf, y0, *kept = layers_forward(
-        tokens, cotangent, mine, frequencies(), scal, dp, 1
+        tokens, cotangent, mine, scal, dp, 1
     )
     weights0, saved0, weights1, saved1 = kept[:4], kept[4:18], kept[18:22], kept[22:]
     in_grads, g_fi, g_fo, g_mix = layers_backward(

time: 340 us -> 339 us (level)
  no operation moved by 1% of the time
where the time goes in v8:
time: 339 us; the launch traced here: 338 us
  Pallas kernels  331 us (98%)
    pallas_call x1, Pallas kernels, layers_backward(): pl.pallas_call(functools.partial(backward_kernel, dp), out_shape=tuple((j...  204 us
    pallas_call x1, Pallas kernels, layers_forward(): pl.pallas_call(functools.partial(forward_kernel, dp), out_shape=tuple((ja...  119 us
    pallas_call x1, Pallas kernels, widen(): pl.pallas_call(widen_kernel, out_shape=tuple((jax.ShapeDtypeStruct(a, f32...  8.4 us
  transfers between devices with their start and end apart: 1, of which 0 were waited for; matrix products, arithmetic and copies ran while one was open for 1% of the time, Pallas kernels for 0%

profile of v8, /device:TPU:0, one launch (start us, length us, event | category | flops | bytes accessed | tf_op | source)
XLA Modules:
  0.0 338.3 jit_solution(7865618171533611429)
XLA Ops:
  0.6 0.5 collective-permute-start
  1.1 0.7 compare_bitcast_fusion
  1.8 0.7 subtract_reduce_fusion
  2.6 0.1 select_reduce_fusion
  2.7 0.1 sub.16
  2.8 0.1 reduce_prod.27
  2.9 0.1 dynamic-slice_convert_fusion
  3.0 0.1 fusion.1
  3.0 0.7 multiply_exponential_fusion
  3.7 0.1 broadcast_multiply_fusion.1
  3.8 0.2 select_reduce_fusion.1
  4.0 0.1 copy.16
  4.1 0.1 select_n.74
  4.2 0.1 copy.15
  4.2 0.1 select_n.72
  4.3 0.1 copy.17
  4.4 0.1 select_n.80
  4.5 0.1 copy.18
  4.6 0.1 select_n.82
  4.7 1.3 concatenate.3.scal
  6.0 119.0 %layers_forward.1 = (bf16[2,192,1024]{2,1,0:T(8,128)(2,1)}, bf16[2,192,1024]{2,1,0:T(8,128)(2,1)}, f32[2,768,128]{2,1,0:T(8,128)}, bf16[768,1024]{1,0:T(8,128)(2...) custom-call(bf16[2,192,1024]{2,1,0:T(8,128)(2,1)} %tok_in.3, ...), custom_call_target="tpu_custom_call" | custom-call | flops 13690208256 | bytes 62914560 | tf_op jit(solution)/shard_map/layers_forward/pallas_call | solution.py:654
  124.9 204.1 %layers_backward.1 = (bf16[2,192,1024]{2,1,0:T(8,128)(2,1)}, bf16[2,768,1024]{2,1,0:T(8,128)(2,1)}, bf16[2,768,512]{2,1,0:T(8,128)(2,1)}, bf16[2,1280,512]{2,1,0:T(8,128)(2,1)}) custom-call(bf16[768,1024]{1,0:T(8,128)(2,1)} %get-tuple-element.56.gf_in, bf16[192,1024]{1,0:T(8,128)(2,1)} %get-tuple-element.57.y0_in, bf16[2,192,1024]{2,1,0:T(8,128)(2,1)} %tok_in.3, ...), custom_call_target="tpu_custom_call" | custom-call | flops 22548578304 | bytes 62914560 | tf_op jit(solution)/shard_map/layers_backward/pallas_call | solution.py:1288
  329.0 8.4 %widen.1 = (f32[1024,4,256]{2,1,0:T(4,128)}, f32[2,704,1024]{2,1,0:T(8,128)}, f32[256,1024]{1,0:T(8,128)}, f32[704,1024]{1,0:T(8,128)}, bf16[2,192,1024]{2,1,0:T(8,128)(2,1)}) custom-call(s32[1]{0:T(128)} %bitcast.section, bf16[2,768,1024]{2,1,0:T(8,128)(2,1)} %get-tuple-element.95.fi, bf16[2,768,512]{2,1,0:T(8,128)(2,1)} %get-tuple-element.96.fo, ...), custom_call_target="tpu_custom_call" | custom-call | bytes 25165824 | tf_op jit(solution)/shard_map/widen/pallas_call | solution.py:1334
  337.4 0.9 copy.20
  (9 shorter events, 0.0 us)
Async XLA Ops:
  0.6 2.4 collective-permute-start
  329.0 8.4 %copy-start = (bf16[2,192,1024]{2,1,0:T(8,128)(2,1)S(1)}, bf16[2,192,1024]{2,1,0:T(8,128)(2,1)}, u32[]{:S(2)}) copy-start(bf16[2,192,1024]{2,1,0:T(8,128)(2,1)} %get-tuple-element.101) | copy-start | bytes 2359300

commit v9 on v8

--- a/solution.py
+++ b/solution.py
@@ -1304,7 +1304,10 @@
     )(gathered, y0, tokens, turn, scal, *flat, *kept)
 
 
-def widen_kernel(section, fi, fo, mix, mix_out, both0, both1, g_in, g_fi, g_out, g_fo, outputs):
+def widen_kernel(
+    section, fi, fo, mix, mix_out, both0, both1, grads, g_in, g_fi, g_out, g_fo, outputs, in_grads
+):
+    in_grads[...] = grads[...]
     for n in range(4):
         lanes = slice((n % 2) * WIDTH, (n % 2 + 1) * WIDTH)
         g_in[:, n, :] = mix[n // 2, :, lanes].astype(f32)
@@ -1323,7 +1326,7 @@
         outputs[...] = both1[...]
 
 
-def widen(s, g_fi, g_fo, g_mix, both0, both1, ff):
+def widen(s, g_fi, g_fo, g_mix, both0, both1, grads, ff):
     cuts = 2
     rows = both0.shape[1]
     n = D // cuts
@@ -1334,7 +1337,7 @@
     return pl.pallas_call(
         widen_kernel,
         out_shape=tuple(jax.ShapeDtypeStruct(a, f32) for a in shapes)
-        + (jax.ShapeDtypeStruct(both0.shape, bf16),),
+        + (jax.ShapeDtypeStruct(both0.shape, bf16),) * 2,
         grid_spec=pltpu.PrefetchScalarGridSpec(
             num_scalar_prefetch=1,
             grid=(cuts,),
@@ -1345,17 +1348,19 @@
                 pl.BlockSpec((2, WIDTH // cuts, D // 2), lambda i, _: (0, ahead + i, 0)),
                 halves(2, rows // cuts, D),
                 halves(2, rows // cuts, D),
+                halves(2, rows // cuts, D),
             ],
             out_specs=(
                 per_row(n, 4, WIDTH), halves(2, ff // cuts, D), per_row(WIDTH // cuts, D),
                 per_row(ff // cuts, D),
+                halves(2, rows // cuts, D),
                 halves(2, rows // cuts, D),
             ),
         ),
         compiler_params=pltpu.CompilerParams(vmem_limit_bytes=VMEM_BYTES),
         cost_estimate=pl.CostEstimate(flops=0, bytes_accessed=24 << 20, transcendentals=0),
         name="widen",
-    )(s.reshape(1), g_fi, g_fo, g_mix, g_mix, both0, both1)
+    )(s.reshape(1), g_fi, g_fo, g_mix, g_mix, both0, both1, grads)
 
 
 def frequencies():
@@ -1393,7 +1398,9 @@
         gf, y0, tokens, turn, scal, (weights0, weights1),
         (saved0, saved1), dp, ff, 2,
     )
-    g_in, g_feed_in, g_out, g_feed_out, outputs = widen(s, g_fi, g_fo, g_mix, both0, both1, ff)
+    g_in, g_feed_in, g_out, g_feed_out, outputs, in_grads = widen(
+        s, g_fi, g_fo, g_mix, both0, both1, in_grads, ff
+    )
     g_feed_in = jnp.transpose(g_feed_in, (2, 0, 1))
     return outputs[None], in_grads[None], g_in[None], g_out[None], g_feed_in[None], g_feed_out[None]
 

time: 339 us -> 338 us (level)
  no operation moved by 1% of the time
where the time goes in v9:
time: 338 us
  Pallas kernels  332 us (98%)
    pallas_call x1, Pallas kernels, layers_backward(): pl.pallas_call(functools.partial(backward_kernel, dp), out_shape=tuple((j...  204 us
    pallas_call x1, Pallas kernels, layers_forward(): pl.pallas_call(functools.partial(forward_kernel, dp), out_shape=tuple((ja...  119 us
    pallas_call x1, Pallas kernels, widen(): pl.pallas_call(widen_kernel, out_shape=tuple((jax.ShapeDtypeStruct(a, f32...  8.72 us
  transfers between devices with their start and end apart: 1, of which 0 were waited for; matrix products, arithmetic and copies ran while one was open for 1% of the time, Pallas kernels for 0%

profile of v9, /device:TPU:0, one launch (start us, length us, event | category | flops | bytes accessed | tf_op | source)
XLA Modules:
  0.0 337.8 jit_solution(14352505495815071977)
XLA Ops:
  0.6 0.5 collective-permute-start
  1.1 0.7 compare_bitcast_fusion
  1.8 0.7 subtract_reduce_fusion
  2.6 0.1 select_reduce_fusion
  2.7 0.1 sub.16
  2.8 0.1 reduce_prod.27
  2.9 0.1 dynamic-slice_convert_fusion
  3.0 0.1 fusion.1
  3.0 0.0 collective-permute-done
  3.0 0.7 multiply_exponential_fusion
  3.7 0.1 broadcast_multiply_fusion.1
  3.8 0.2 select_reduce_fusion.1
  4.0 0.1 copy.16
  4.1 0.1 select_n.74
  4.2 0.1 copy.15
  4.2 0.1 select_n.72
  4.3 0.1 copy.17
  4.4 0.1 select_n.80
  4.5 0.1 copy.18
  4.6 0.1 select_n.82
  4.7 1.3 concatenate.3.scal
  6.0 119.0 %layers_forward.1 = (bf16[2,192,1024]{2,1,0:T(8,128)(2,1)}, bf16[2,192,1024]{2,1,0:T(8,128)(2,1)}, f32[2,768,128]{2,1,0:T(8,128)}, bf16[768,1024]{1,0:T(8,128)(2...) custom-call(bf16[2,192,1024]{2,1,0:T(8,128)(2,1)} %tok_in.3, ...), custom_call_target="tpu_custom_call" | custom-call | flops 13690208256 | bytes 62914560 | tf_op jit(solution)/shard_map/layers_forward/pallas_call | solution.py:654
  124.9 204.1 %layers_backward.1 = (bf16[2,192,1024]{2,1,0:T(8,128)(2,1)}, bf16[2,768,1024]{2,1,0:T(8,128)(2,1)}, bf16[2,768,512]{2,1,0:T(8,128)(2,1)}, bf16[2,1280,512]{2,1,0:T(8,128)(2,1)}) custom-call(bf16[768,1024]{1,0:T(8,128)(2,1)} %get-tuple-element.57.gf_in, bf16[192,1024]{1,0:T(8,128)(2,1)} %get-tuple-element.58.y0_in, bf16[2,192,1024]{2,1,0:T(8,128)(2,1)} %tok_in.3, ...), custom_call_target="tpu_custom_call" | custom-call | flops 22548578304 | bytes 62914560 | tf_op jit(solution)/shard_map/layers_backward/pallas_call | solution.py:1288
  329.0 8.7 %widen.1 = (f32[1024,4,256]{2,1,0:T(4,128)}, f32[2,704,1024]{2,1,0:T(8,128)}, f32[256,1024]{1,0:T(8,128)}, f32[704,1024]{1,0:T(8,128)}, bf16[2,192,1024]{2,1,0:T(8,128)(2,1)}, /*index=5*/bf16[2,192,1024]{2,1,0:T(8,128)(2,1)}) custom-call(s32[1]{0:T(128)} %bitcast.section, bf16[2,768,1024]{2,1,0:T(8,128)(2,1)} %get-tuple-element.96.fi, ...), custom_call_target="tpu_custom_call" | custom-call | bytes 25165824 | tf_op jit(solution)/shard_map/widen/pallas_call | solution.py:1337
  (6 shorter events, 0.0 us)
Async XLA Ops:
  0.6 2.4 collective-permute-start
